TPU v7x, 32 devices: a whole 2x2x4 slice. The times are simulated.
32 devices in a mesh: dp: 8 (over z, y), tensor: 4 (over x, core).
Axes of the slice: x: 2, y: 2, z: 4, core: 2. Of those that a mesh axis runs over, the one named last changes fastest.
Arguments:
- patches: bfloat16 [8, 1536, 576], P('dp', 'tensor'), may hold values from -6 to 6
- view_counts: int32 [8], P('dp'), may hold values from 2 to 8, as said below
- splat_index: int32 [8, 4, 24576], P('dp', None, 'tensor'), may hold values from 0 to 98303, as said below
- splat_dist: int32 [8, 4, 24576], P('dp', None, 'tensor'), may hold values from 1 to 8
- alpha_label: int32 [8, 24576], P('dp', 'tensor'), may hold values from 0 to 2, as said below
- step_count: int32 [1], replicated, may hold values from 2 to 20
- row_master: float32 [4, 3145728], P('tensor', 'dp')
- row_first: float32 [4, 3145728], P('tensor', 'dp')
- row_second: float32 [4, 3145728], P('tensor', 'dp')
- row_ema: float32 [4, 3145728], P('tensor', 'dp')
- shared_master: float32 [1380352], P('dp')
- shared_first: float32 [1380352], P('dp')
- shared_second: float32 [1380352], P('dp')
- shared_ema: float32 [1380352], P('dp')
Outputs:
- grad_norm: float32 [1], replicated
- loss: float32 [1], replicated
- row_new: float32 [4, 3145728], P('tensor', 'dp')
- row_first_new: float32 [4, 3145728], P('tensor', 'dp')
- row_second_new: float32 [4, 3145728], P('tensor', 'dp')
- row_ema_new: float32 [4, 3145728], P('tensor', 'dp')
- row_copy: bfloat16 [4, 3145728], P('tensor', 'dp')
- shared_new: float32 [1380352], P('dp')
- shared_first_new: float32 [1380352], P('dp')
- shared_second_new: float32 [1380352], P('dp')
- shared_ema_new: float32 [1380352], P('dp')
- shared_copy: bfloat16 [1380352], P('dp')
Inputs may be any that keep to these rules, and one draw needn't show every extreme that they name: Key slots from view_counts[s] * 192 on are padding views. `splat_index`: every entry of scene s names a Gaussian of that scene's real views: it is below view_counts[s] * 192 * 8 * 8. Every scene has at least one pixel whose alpha_label is below 2.
All inputs are finite; a program needn't handle non-finite values.
Results may differ from a plain program's by a relative error of at most 0.002.
The roundings to bfloat16 on the way count: a program that leaves them out, or rounds other values in their place, can miss the bound.
Values may be sent and summed in bfloat16 or wider, within the bound.
A program may use at most 128 MiB of HBM per device.

v0:
```python
from functools import partial

import jax
import jax.numpy as jnp
from jax import lax
from jax.sharding import PartitionSpec as P

D = 1024
DH = 64
FF = 4096
PATCH = 8
VTOK = 192
PIN = 576
POUT = 768


clip_norm = 0.005
beta_one = 0.9
beta_two = 0.95
adam_eps = 1e-08
decay_rate = 0.05
learn_rate = 0.03
ema_rate = 0.9
norm_eps = 1e-05
masked_score = -1e30


def contract_rows(left_op, right_op):
    return lax.dot_general(
        left_op, right_op, (((0,), (0,)), ((), ())), preferred_element_type=jnp.float32
    )


def contract_last(left_op, right_op):
    return lax.dot_general(
        left_op, right_op, (((1,), (1,)), ((), ())), preferred_element_type=jnp.float32
    )


def layer_norm(residual, gain_vec, bias_vec):
    centre = residual - jnp.mean(residual, -1, keepdims=True)
    inverse = lax.rsqrt(jnp.mean(centre * centre, -1, keepdims=True) + norm_eps)
    scaled = centre * inverse
    return (scaled * gain_vec + bias_vec, scaled, inverse)


def norm_back(grad_out, scaled, inverse, gain_vec):
    grad_scaled = grad_out * gain_vec
    return inverse * (
        grad_scaled
        - jnp.mean(grad_scaled, -1, keepdims=True)
        - scaled * jnp.mean(grad_scaled * scaled, -1, keepdims=True)
    )


def score_block(q_part, keyset, key_valid):
    factor = q_part.shape[-1] ** (-0.5)
    scores = jnp.einsum("qhd,khd->hqk", q_part, keyset, preferred_element_type=jnp.float32) * factor
    return jnp.where(key_valid[None, None, :], scores, masked_score)


def attend_forward(queries, keyset, values, key_valid, block_rows):
    length = queries.shape[0]

    def one_block(q_part):
        scores = score_block(q_part, keyset, key_valid)
        top_score = jnp.max(scores, -1, keepdims=True)
        weights_exp = jnp.exp(scores - top_score)
        row_total = jnp.sum(weights_exp, -1, keepdims=True)
        weights_low = (weights_exp / row_total).astype(jnp.bfloat16)
        results = jnp.einsum(
            "hqk,khd->qhd", weights_low, values, preferred_element_type=jnp.float32
        )
        return (results, (top_score + jnp.log(row_total))[..., 0])

    q_blocks = queries.reshape(length // block_rows, block_rows, queries.shape[1], queries.shape[2])
    results, log_total = lax.map(one_block, q_blocks)
    return (results.reshape(length, queries.shape[1] * queries.shape[2]), log_total)


def attend_back(queries, keyset, values, key_valid, attended_grad, log_total, block_rows):
    length = queries.shape[0]
    factor = queries.shape[-1] ** (-0.5)

    def one_block(carried, inputs):
        grad_keys, grad_values = carried
        q_part, g_part, l_part = inputs
        scores = score_block(q_part, keyset, key_valid)
        weights = jnp.exp(scores - l_part[..., None])
        grad_weights = jnp.einsum(
            "qhd,khd->hqk", g_part, values, preferred_element_type=jnp.float32
        )
        centre = jnp.sum(weights * grad_weights, -1, keepdims=True)
        grad_scores = (weights * (grad_weights - centre)).astype(jnp.bfloat16)
        grad_query = (
            jnp.einsum("hqk,khd->qhd", grad_scores, keyset, preferred_element_type=jnp.float32)
            * factor
        )
        grad_keys = (
            grad_keys
            + jnp.einsum("hqk,qhd->khd", grad_scores, q_part, preferred_element_type=jnp.float32)
            * factor
        )
        grad_values = grad_values + jnp.einsum(
            "hqk,qhd->khd", weights.astype(jnp.bfloat16), g_part, preferred_element_type=jnp.float32
        )
        return ((grad_keys, grad_values), grad_query)

    block_shape = (length // block_rows, block_rows, queries.shape[1], queries.shape[2])
    zeros_kv = jnp.zeros(keyset.shape, jnp.float32)
    (grad_keys, grad_values), grad_query = lax.scan(
        one_block,
        (zeros_kv, zeros_kv),
        (queries.reshape(block_shape), attended_grad.reshape(block_shape), log_total),
    )
    return (
        grad_query.reshape(length, -1),
        grad_keys.reshape(length, -1),
        grad_values.reshape(length, -1),
    )


def layer_forward(embedded, weights, key_valid):
    qkv_proj, out_proj, up_proj, down_proj, norm_params = weights
    local_width = out_proj.shape[0]
    heads_here = local_width // DH
    normed1, scaled1, inverse1 = layer_norm(embedded, norm_params[0], norm_params[1])
    normed1_all = lax.all_gather(normed1.astype(jnp.bfloat16), "tensor", axis=0, tiled=True)
    length = normed1_all.shape[0]
    block_rows = min(512, length)
    qkv = jnp.dot(normed1_all, qkv_proj, preferred_element_type=jnp.float32).astype(jnp.bfloat16)
    queries = qkv[:, :local_width].reshape(length, heads_here, DH)
    keyset = qkv[:, local_width : 2 * local_width].reshape(length, heads_here, DH)
    values = qkv[:, 2 * local_width :].reshape(length, heads_here, DH)
    attended, log_total = attend_forward(queries, keyset, values, key_valid, block_rows)
    attended = attended.astype(jnp.bfloat16)
    resid1 = embedded + lax.psum_scatter(
        jnp.dot(attended, out_proj, preferred_element_type=jnp.float32),
        "tensor",
        scatter_dimension=0,
        tiled=True,
    )
    normed2, scaled2, inverse2 = layer_norm(resid1, norm_params[2], norm_params[3])
    normed2_all = lax.all_gather(normed2.astype(jnp.bfloat16), "tensor", axis=0, tiled=True)
    hidden_pre = jnp.dot(normed2_all, up_proj, preferred_element_type=jnp.float32)
    active = jax.nn.gelu(hidden_pre, approximate=False).astype(jnp.bfloat16)
    resid2 = resid1 + lax.psum_scatter(
        jnp.dot(active, down_proj, preferred_element_type=jnp.float32).astype(jnp.bfloat16),
        "tensor",
        scatter_dimension=0,
        tiled=True,
    ).astype(jnp.float32)
    saved_values = (
        scaled1,
        inverse1,
        normed1_all,
        queries,
        keyset,
        values,
        log_total,
        attended,
        scaled2,
        inverse2,
        normed2_all,
        hidden_pre,
        active,
    )
    return (resid2, saved_values)


def layer_backward(resid2_grad, weights, key_valid, saved_values):
    qkv_proj, out_proj, up_proj, down_proj, norm_params = weights
    (
        scaled1,
        inverse1,
        normed1_all,
        queries,
        keyset,
        values,
        log_total,
        attended,
        scaled2,
        inverse2,
        normed2_all,
        hidden_pre,
        active,
    ) = saved_values
    length = normed1_all.shape[0]
    block_rows = min(512, length)
    down_in = lax.all_gather(resid2_grad.astype(jnp.bfloat16), "tensor", axis=0, tiled=True)
    down_grad = contract_rows(active, down_in)
    active_grad = contract_last(down_in, down_proj)
    gelu_back = jax.vjp(partial(jax.nn.gelu, approximate=False), hidden_pre)[1]
    hidden_grad = gelu_back(active_grad)[0].astype(jnp.bfloat16)
    up_grad = contract_rows(normed2_all, hidden_grad)
    normed2_grad = lax.psum_scatter(
        contract_last(hidden_grad, up_proj).astype(jnp.bfloat16),
        "tensor",
        scatter_dimension=0,
        tiled=True,
    ).astype(jnp.float32)
    resid1_grad = resid2_grad + norm_back(normed2_grad, scaled2, inverse2, norm_params[2])
    branch_in = lax.all_gather(resid1_grad.astype(jnp.bfloat16), "tensor", axis=0, tiled=True)
    out_grad = contract_rows(attended, branch_in)
    attended_grad = contract_last(branch_in, out_proj).astype(jnp.bfloat16).reshape(queries.shape)
    grad_query, grad_key, grad_value = attend_back(
        queries, keyset, values, key_valid, attended_grad, log_total, block_rows
    )
    qkv_grad = jnp.concatenate([grad_query, grad_key, grad_value], 1).astype(jnp.bfloat16)
    qkv_weight_grad = contract_rows(normed1_all, qkv_grad)
    normed1_grad = lax.psum_scatter(
        contract_last(qkv_grad, qkv_proj).astype(jnp.bfloat16),
        "tensor",
        scatter_dimension=0,
        tiled=True,
    ).astype(jnp.float32)
    embed_grad = resid1_grad + norm_back(normed1_grad, scaled1, inverse1, norm_params[0])
    gain_grad = jnp.stack(
        [
            jnp.sum(normed1_grad * scaled1, 0),
            jnp.sum(normed1_grad, 0),
            jnp.sum(normed2_grad * scaled2, 0),
            jnp.sum(normed2_grad, 0),
        ]
    )
    weight_grad = jnp.concatenate(
        [
            qkv_weight_grad.reshape(-1),
            out_grad.reshape(-1),
            up_grad.reshape(-1),
            down_grad.reshape(-1),
        ]
    )
    return (embed_grad, weight_grad, gain_grad)


def pixel_loss(opacity, spread, distance, valid_px, target):
    contrib = (0.02 + 0.96 * jax.nn.sigmoid(opacity)) * jnp.exp(
        -0.25 * distance * jax.nn.sigmoid(spread)
    )
    keep_log = jnp.sum(jnp.log1p(-contrib), 0)
    alpha_log = jnp.log(-jnp.expm1(keep_log))
    return jnp.sum(valid_px * -(target * alpha_log + (1.0 - target) * keep_log))


def render_with_grad(gauss_table, splats, distance, valid_px, target):
    area = PATCH * PATCH
    slot_count = gauss_table.shape[0]
    splat_rows, pixel_count = splats.shape
    block_px = min(128, pixel_count)
    block_count = pixel_count // block_px
    slot_ids = jnp.arange(slot_count, dtype=jnp.int32)
    cell_ids = jnp.arange(area, dtype=jnp.int32)

    def to_blocks(array):
        return array.reshape(splat_rows, block_count, block_px).transpose(1, 0, 2)

    def one_block(carried, inputs):
        loss_acc, grad_acc = carried
        index_part, dist_part, valid_part, target_part = inputs
        flat_index = index_part.reshape(-1)
        token_hot = (flat_index[:, None] // area == slot_ids[None, :]).astype(jnp.float32)
        cell_hot = (flat_index[:, None] % area == cell_ids[None, :]).astype(jnp.float32)
        picked = jnp.dot(
            token_hot,
            gauss_table,
            precision=lax.Precision.HIGHEST,
            preferred_element_type=jnp.float32,
        )
        opacity = jnp.sum(picked[:, :area] * cell_hot, 1).reshape(index_part.shape)
        spread = jnp.sum(picked[:, area:] * cell_hot, 1).reshape(index_part.shape)
        part_loss, part_back = jax.vjp(
            lambda op_in, sp_in: pixel_loss(op_in, sp_in, dist_part, valid_part, target_part),
            opacity,
            spread,
        )
        grad_op, grad_sp = part_back(jnp.float32(1.0))
        weighted = jnp.concatenate(
            [grad_op.reshape(-1, 1) * cell_hot, grad_sp.reshape(-1, 1) * cell_hot], 1
        )
        grad_acc = grad_acc + lax.dot_general(
            token_hot,
            weighted,
            (((0,), (0,)), ((), ())),
            precision=lax.Precision.HIGHEST,
            preferred_element_type=jnp.float32,
        )
        return ((loss_acc + part_loss, grad_acc), None)

    inputs = (
        to_blocks(splats),
        to_blocks(distance),
        valid_px.reshape(block_count, block_px),
        target.reshape(block_count, block_px),
    )
    start = (jnp.zeros((), jnp.float32), jnp.zeros(gauss_table.shape, jnp.float32))
    (loss_part, table_grad), unused = lax.scan(one_block, start, inputs)
    return (loss_part, table_grad)


def adam_update(master, first_mom, second_mom, gradient, step_float):
    first_new = beta_one * first_mom + (1.0 - beta_one) * gradient
    second_new = beta_two * second_mom + (1.0 - beta_two) * gradient * gradient
    first_hat = first_new / (1.0 - jnp.power(beta_one, step_float))
    second_hat = second_new / (1.0 - jnp.power(beta_two, step_float))
    master_new = master - learn_rate * (
        first_hat / (jnp.sqrt(second_hat) + adam_eps) + decay_rate * master
    )
    return (master_new, first_new, second_new)


def per_device(
    patches,
    view_counts,
    splat_index,
    splat_dist,
    alpha_label,
    step_count,
    row_master,
    row_first,
    row_second,
    row_ema,
    shared_master,
    shared_first,
    shared_second,
    shared_ema,
):
    my_slot = lax.axis_index("tensor")
    groups = lax.axis_size("tensor")
    row_weights, shared_weights = (
        lax.all_gather(row_master[0].astype(jnp.bfloat16), "dp", axis=0, tiled=True),
        lax.all_gather(shared_master.astype(jnp.bfloat16), "dp", axis=0, tiled=True),
    )
    local_width = D // groups
    local_hidden = FF // groups
    qkv_end = 3 * D * local_width
    out_end = qkv_end + local_width * D
    up_end = out_end + D * local_hidden
    weights = (
        row_weights[:qkv_end].reshape(D, 3 * local_width),
        row_weights[qkv_end:out_end].reshape(local_width, D),
        row_weights[out_end:up_end].reshape(D, local_hidden),
        row_weights[up_end:].reshape(local_hidden, D),
        shared_weights[PIN * D + D * POUT :].reshape(4, D).astype(jnp.float32),
    )
    patch_proj = shared_weights[: PIN * D].reshape(PIN, D)
    used_cols = shared_weights[PIN * D : PIN * D + D * POUT].reshape(D, POUT)[
        :, : 2 * PATCH * PATCH
    ]
    own_patches = patches[0]
    row_count = own_patches.shape[0]
    key_valid = jnp.arange(row_count * groups) < view_counts[0] * VTOK
    embedded = jnp.dot(own_patches, patch_proj, preferred_element_type=jnp.float32)
    resid2, saved_values = layer_forward(embedded, weights, key_valid)
    resid2_low = resid2.astype(jnp.bfloat16)
    gauss_table = lax.all_gather(
        jnp.dot(resid2_low, used_cols, preferred_element_type=jnp.float32).astype(jnp.bfloat16),
        "tensor",
        axis=0,
        tiled=True,
    ).astype(jnp.float32)
    labels = alpha_label[0]
    valid_px = (labels < 2).astype(jnp.float32)
    target = (labels == 1).astype(jnp.float32)
    loss_part, table_grad = render_with_grad(
        gauss_table, splat_index[0], splat_dist[0].astype(jnp.float32), valid_px, target
    )
    gauss_grad = lax.psum_scatter(
        table_grad.astype(jnp.bfloat16), "tensor", scatter_dimension=0, tiled=True
    )
    unpatch_used = contract_rows(resid2_low, gauss_grad)
    resid2_grad = contract_last(gauss_grad, used_cols)
    embed_grad, weight_grad, gain_grad = layer_backward(
        resid2_grad, weights, key_valid, saved_values
    )
    patch_grad = contract_rows(own_patches, embed_grad.astype(jnp.bfloat16))
    unpatch_grad = jnp.concatenate(
        [unpatch_used, jnp.zeros((D, POUT - unpatch_used.shape[1]), jnp.float32)], 1
    )
    shared_grad = jnp.concatenate(
        [patch_grad.reshape(-1), unpatch_grad.reshape(-1), gain_grad.reshape(-1)]
    )
    row_share, shared_part = (
        lax.psum_scatter(weight_grad, "dp", scatter_dimension=0, tiled=True),
        lax.psum_scatter(shared_grad, "dp", scatter_dimension=0, tiled=True),
    )
    shared_share = lax.psum(shared_part, "tensor")
    own_squares = jnp.sum(row_share * row_share) + jnp.where(
        my_slot == 0, jnp.sum(shared_share * shared_share), 0.0
    )
    square_total, loss_total, pixel_total = lax.psum(
        (own_squares, loss_part, jnp.sum(valid_px)), ("dp", "tensor")
    )
    norm_value = jnp.sqrt(square_total) / pixel_total
    factor = clip_norm / jnp.maximum(norm_value, clip_norm) / pixel_total
    step_float = step_count[0].astype(jnp.float32)
    row_new, row_first_new, row_second_new = adam_update(
        row_master[0], row_first[0], row_second[0], row_share * factor, step_float
    )
    shared_new, shared_first_new, shared_second_new = adam_update(
        shared_master, shared_first, shared_second, shared_share * factor, step_float
    )
    row_ema_new = ema_rate * row_ema[0] + (1.0 - ema_rate) * row_new
    shared_ema_new = ema_rate * shared_ema + (1.0 - ema_rate) * shared_new
    return (
        norm_value.reshape(1),
        (loss_total / pixel_total).reshape(1),
        row_new[None],
        row_first_new[None],
        row_second_new[None],
        row_ema_new[None],
        row_new.astype(jnp.bfloat16)[None],
        shared_new,
        shared_first_new,
        shared_second_new,
        shared_ema_new,
        shared_new.astype(jnp.bfloat16),
    )


def solution(mesh):
    placed = (
        P("dp", "tensor", None),
        P("dp"),
        P("dp", None, "tensor"),
        P("dp", None, "tensor"),
        P("dp", "tensor"),
        P(),
        P("tensor", "dp"),
        P("tensor", "dp"),
        P("tensor", "dp"),
        P("tensor", "dp"),
        P("dp"),
        P("dp"),
        P("dp"),
        P("dp"),
    )
    return jax.shard_map(
        per_device,
        mesh=mesh,
        in_specs=placed,
        out_specs=(
            P(),
            P(),
            P("tensor", "dp"),
            P("tensor", "dp"),
            P("tensor", "dp"),
            P("tensor", "dp"),
            P("tensor", "dp"),
            P("dp"),
            P("dp"),
            P("dp"),
            P("dp"),
            P("dp"),
        ),
        check_vma=False,
    )
```

profile of v0, /device:TPU:0, one launch (start us, length us, event | category | flops | bytes accessed | tf_op | source)
XLA Modules:
  0.0 1847.9 jit_solution(13719993758717065283)
XLA Ops:
  14.6 91.1 %all-gather.18.cloned.1.call-done = bf16[8,1,172544]{2,1,0:T(2,128)(2,1)} async-done(((bf16[1,1,172544]{2,1,0:T(2,128)(2,1)}), bf16[8,1,172544]{2,1,0:T(2,128)(2,1)}) %all-gather.18.cloned.1.call-update) | async-done | bytes 2760720 | tf_op jit(solution)/shard_map/all_gather | solution.py:332
  105.7 41.4 %reduce.1 = bf16[8,172544]{1,0:T(8,128)(2,1)} reduce(bf16[8,1,172544]{2,1,0:T(2,128)(2,1)} %all-gather.18.cloned.1.call-done, bf16[]{:T(256)} %constant.272), dimensions={1}, to_apply=%all-gather.reduce_sub_computation | reduce | bytes 5521410 | tf_op jit(solution)/shard_map/all_gather | solution.py:332
  147.1 7.4 reshape.460
  163.1 42.7 %all-gather.10.cloned.1.call-done = bf16[3145728]{0:T(1024)(128)(2,1)} async-done(((bf16[393216]{0:T(1024)(128)(2,1)}), bf16[3145728]{0:T(1024)(128)(2,1)}) %all-gather.10.cloned.1.call-update) | async-done | bytes 6291472 | tf_op jit(solution)/shard_map/all_gather | solution.py:331
  209.4 25.2 %all-gather.8.cloned.1.call-done = bf16[1536,1024]{1,0:T(8,128)(2,1)} async-done(((bf16[384,1024]{1,0:T(8,128)(2,1)}), bf16[1536,1024]{1,0:T(8,128)(2,1)}) %all-gather.8.cloned.1.call-update) | async-done | bytes 3145744 | tf_op jit(solution)/shard_map/all_gather | solution.py:128
  243.5 27.4 %while.43 = (s32[]{:T(128)}, bf16[3,512,4,64]{1,3,2,0:T(8,128)(2,1)}, f32[3,4,512]{2,1,0:T(4,128)S(1)}, bf16[3,512,4,64]{1,3,2,0:T(8,128)(2,1)S(1)}, bf16[1536,4...) while((s32[]{:T(128)}, ...), condition=%wide.region_5.6_spmd.clone, body=%wide.region_2.5_spmd.clone.sunk | while | flops 843054592 | bytes 40180332 | solution.py:77
  280.6 58.3 %reduce-scatter.6.cloned.1.call-done = f32[384,1024]{1,0:T(8,128)} async-done(((f32[1536,1024]{1,0:T(8,128)}), f32[384,1024]{1,0:T(8,128)}) %reduce-scatter.6.cloned.1.call-update) | async-done | bytes 1572880 | tf_op jit(solution)/shard_map/reduce_scatter | solution.py:137
  355.6 15.7 all-gather.12.cloned.1.call-done
  371.2 20.0 %multiply_convert_fusion.1 = (bf16[1536,1024]{1,0:T(8,128)(2,1)S(1)}, f32[1536,1024]{1,0:T(8,128)}, f32[1536,1024]{1,0:T(8,128)}) fusion(bf16[1536,1024]{1,0:T(8,128)(2,1)} %all-gather.12.cloned.1.call-done, bf16[1024,1024]{1,0:T(8,128)(2,1)} %slice.136), kind=kOutput, calls=%fused_computation.106 | convolution fusion | flops 3323461632 | bytes 20971520 | tf_op jit(solution)/shard_map/dot_general | solution.py:145
  405.3 30.5 %reduce-scatter.8.cloned.1.call-done = bf16[384,1024]{1,0:T(8,128)(2,1)} async-done(((bf16[1536,1024]{1,0:T(8,128)(2,1)}), bf16[384,1024]{1,0:T(8,128)(2,1)}) %reduce-scatter.8.cloned.1.call-update) | async-done | bytes 786448 | tf_op jit(solution)/shard_map/reduce_scatter | solution.py:147
  437.4 6.4 all_gather.25
  444.7 435.4 %while.44 = (s32[]{:T(128)}, f32[]{:T(128)}, f32[1536,128]{1,0:T(8,128)}, f32[48,128]{1,0:T(8,128)S(1)}, f32[48,128]{1,0:T(8,128)S(1)}, /*index=5*/s32[48,4,128]...) while((s32[]{:T(128)}, f32[]{:T(128)}, ...), condition=%wide.region_15.16_spmd.clone, body=%wide.region_10.15_spmd.clone.sunk | while | flops 2419029760 | bytes 3450007 | solution.py:297
  882.1 21.2 %reduce-scatter.10.cloned.1.call-done = bf16[384,128]{1,0:T(8,128)(2,1)} async-done(((bf16[1536,128]{1,0:T(8,128)(2,1)}), bf16[384,128]{1,0:T(8,128)(2,1)}) %reduce-scatter.10.cloned.1.call-update) | async-done | bytes 98320 | tf_op jit(solution)/shard_map/reduce_scatter | solution.py:368
  906.2 28.6 %all-gather.14.cloned.1.call-done = bf16[1536,1024]{1,0:T(8,128)(2,1)} async-done(((bf16[384,1024]{1,0:T(8,128)(2,1)}), bf16[1536,1024]{1,0:T(8,128)(2,1)}) %all-gather.14.cloned.1.call-update) | async-done | bytes 3145744 | tf_op jit(solution)/shard_map/all_gather | solution.py:190
  934.8 11.6 add_convert_fusion
  953.1 38.1 %reduce-scatter.12.cloned.1.call-done = bf16[384,1024]{1,0:T(8,128)(2,1)} async-done(((bf16[1536,1024]{1,0:T(8,128)(2,1)}), bf16[384,1024]{1,0:T(8,128)(2,1)}) %reduce-scatter.12.cloned.1.call-update) | async-done | bytes 786448 | tf_op jit(solution)/shard_map/reduce_scatter | solution.py:196
  1009.7 6.3 convolution_bitcast_fusion
  1041.3 84.2 %while.45 = (s32[]{:T(128)}, f32[1536,4,64]{0,2,1:T(8,128)}, f32[1536,4,64]{0,2,1:T(8,128)}, bf16[3,512,4,64]{1,3,2,0:T(8,128)(2,1)}, bf16[3,512,4,64]{1,3,2,0:T...) while((s32[]{:T(128)}, f32[1536,4,64]{0,2,1:T(8,128)}, ...), condition=%wide.region_22.23_spmd.clone, body=%wide.region_20.22_spmd.clone.sunk | while | flops 2043674112 | bytes 192720752 | solution.py:111
  1143.6 12.4 pad_maximum_fusion
  1156.0 25.5 %reduce-scatter.14.cloned.1.call-done = bf16[384,1024]{1,0:T(8,128)(2,1)} async-done(((bf16[1536,1024]{1,0:T(8,128)(2,1)}), bf16[384,1024]{1,0:T(8,128)(2,1)}) %reduce-scatter.14.cloned.1.call-update) | async-done | bytes 786448 | tf_op jit(solution)/shard_map/reduce_scatter | solution.py:211
  1187.7 6.3 pad_maximum_fusion.1
  1199.7 544.6 %all-reduce.10.cloned.1.call-done = (f32[3145728]{0:T(1024)}, f32[1380352]{0:T(1024)}) async-done(((f32[3145728]{0:T(1024)}, f32[1380352]{0:T(1024)}), (f32[3145728]{0:T(1024)}, f32[1380352]{0:T(1024)})) %all-reduce.10.cloned.1.call-update) | async-done | bytes 18104336
  1755.3 24.9 %all-reduce.8.cloned.1.call-done = f32[172544]{0:T(1024)} async-done(((f32[172544]{0:T(1024)}), f32[172544]{0:T(1024)}) %all-reduce.8.cloned.1.call-update) | async-done | bytes 690192 | tf_op jit(solution)/shard_map/psum | solution.py:387
  1783.4 40.5 %all-reduce.3 = (f32[]{:T(128)}, f32[]{:T(128)}, f32[]{:T(128)}) all-reduce(f32[]{:T(128)S(6)} %add.268, f32[]{:T(128)} %fusion.110, f32[]{:T(128)} %get-tuple-element.239), channel_id=1, replica_groups=mesh['dp'=8,'tensor'=4] {'dp','tensor'}, use_global_device_ids=true, to_apply=%region_35.36 | all-reduce | flops 3 | bytes 24 | tf_op jit(solution)/shard_map/psum | solution.py:391
  (684 shorter events, 691.4 us)
Async XLA Ops:
  7.2 150.0 %copy-start = (bf16[1,384,576]{1,2,0:T(8,128)(2,1)S(1)}, bf16[1,384,576]{1,2,0:T(8,128)(2,1)}, u32[]{:S(2)}) copy-start(bf16[1,384,576]{1,2,0:T(8,128)(2,1)} %param.20) | copy-start | bytes 1327108
  7.2 98.5 %all-gather.18.cloned.1.call-start = ((), (), s32[]{:S(2)}) async-start(), calls=%async_computation.16 | async-start | bytes 6211584 | tf_op jit(solution)/shard_map/all_gather | solution.py:332
  13.2 192.5 %all-gather.10.cloned.1.call-start = ((), (), s32[]{:S(2)}) async-start(), calls=%async_computation.6 | async-start | bytes 7077888 | tf_op jit(solution)/shard_map/all_gather | solution.py:331
  14.3 220.4 %all-gather.8.cloned.1.call-start = ((), (), s32[]{:S(2)}) async-start(), calls=%async_computation.5 | async-start | bytes 3932160 | tf_op jit(solution)/shard_map/all_gather | solution.py:128
  159.5 46.3 %copy-start.41 = (f32[384]{0:T(512)}, f32[384]{0:T(512)S(1)}, u32[]{:S(2)}) copy-start(f32[384]{0:T(512)S(1)} %broadcast_multiply_fusion.8) | copy-start | bytes 4612
  159.8 45.9 %copy-start.43 = (f32[384]{0:T(512)}, f32[384]{0:T(512)S(1)}, u32[]{:S(2)}) copy-start(f32[384]{0:T(512)S(1)} %add_rsqrt_fusion.1) | copy-start | bytes 4612
  160.6 45.2 %copy-start.38 = (f32[1024]{0:T(1024)}, f32[1024]{0:T(1024)S(1)}, u32[]{:S(2)}) copy-start(f32[1024]{0:T(1024)S(1)} %get-tuple-element.476) | copy-start | bytes 12292
  161.8 177.0 %reduce-scatter.6.cloned.1.call-start = ((), (), s32[]{:S(2)}) async-start(), calls=%async_computation.7 | async-start | bytes 7864320 | tf_op jit(solution)/shard_map/reduce_scatter | solution.py:137
  280.4 61.0 %copy-start.40 = (f32[1024]{0:T(1024)S(1)}, f32[1024]{0:T(1024)}, u32[]{:S(2)}) copy-start(f32[1024]{0:T(1024)} %get-tuple-element.473) | copy-start | bytes 12292
  280.4 61.0 %copy-start.47 = (f32[1024]{0:T(1024)S(1)}, f32[1024]{0:T(1024)}, u32[]{:S(2)}) copy-start(f32[1024]{0:T(1024)} %get-tuple-element.474) | copy-start | bytes 12292
  280.4 90.9 %all-gather.12.cloned.1.call-start = ((), (), s32[]{:S(2)}) async-start(), calls=%async_computation.8 | async-start | bytes 3932160 | tf_op jit(solution)/shard_map/all_gather | solution.py:144
  342.6 93.3 %reduce-scatter.8.cloned.1.call-start = ((), (), s32[]{:S(2)}) async-start(), calls=%async_computation.9 | async-start | bytes 3932160 | tf_op jit(solution)/shard_map/reduce_scatter | solution.py:147
  397.7 505.6 %reduce-scatter.10.cloned.1.call-start = ((), (), s32[]{:S(2)}) async-start(), calls=%async_computation.10 | async-start | bytes 491520 | tf_op jit(solution)/shard_map/reduce_scatter | solution.py:368
  882.1 52.8 %all-gather.14.cloned.1.call-start = ((), (), s32[]{:S(2)}) async-start(), calls=%async_computation.11 | async-start | bytes 3932160 | tf_op jit(solution)/shard_map/all_gather | solution.py:190
  906.1 85.0 %reduce-scatter.12.cloned.1.call-start = ((), (), s32[]{:S(2)}) async-start(), calls=%async_computation.12 | async-start | bytes 3932160 | tf_op jit(solution)/shard_map/reduce_scatter | solution.py:196
  953.1 74.0 %all-gather.16.cloned.1.call-start = ((), (), s32[]{:S(2)}) async-start(), calls=%async_computation.13 | async-start | bytes 3932160 | tf_op jit(solution)/shard_map/all_gather | solution.py:203
  997.0 184.6 %reduce-scatter.14.cloned.1.call-start = ((), (), s32[]{:S(2)}) async-start(), calls=%async_computation.14 | async-start | bytes 3932160 | tf_op jit(solution)/shard_map/reduce_scatter | solution.py:211
  1143.5 600.8 %all-reduce.10.cloned.1.call-start = ((), (), s32[]{:S(2)}) async-start(), calls=%async_computation.17 | async-start | bytes 36208640
  1143.5 38.1 %copy-start.6 = (f32[384,1024]{1,0:T(8,128)S(1)}, f32[384,1024]{1,0:T(8,128)}, u32[]{:S(2)}) copy-start(f32[384,1024]{1,0:T(8,128)} %copy-done.5) | copy-start | bytes 4718596
  1143.6 40.0 %copy-start.45 = (f32[1024]{0:T(1024)S(1)}, f32[1024]{0:T(1024)}, u32[]{:S(2)}) copy-start(f32[1024]{0:T(1024)} %get-tuple-element.379) | copy-start | bytes 12292
  1143.6 40.0 %copy-start.46 = (f32[1024]{0:T(1024)S(1)}, f32[1024]{0:T(1024)}, u32[]{:S(2)}) copy-start(f32[1024]{0:T(1024)} %get-tuple-element.384) | copy-start | bytes 12292
  1194.1 586.1 %all-reduce.8.cloned.1.call-start = ((), (), s32[]{:S(2)}) async-start(), calls=%async_computation.15 | async-start | bytes 1384448 | tf_op jit(solution)/shard_map/psum | solution.py:387
  1198.4 553.8 %copy-start.37 = (s32[1,6144]{1,0:T(1,128)S(1)}, s32[1,6144]{1,0:T(1,128)}, u32[]{:S(2)}) copy-start(s32[1,6144]{1,0:T(1,128)} %param.24) | copy-start | bytes 73732
  1746.5 80.8 %copy-start.14 = (f32[1,393216]{1,0:T(1,128)S(1)}, f32[1,393216]{1,0:T(1,128)}, u32[]{:S(2)}) copy-start(f32[1,393216]{1,0:T(1,128)} %param.26) | copy-start | bytes 4718596
  (62 other events, 388.3 us)
Sparse Core Ops, SparseCore 0:
  13.3 92.3 all-gather.17
  108.5 97.2 all-gather.9
  207.9 26.7 all-gather.7
  280.5 58.3 reduce-scatter.5
  342.7 28.5 all-gather.11
  397.8 37.9 reduce-scatter.7
  882.2 21.1 reduce-scatter.9
  906.2 28.5 all-gather.13
  953.2 37.9 reduce-scatter.11
  997.1 28.5 all-gather.15
  1143.6 37.9 reduce-scatter.13
  1194.2 550.0 all-reduce.9
  1747.2 32.9 all-reduce.7
where the time goes:
time: 1860 us; the launch traced here: 1850 us
  waiting for transfers between devices  947 us (51%)
  matrix products  500 us (27%)
  other arithmetic  197 us (11%)
  local copies, waits for them, and re-layouts  97.2 us (5%)
  blocking collectives  46.8 us (3%)
  loops' own time  33.2 us (2%)
  between operations  24.4 us (1%)
    unnamed x14, waiting for transfers between devices  545 us
    dot_general x48, matrix products, one_block(): lax.dot_general(token_hot, weighted, (((0,), (0,)), ((), ())), precision=...  187 us
    dot_general x48, matrix products, one_block(): jnp.dot(token_hot, gauss_table, precision=lax.Precision.HIGHEST, preferre...  145 us
    all_gather x1, waiting for transfers between devices, per_device(): lax.all_gather(shared_master.astype(jnp.bfloat16), 'dp', axis=0, tiled=True)  91.1 us
    reduce_scatter x1, waiting for transfers between devices, layer_forward(): lax.psum_scatter(jnp.dot(attended, out_proj, preferred_element_type=jnp.f...  58.3 us
    all_gather x1, waiting for transfers between devices, per_device(): lax.all_gather(row_master[0].astype(jnp.bfloat16), 'dp', axis=0, tiled=True)  42.7 us
    all_gather x1, other arithmetic, per_device(): lax.all_gather(shared_master.astype(jnp.bfloat16), 'dp', axis=0, tiled=True)  41.4 us
    psum x1, blocking collectives, per_device(): lax.psum((own_squares, loss_part, jnp.sum(valid_px)), ('dp', 'tensor'))  40.5 us
  transfers between devices with their start and end apart: 13, of which 12 were waited for; matrix products, arithmetic and copies ran while one was open for 7% of the time, Pallas kernels for 0%

commit v1 on v0

--- a/solution.py
+++ b/solution.py
@@ -1,10 +1,15 @@
+import functools
+import math
 from functools import partial
 
 import jax
 import jax.numpy as jnp
 from jax import lax
+from jax.experimental import pallas as pl
+from jax.experimental.pallas import tpu as pltpu
 from jax.sharding import PartitionSpec as P
 
+MESH = pl.DeviceIdType.MESH
 D = 1024
 DH = 64
 FF = 4096
@@ -223,80 +228,329 @@
             jnp.sum(normed2_grad, 0),
         ]
     )
-    weight_grad = jnp.concatenate(
-        [
-            qkv_weight_grad.reshape(-1),
-            out_grad.reshape(-1),
-            up_grad.reshape(-1),
-            down_grad.reshape(-1),
+    return (embed_grad, (qkv_weight_grad, out_grad, up_grad, down_grad), gain_grad)
+
+
+NT = (((1,), (1,)), ((), ()))
+NN = (((1,), (0,)), ((), ()))
+
+def render_kernel(area, wide, block, split, table_ref, splat_ref, dist_ref, label_ref, loss_ref, grad_ref, flip, picked, hot, spread_grad):
+    tokens = table_ref.shape[0]
+    groups = tokens // wide
+    splats, pixels = splat_ref.shape
+    for j in range(groups):
+        flip[j * 2 * area : (j + 1) * 2 * area] = jnp.transpose(table_ref[j * wide : (j + 1) * wide].astype(jnp.float32)).astype(jnp.bfloat16)
+    spread_grad[...] = jnp.zeros_like(spread_grad)
+    wide_ids = lax.broadcasted_iota(jnp.int32, (wide, block), 0).astype(jnp.float32).astype(jnp.bfloat16)
+    cell_ids = lax.broadcasted_iota(jnp.int32, (area, block), 0).astype(jnp.float32)
+    cell_low = cell_ids.astype(jnp.bfloat16)
+    one, nil = jnp.ones((wide, block), jnp.bfloat16), jnp.zeros((wide, block), jnp.bfloat16)
+
+    def one_block(step, loss):
+        here = pl.ds(pl.multiple_of(step * block, block), block)
+        opacities, spreads, lows = [], [], []
+        for k in range(splats):
+            index = splat_ref[k : k + 1, here]
+            token = index // area
+            column = (token % wide).astype(jnp.float32).astype(jnp.bfloat16)
+            group = (token // wide)
+            cell = (index % area).astype(jnp.float32)
+            match = jnp.where(wide_ids == column, one, nil)
+            hot[k] = match
+            picked[...] = lax.dot_general(flip[...], match, NN, preferred_element_type=jnp.float32)
+            op_sum = jnp.zeros((area, block), jnp.float32)
+            sp_sum = jnp.zeros((area, block), jnp.float32)
+            for j in range(groups):
+                same = cell_ids == jnp.where(group == j, cell, -1.0)
+                op_sum += jnp.where(same, picked[j * 2 * area : j * 2 * area + area], 0.0)
+                sp_sum += jnp.where(same, picked[j * 2 * area + area : (j + 1) * 2 * area], 0.0)
+            opacities.append(jnp.sum(op_sum, 0, keepdims=True))
+            spreads.append(jnp.sum(sp_sum, 0, keepdims=True))
+            lows.append((group, cell))
+        opacity, spread = jnp.concatenate(opacities, 0), jnp.concatenate(spreads, 0)
+        distance = dist_ref[:, here].astype(jnp.float32)
+        labels = label_ref[:, here]
+        valid = jnp.where(labels < 2, 1.0, 0.0)
+        target = jnp.where(labels == 1, 1.0, 0.0)
+        op_sig, sp_sig = jax.nn.sigmoid(opacity), jax.nn.sigmoid(spread)
+        fade = jnp.exp(-0.25 * distance * sp_sig)
+        contrib = (0.02 + 0.96 * op_sig) * fade
+        keep_log = jnp.sum(jnp.log1p(-contrib), 0, keepdims=True)
+        keep = jnp.exp(keep_log)
+        alpha = 1.0 - keep
+        alpha_log = jnp.log(alpha)
+        loss = loss - valid * (target * alpha_log + (1.0 - target) * keep_log)
+        keep_grad = valid * (target * keep / alpha - (1.0 - target))
+        contrib_grad = -keep_grad / (1.0 - contrib)
+        op_grad = contrib_grad * (0.96 * op_sig * (1.0 - op_sig)) * fade
+        sp_grad = contrib_grad * contrib * (-0.25 * distance * sp_sig * (1.0 - sp_sig))
+        for k in range(splats):
+            group, cell = lows[k]
+            parts_op, parts_sp = op_grad[k : k + 1], sp_grad[k : k + 1]
+            for part in range(split):
+                low_op, low_sp = parts_op.astype(jnp.bfloat16), parts_sp.astype(jnp.bfloat16)
+                parts_op, parts_sp = parts_op - low_op.astype(jnp.float32), parts_sp - low_sp.astype(jnp.float32)
+                pieces = []
+                for j in range(groups):
+                    same = cell_low == jnp.where(group == j, cell, -1.0).astype(jnp.bfloat16)
+                    pieces.append(jnp.where(same, low_op, jnp.bfloat16(0)))
+                    pieces.append(jnp.where(same, low_sp, jnp.bfloat16(0)))
+                weighted = jnp.concatenate(pieces, 0)
+                spread_grad[...] += lax.dot_general(weighted, hot[k], NT, preferred_element_type=jnp.float32)
+        return loss
+
+    loss = lax.fori_loop(0, pixels // block, one_block, jnp.zeros((1, block), jnp.float32))
+    loss_ref[...] = jnp.broadcast_to(jnp.sum(loss, 1, keepdims=True), loss_ref.shape)
+    for j in range(groups):
+        grad_ref[j * wide : (j + 1) * wide] = jnp.transpose(spread_grad[j * 2 * area : (j + 1) * 2 * area]).astype(grad_ref.dtype)
+
+def render(table, splats, distance, labels, area, block=512, wide=256, split=2):
+    tokens = table.shape[0]
+    vm = pl.BlockSpec(memory_space=pltpu.VMEM)
+    groups = tokens // wide
+    return pl.pallas_call(
+        functools.partial(render_kernel, area, wide, block, split),
+        out_shape=(jax.ShapeDtypeStruct((8, 128), jnp.float32), jax.ShapeDtypeStruct(table.shape, jnp.bfloat16)),
+        in_specs=[vm] * 4, out_specs=(vm, vm),
+        scratch_shapes=[pltpu.VMEM((groups * 2 * area, wide), jnp.bfloat16), pltpu.VMEM((groups * 2 * area, block), jnp.float32),
+            pltpu.VMEM((splats.shape[0], wide, block), jnp.bfloat16), pltpu.VMEM((groups * 2 * area, wide), jnp.float32)],
+        compiler_params=pltpu.CompilerParams(vmem_limit_bytes=48 * 2**20),
+    )(table, splats, distance, labels)
+
+
+def owner_sum_kernel(lines, pieces, g_ref, o_ref, pair_out, pair_in, part, line_in, own_in, p_send, p_recv, l_send, up_recv, down_recv):
+    me = lax.axis_index("dp")
+    line, side = me // 2, lax.rem(me, 2)
+    chunk = o_ref.shape[0]
+    rows = chunk // pieces
+    count = lines * pieces
+    pair = {"dp": line * 2 + 1 - side}
+    above = {"dp": lax.rem(line + 1, lines) * 2 + side}
+    below = {"dp": lax.rem(line + lines - 1, lines) * 2 + side}
+    has_below, has_above = line > 0, line < lines - 1
+
+    def target(step):
+        turn = lax.rem(step, lines)
+        odd = lax.rem(turn, 2)
+        return (1 - odd) * (lines - 1 - turn // 2) + odd * (turn // 2)
+
+    def slot(step):
+        return pl.ds(pl.multiple_of(step * rows, rows), rows)
+
+    def here(step):
+        return pl.ds(pl.multiple_of(step // lines * rows, rows), rows)
+
+    def source(step, owner):
+        return pl.ds(pl.multiple_of((target(step) * 2 + owner) * chunk + step // lines * rows, rows), rows)
+
+    def copy(src, dst, send, recv, to):
+        return pltpu.make_async_remote_copy(
+            src_ref=src, dst_ref=dst, send_sem=send, recv_sem=recv, device_id=to, device_id_type=MESH
+        )
+
+    def pair_copy(step):
+        return copy(pair_out.at[slot(step)], pair_in.at[slot(step)], p_send.at[step], p_recv.at[step], pair)
+
+    def line_copy(step, to, recv):
+        return copy(part.at[slot(step)], line_in.at[slot(step)], l_send.at[step], recv.at[step], to)
+
+    def last_copy(step):
+        return copy(part.at[slot(step)], own_in.at[here(step)], l_send.at[step], down_recv.at[step], below)
+
+    barrier = pltpu.get_barrier_semaphore()
+    pl.semaphore_signal(barrier, inc=1, device_id=pair, device_id_type=MESH)
+
+    @pl.when(has_below)
+    def _():
+        pl.semaphore_signal(barrier, inc=1, device_id=below, device_id_type=MESH)
+
+    @pl.when(has_above)
+    def _():
+        pl.semaphore_signal(barrier, inc=1, device_id=above, device_id_type=MESH)
+
+    pl.semaphore_wait(barrier, 1 + jnp.minimum(line, 1) + jnp.minimum(lines - 1 - line, 1))
+
+    @pl.loop(0, count)
+    def _(step):
+        pair_out[slot(step)] = g_ref[source(step, 1 - side)].astype(jnp.bfloat16)
+        pair_copy(step).start()
+
+    @pl.loop(0, count + lines - 1)
+    def _(step):
+        @pl.when(step < count)
+        def _():
+            pair_copy(step).wait_recv()
+            part[slot(step)] = g_ref[source(step, side)].astype(jnp.float32) + pair_in[slot(step)].astype(jnp.float32)
+
+        rising = step - line
+
+        @pl.when((rising >= 0) & (rising < count) & (target(rising) > line))
+        def _():
+            @pl.when(has_below)
+            def _():
+                line_copy(rising, above, up_recv).wait_recv()
+                part[slot(rising)] += line_in[slot(rising)]
+
+            line_copy(rising, above, up_recv).start()
+
+        falling = step - (lines - 1 - line)
+
+        @pl.when((falling >= 0) & (falling < count) & (target(falling) < line))
+        def _():
+            @pl.when(has_above)
+            def _():
+                line_copy(falling, below, down_recv).wait_recv()
+                part[slot(falling)] += line_in[slot(falling)]
+
+            @pl.when(target(falling) == line - 1)
+            def _():
+                last_copy(falling).start()
+
+            @pl.when(target(falling) < line - 1)
+            def _():
+                line_copy(falling, below, down_recv).start()
+
+    @pl.loop(0, count)
+    def _(step):
+        pair_copy(step).wait_send()
+
+        @pl.when(target(step) > line)
+        def _():
+            line_copy(step, above, up_recv).wait_send()
+
+        @pl.when(target(step) < line)
+        def _():
+            line_copy(step, below, down_recv).wait_send()
+
+        @pl.when(target(step) == line)
+        def _():
+            o_ref[here(step)] = part[slot(step)]
+
+            @pl.when(has_below)
+            def _():
+                line_copy(step, above, up_recv).wait_recv()
+                o_ref[here(step)] += line_in[slot(step)]
+
+            @pl.when(has_above)
+            def _():
+                last_copy(step).wait_recv()
+                o_ref[here(step)] += own_in[here(step)]
+
+
+def owner_sum(grad, count_dp, collective_id, pieces):
+    lines = count_dp // 2
+    total, width = grad.shape
+    chunk = total // count_dp
+    half = (lines * chunk, width)
+    vmem = pl.BlockSpec(memory_space=pltpu.VMEM)
+    return pl.pallas_call(
+        functools.partial(owner_sum_kernel, lines, pieces),
+        out_shape=jax.ShapeDtypeStruct((chunk, width), jnp.float32),
+        in_specs=[vmem],
+        out_specs=vmem,
+        scratch_shapes=[
+            pltpu.VMEM(half, jnp.bfloat16),
+            pltpu.VMEM(half, jnp.bfloat16),
+            pltpu.VMEM(half, jnp.float32),
+            pltpu.VMEM(half, jnp.float32),
+            pltpu.VMEM((chunk, width), jnp.float32),
         ]
-    )
-    return (embed_grad, weight_grad, gain_grad)
-
-
-def pixel_loss(opacity, spread, distance, valid_px, target):
-    contrib = (0.02 + 0.96 * jax.nn.sigmoid(opacity)) * jnp.exp(
-        -0.25 * distance * jax.nn.sigmoid(spread)
-    )
-    keep_log = jnp.sum(jnp.log1p(-contrib), 0)
-    alpha_log = jnp.log(-jnp.expm1(keep_log))
-    return jnp.sum(valid_px * -(target * alpha_log + (1.0 - target) * keep_log))
-
-
-def render_with_grad(gauss_table, splats, distance, valid_px, target):
-    area = PATCH * PATCH
-    slot_count = gauss_table.shape[0]
-    splat_rows, pixel_count = splats.shape
-    block_px = min(128, pixel_count)
-    block_count = pixel_count // block_px
-    slot_ids = jnp.arange(slot_count, dtype=jnp.int32)
-    cell_ids = jnp.arange(area, dtype=jnp.int32)
-
-    def to_blocks(array):
-        return array.reshape(splat_rows, block_count, block_px).transpose(1, 0, 2)
-
-    def one_block(carried, inputs):
-        loss_acc, grad_acc = carried
-        index_part, dist_part, valid_part, target_part = inputs
-        flat_index = index_part.reshape(-1)
-        token_hot = (flat_index[:, None] // area == slot_ids[None, :]).astype(jnp.float32)
-        cell_hot = (flat_index[:, None] % area == cell_ids[None, :]).astype(jnp.float32)
-        picked = jnp.dot(
-            token_hot,
-            gauss_table,
-            precision=lax.Precision.HIGHEST,
-            preferred_element_type=jnp.float32,
+        + [pltpu.SemaphoreType.DMA((lines * pieces,))] * 5,
+        compiler_params=pltpu.CompilerParams(
+            collective_id=collective_id, has_side_effects=True, vmem_limit_bytes=62 * 2**20
+        ),
+    )(grad)
+
+
+def total_kernel(mine_ref, sum_ref, slots, own_sem, send_sem, recv_sem):
+    first, second = lax.axis_size("dp"), lax.axis_size("tensor")
+    count = first * second
+    me = lax.axis_index("dp") * second + lax.axis_index("tensor")
+
+    def peer(step):
+        other = lax.rem(me + step, count)
+        return {"dp": other // second, "tensor": lax.rem(other, second)}
+
+    barrier = pltpu.get_barrier_semaphore()
+
+    @pl.loop(1, count)
+    def _(step):
+        pl.semaphore_signal(barrier, inc=1, device_id=peer(step), device_id_type=MESH)
+
+    pl.semaphore_wait(barrier, count - 1)
+    own = pltpu.make_async_copy(mine_ref, slots.at[me], own_sem)
+    own.start()
+
+    def send(step):
+        return pltpu.make_async_remote_copy(
+            src_ref=mine_ref,
+            dst_ref=slots.at[me],
+            send_sem=send_sem.at[step],
+            recv_sem=recv_sem.at[step],
+            device_id=peer(step),
+            device_id_type=MESH,
         )
-        opacity = jnp.sum(picked[:, :area] * cell_hot, 1).reshape(index_part.shape)
-        spread = jnp.sum(picked[:, area:] * cell_hot, 1).reshape(index_part.shape)
-        part_loss, part_back = jax.vjp(
-            lambda op_in, sp_in: pixel_loss(op_in, sp_in, dist_part, valid_part, target_part),
-            opacity,
-            spread,
-        )
-        grad_op, grad_sp = part_back(jnp.float32(1.0))
-        weighted = jnp.concatenate(
-            [grad_op.reshape(-1, 1) * cell_hot, grad_sp.reshape(-1, 1) * cell_hot], 1
-        )
-        grad_acc = grad_acc + lax.dot_general(
-            token_hot,
-            weighted,
-            (((0,), (0,)), ((), ())),
-            precision=lax.Precision.HIGHEST,
-            preferred_element_type=jnp.float32,
-        )
-        return ((loss_acc + part_loss, grad_acc), None)
-
-    inputs = (
-        to_blocks(splats),
-        to_blocks(distance),
-        valid_px.reshape(block_count, block_px),
-        target.reshape(block_count, block_px),
-    )
-    start = (jnp.zeros((), jnp.float32), jnp.zeros(gauss_table.shape, jnp.float32))
-    (loss_part, table_grad), unused = lax.scan(one_block, start, inputs)
-    return (loss_part, table_grad)
-
+
+    @pl.loop(1, count)
+    def _(step):
+        send(step).start()
+
+    @pl.loop(1, count)
+    def _(step):
+        send(step).wait()
+
+    own.wait()
+    sum_ref[...] = jnp.sum(slots[...], 0)
+
+
+def total_over_all(mine, collective_id):
+    count = lax.axis_size("dp") * lax.axis_size("tensor")
+    vmem = pl.BlockSpec(memory_space=pltpu.VMEM)
+    return pl.pallas_call(
+        total_kernel,
+        out_shape=jax.ShapeDtypeStruct(mine.shape, jnp.float32),
+        in_specs=[vmem],
+        out_specs=vmem,
+        scratch_shapes=[
+            pltpu.VMEM((count,) + mine.shape, jnp.float32),
+            pltpu.SemaphoreType.DMA(()),
+            pltpu.SemaphoreType.DMA((count,)),
+            pltpu.SemaphoreType.DMA((count,)),
+        ],
+        compiler_params=pltpu.CompilerParams(collective_id=collective_id, has_side_effects=True),
+    )(mine)
+
+
+def pack_qkv(matrix, parts):
+    rows, cols = matrix.shape
+    first = matrix[:, :512].reshape(parts, 2, rows // parts // 2, 512).transpose(0, 2, 1, 3)
+    second = matrix[:, 512:].reshape(parts, 4, rows // parts // 4, 256).transpose(0, 2, 1, 3)
+    return jnp.concatenate([first.reshape(parts, -1, 1024), second.reshape(parts, -1, 1024)], 1).reshape(-1, 1024)
+
+
+def unpack_qkv(packed, parts):
+    rows = packed.shape[0] // parts
+    packed = packed.reshape(parts, rows, 1024)
+    cut = rows * 2 // 3
+    first = packed[:, :cut].reshape(parts, cut, 2, 512).transpose(0, 2, 1, 3).reshape(-1, 512)
+    second = packed[:, cut:].reshape(parts, rows - cut, 4, 256).transpose(0, 2, 1, 3).reshape(-1, 256)
+    return jnp.concatenate([first, second], 1)
+
+
+def by_lanes(flat, outer):
+    size = flat.size // math.prod(outer)
+    return flat.reshape(outer + ((size // 128, 128) if size % 128 == 0 else (size,)))
+
+
+def pad_first(array, axis, unit):
+    short = -array.shape[axis] % unit
+    return jnp.pad(array, [(0, short if at == axis else 0) for at in range(array.ndim)])
+
+
+def sum_to_owners(stack, count_dp):
+    if count_dp == 8:
+        return owner_sum(stack, count_dp, 1, 9)
+    return lax.psum_scatter(stack, "dp", scatter_dimension=0, tiled=True)
 
 def adam_update(master, first_mom, second_mom, gradient, step_float):
     first_new = beta_one * first_mom + (1.0 - beta_one) * gradient
@@ -325,28 +579,39 @@
     shared_second,
     shared_ema,
 ):
-    my_slot = lax.axis_index("tensor")
     groups = lax.axis_size("tensor")
-    row_weights, shared_weights = (
-        lax.all_gather(row_master[0].astype(jnp.bfloat16), "dp", axis=0, tiled=True),
-        lax.all_gather(shared_master.astype(jnp.bfloat16), "dp", axis=0, tiled=True),
-    )
+    my_dp = lax.axis_index("dp")
+    count_dp = lax.axis_size("dp")
     local_width = D // groups
     local_hidden = FF // groups
-    qkv_end = 3 * D * local_width
-    out_end = qkv_end + local_width * D
-    up_end = out_end + D * local_hidden
+    qkv_parts = count_dp // 4
+    share_rows = row_master.shape[1] // D
+    own_row = row_master[0].astype(jnp.bfloat16)
+    own_tiles = jnp.where(
+        my_dp < qkv_parts,
+        pack_qkv(own_row.reshape(-1, 3 * local_width), 1),
+        own_row.reshape(share_rows, D),
+    )
+    row_weights = lax.all_gather(own_tiles, "dp", axis=0, tiled=True)
+    own_flat = shared_master.astype(jnp.bfloat16)
+    own_shared = by_lanes(own_flat, ())
+    lead = own_shared.shape[0]
+    own_shared = pad_first(own_shared, 0, 2048 // own_shared[0].size)
+    shared_weights = lax.all_gather(own_shared, "dp", axis=0, tiled=False)[:, :lead].reshape(-1, 128)
+    qkv_rows = 3 * local_width
+    out_end = qkv_rows + local_width
+    up_end = out_end + local_hidden
+    patch_rows = PIN * D // 128
+    unpatch_rows = D * POUT // 128
     weights = (
-        row_weights[:qkv_end].reshape(D, 3 * local_width),
-        row_weights[qkv_end:out_end].reshape(local_width, D),
-        row_weights[out_end:up_end].reshape(D, local_hidden),
-        row_weights[up_end:].reshape(local_hidden, D),
-        shared_weights[PIN * D + D * POUT :].reshape(4, D).astype(jnp.float32),
-    )
-    patch_proj = shared_weights[: PIN * D].reshape(PIN, D)
-    used_cols = shared_weights[PIN * D : PIN * D + D * POUT].reshape(D, POUT)[
-        :, : 2 * PATCH * PATCH
-    ]
+        unpack_qkv(row_weights[:qkv_rows], qkv_parts),
+        row_weights[qkv_rows:out_end],
+        row_weights[out_end:up_end],
+        row_weights[up_end:],
+        shared_weights[patch_rows + unpatch_rows :].reshape(4, D).astype(jnp.float32),
+    )
+    patch_proj = shared_weights[:patch_rows].reshape(PIN, D)
+    used_cols = shared_weights[patch_rows : patch_rows + unpatch_rows].reshape(D, POUT // 128, 128)[:, 0]
     own_patches = patches[0]
     row_count = own_patches.shape[0]
     key_valid = jnp.arange(row_count * groups) < view_counts[0] * VTOK
@@ -358,16 +623,10 @@
         "tensor",
         axis=0,
         tiled=True,
-    ).astype(jnp.float32)
-    labels = alpha_label[0]
-    valid_px = (labels < 2).astype(jnp.float32)
-    target = (labels == 1).astype(jnp.float32)
-    loss_part, table_grad = render_with_grad(
-        gauss_table, splat_index[0], splat_dist[0].astype(jnp.float32), valid_px, target
-    )
-    gauss_grad = lax.psum_scatter(
-        table_grad.astype(jnp.bfloat16), "tensor", scatter_dimension=0, tiled=True
-    )
+    )
+    loss_tile, table_grad = render(gauss_table, splat_index[0], splat_dist[0], alpha_label, PATCH * PATCH)
+    loss_part = loss_tile[0, 0]
+    gauss_grad = lax.psum_scatter(table_grad, "tensor", scatter_dimension=0, tiled=True)
     unpatch_used = contract_rows(resid2_low, gauss_grad)
     resid2_grad = contract_last(gauss_grad, used_cols)
     embed_grad, weight_grad, gain_grad = layer_backward(
@@ -380,17 +639,25 @@
     shared_grad = jnp.concatenate(
         [patch_grad.reshape(-1), unpatch_grad.reshape(-1), gain_grad.reshape(-1)]
     )
-    row_share, shared_part = (
-        lax.psum_scatter(weight_grad, "dp", scatter_dimension=0, tiled=True),
-        lax.psum_scatter(shared_grad, "dp", scatter_dimension=0, tiled=True),
-    )
-    shared_share = lax.psum(shared_part, "tensor")
-    own_squares = jnp.sum(row_share * row_share) + jnp.where(
-        my_slot == 0, jnp.sum(shared_share * shared_share), 0.0
-    )
-    square_total, loss_total, pixel_total = lax.psum(
-        (own_squares, loss_part, jnp.sum(valid_px)), ("dp", "tensor")
-    )
+    split_grad = by_lanes(shared_grad, (count_dp, groups))
+    lead = split_grad.shape[2]
+    shared_stack = pad_first(split_grad, 2, 16 * D // split_grad[0, 0, 0].size).swapaxes(0, 1)
+    shared_sum = lax.psum_scatter(shared_stack, "tensor", scatter_dimension=0, tiled=True)
+    qkv_grad, out_grad, up_grad, down_grad = weight_grad
+    row_stack = jnp.concatenate([pack_qkv(qkv_grad, qkv_parts), out_grad, up_grad, down_grad], 0)
+    stack = jnp.concatenate(
+        [row_stack.reshape(count_dp, share_rows, D), shared_sum.reshape(count_dp, -1, D)], 1
+    ).reshape(-1, D)
+    own_share = sum_to_owners(stack, count_dp)
+    own_rows = own_share[:share_rows]
+    row_share = jnp.where(my_dp < qkv_parts, unpack_qkv(own_rows, 1).reshape(-1), own_rows.reshape(-1))
+    shared_part = own_share[share_rows:].reshape((-1,) + split_grad.shape[3:])[:lead]
+    shared_share = lax.all_gather(shared_part, "tensor", axis=0, tiled=False).reshape(-1)
+    own_squares = jnp.sum(row_share * row_share) + jnp.sum(shared_part * shared_part)
+    pixel_part = jnp.sum((alpha_label < 2).astype(jnp.float32))
+    scalars = jnp.stack([own_squares, loss_part, pixel_part]).reshape(3, 1)
+    totals = total_over_all(jnp.pad(jnp.broadcast_to(scalars, (3, 128)), ((0, 5), (0, 0))), 2)
+    square_total, loss_total, pixel_total = totals[0, 0], totals[1, 0], totals[2, 0]
     norm_value = jnp.sqrt(square_total) / pixel_total
     factor = clip_norm / jnp.maximum(norm_value, clip_norm) / pixel_total
     step_float = step_count[0].astype(jnp.float32)

time: 1860 us -> 1110 us (0.60)
  waiting for transfers between devices: 947 us -> 489 us
  matrix products: 500 us -> 152 us
  Pallas kernels: 0 us -> 198 us
  other arithmetic: 197 us -> 110 us
  loops' own time: 33.2 us -> 0.17 us
  blocking collectives: 46.8 us -> 15 us
    unnamed x14 -> x16, waiting for transfers between devices: 545 us -> 170 us
    dot_general x96 -> x0, matrix products: 332 us -> none  [the longest x48 187 us: one_block(): lax.dot_general(token_hot, weighted, (((0,), (0,)), ((), ())), precision=...]
    pallas_call x0 -> x3, Pallas kernels: none -> 198 us  [the longest x1 138 us: owner_sum(): pl.pallas_call(functools.partial(owner_sum_kernel, lines, pieces), out_sh...]
    reduce_scatter x4 -> x1, waiting for transfers between devices: 115 us -> 21.2 us  [per_device(): lax.psum_scatter(table_grad, 'tensor', scatter_dimension=0, tiled=True)]
    all_gather x1 -> x0, other arithmetic: 41.4 us -> none  [per_device(): lax.all_gather(shared_master.astype(jnp.bfloat16), 'dp', axis=0, tiled=True)]
    psum x1 -> x0, blocking collectives: 40.5 us -> none  [per_device(): lax.psum((own_squares, loss_part, jnp.sum(valid_px)), ('dp', 'tensor'))]
    another operation x1 -> x0, loops' own time: 32.8 us -> none  [render_with_grad(): (loss_part, table_grad), unused = lax.scan(one_block, start, inputs)]
    select_n x48 -> x1, other arithmetic: 33.1 us -> 1.18 us  [per_device(): jnp.where(my_dp < qkv_parts, pack_qkv(own_row.reshape(-1, 3 * local_width...]
  transfers between devices with their start and end apart: 13 -> 12, of which waited for: 12 -> 12; matrix products, arithmetic and copies ran while one was open for 7% -> 9% of each run, Pallas kernels for 0% -> 0%
where the time goes in v1:
time: 1110 us; the launch traced here: 1100 us
  waiting for transfers between devices  489 us (44%)
  Pallas kernels  198 us (18%)
  matrix products  152 us (14%)
  local copies, waits for them, and re-layouts  113 us (10%)
  other arithmetic  110 us (10%)
  between operations  23.9 us (2%)
  blocking collectives  15 us (1%)
    unnamed x16, waiting for transfers between devices  170 us
    pallas_call x1, Pallas kernels, owner_sum(): pl.pallas_call(functools.partial(owner_sum_kernel, lines, pieces), out_sh...  138 us
    all_gather x1, waiting for transfers between devices, per_device(): row_weights = lax.all_gather(own_tiles, 'dp', axis=0, tiled=True)  88.9 us
    reduce_scatter x1, waiting for transfers between devices, layer_forward(): lax.psum_scatter(jnp.dot(attended, out_proj, preferred_element_type=jnp.f...  58.3 us
    pallas_call x1, Pallas kernels, render(): pl.pallas_call(functools.partial(render_kernel, area, wide, block, split)...  50 us
    all_gather x1, waiting for transfers between devices, per_device(): lax.all_gather(own_shared, 'dp', axis=0, tiled=False)[:, :lead]  40.1 us
    unnamed x151, local copies, waits for them, and re-layouts  29.7 us
    dot_general x5, matrix products, contract_last(): lax.dot_general(left_op, right_op, (((1,), (1,)), ((), ())), preferred_el...  28.7 us
  transfers between devices with their start and end apart: 12, of which 12 were waited for; matrix products, arithmetic and copies ran while one was open for 9% of the time, Pallas kernels for 0%

profile of v1, /device:TPU:0, one launch (start us, length us, event | category | flops | bytes accessed | tf_op | source)
XLA Modules:
  0.0 1102.4 jit_solution(1411132580378490866)
XLA Ops:
  9.4 16.3 %convert_reduce_fusion.2 = bf16[393216]{0:T(1024)(128)(2,1)S(1)} fusion(f32[1,393216]{1,0:T(1,128)S(1)} %copy-done.23), kind=kLoop, calls=%fused_computation.119 | loop fusion | flops 393216 | bytes 2359296 | tf_op jit(solution)/shard_map/convert_element_type | solution.py:589
  29.8 40.1 %all-gather.20.cloned.1.call-done = bf16[10880,128]{1,0:T(8,128)(2,1)} async-done(((bf16[1360,128]{1,0:T(8,128)(2,1)}), bf16[10880,128]{1,0:T(8,128)(2,1)}) %all-gather.20.cloned.1.call-update) | async-done | bytes 2785296 | tf_op jit(solution)/shard_map/all_gather | solution.py:600
  81.4 88.9 %all-gather.12.cloned.1.call-done = bf16[3072,1024]{1,0:T(8,128)(2,1)} async-done(((bf16[384,1024]{1,0:T(8,128)(2,1)}), bf16[3072,1024]{1,0:T(8,128)(2,1)}) %all-gather.12.cloned.1.call-update) | async-done | bytes 6291472 | tf_op jit(solution)/shard_map/all_gather | solution.py:595
  174.4 24.8 %all-gather.10.cloned.1.call-done = bf16[1536,1024]{0,1:T(8,128)(2,1)} async-done(((bf16[384,1024]{0,1:T(8,128)(2,1)}), bf16[1536,1024]{0,1:T(8,128)(2,1)}) %all-gather.10.cloned.1.call-update) | async-done | bytes 3145744 | tf_op jit(solution)/shard_map/all_gather | solution.py:133
  207.9 29.1 %while.28 = (s32[]{:T(128)}, bf16[3,512,4,64]{1,3,2,0:T(8,128)(2,1)}, f32[3,4,512]{2,1,0:T(4,128)}, bf16[3,512,4,64]{1,3,2,0:T(8,128)(2,1)S(1)}, bf16[1536,4,64]...) while((s32[]{:T(128)}, bf16[3,512,4,64]{1,3,2,0:T(8,128)(2,1)}, ...), condition=%wide.region_5.6_spmd.clone, body=%wide.region_2.5_spmd.clone.sunk | while | flops 843054592 | bytes 40180332 | solution.py:82
  245.5 58.3 %reduce-scatter.15.cloned.1.call-done = f32[384,1024]{0,1:T(8,128)} async-done(((f32[1536,1024]{0,1:T(8,128)}), f32[384,1024]{0,1:T(8,128)}) %reduce-scatter.15.cloned.1.call-update) | async-done | bytes 1572880 | tf_op jit(solution)/shard_map/reduce_scatter | solution.py:142
  307.5 28.6 %all-gather.14.cloned.1.call-done = bf16[1536,1024]{0,1:T(8,128)(2,1)} async-done(((bf16[384,1024]{0,1:T(8,128)(2,1)}), bf16[1536,1024]{0,1:T(8,128)(2,1)}) %all-gather.14.cloned.1.call-update) | async-done | bytes 3145744 | tf_op jit(solution)/shard_map/all_gather | solution.py:149
  336.1 20.1 %multiply_convert_fusion.1 = (bf16[1536,1024]{1,0:T(8,128)(2,1)S(1)}, f32[1536,1024]{1,0:T(8,128)}, f32[1536,1024]{1,0:T(8,128)}) fusion(bf16[1536,1024]{0,1:T(8,128)(2,1)} %all-gather.14.cloned.1.call-done, bf16[3072,1024]{1,0:T(8,128)(2,1)} %all-gather.12.cloned.1.call-done), kind=kOutput, calls=%fused_computation.52 | convolution fusion | flops 3323461632 | bytes 20971520 | tf_op jit(solution)/shard_map/dot_general | solution.py:150
  373.0 29.2 %reduce-scatter.19.cloned.1.call-done = bf16[384,1024]{1,0:T(8,128)(2,1)} async-done(((bf16[1536,1024]{1,0:T(8,128)(2,1)}), bf16[384,1024]{1,0:T(8,128)(2,1)}) %reduce-scatter.19.cloned.1.call-update) | async-done | bytes 786448
  412.4 50.0 %shard_map.229 = (f32[8,128]{1,0:T(8,128)S(1)}, bf16[1536,128]{1,0:T(8,128)(2,1)}) custom-call(bf16[1536,128]{1,0:T(8,128)(2,1)S(1)} %all_gather.35.table_ref, s32[4,6144]{1,0:T(4,128)S(1)} %bitcast.251, s32[4,6144]{1,0:T(4,128)S(1)} %bitcast.252, s32[1,6144]{1,0:T(1,128)S(1)} %copy-done.1), custom_call_target="tpu_custom_call" | custom-call | tf_op jit(solution)/shard_map/pallas_call | solution.py:311
  462.5 21.2 %reduce-scatter.17.cloned.1.call-done = bf16[384,128]{1,0:T(8,128)(2,1)} async-done(((bf16[1536,128]{1,0:T(8,128)(2,1)}), bf16[384,128]{1,0:T(8,128)(2,1)}) %reduce-scatter.17.cloned.1.call-update) | async-done | bytes 98320 | tf_op jit(solution)/shard_map/reduce_scatter | solution.py:629
  486.7 28.4 %all-gather.16.cloned.1.call-done = bf16[1536,1024]{1,0:T(8,128)(2,1)} async-done(((bf16[384,1024]{1,0:T(8,128)(2,1)}), bf16[1536,1024]{1,0:T(8,128)(2,1)}) %all-gather.16.cloned.1.call-update) | async-done | bytes 3145744 | tf_op jit(solution)/shard_map/all_gather | solution.py:195
  515.1 11.4 %add_convert_fusion = bf16[1536,1024]{1,0:T(8,128)(2,1)S(1)} fusion(f32[1536,1024]{1,0:T(8,128)} %get-tuple-element.285, f32[1536,1024]{1,0:T(8,128)} %get-tuple-element.310, bf16[1536,1024]{1,0:T(8,128)(2,1)} %all-gather.16.cloned.1.call-done, bf16[3072,1024]{1,0:T(8,128)(2,1)} %all-gather.12.cloned.1.call-done), kind=kOutput, calls=%fused_computation.51 | convolution fusion | flops 3243245568 | bytes 20971520 | tf_op jit(solution)/shard_map/dot_general | solution.py:40
  537.7 35.0 %reduce-scatter.21.cloned.1.call-done = bf16[384,1024]{1,0:T(8,128)(2,1)} async-done(((bf16[1536,1024]{1,0:T(8,128)(2,1)}), bf16[384,1024]{1,0:T(8,128)(2,1)}) %reduce-scatter.21.cloned.1.call-update) | async-done | bytes 786448
  580.8 28.2 %all-gather.18.cloned.1.call-done = bf16[1536,1024]{0,1:T(8,128)(2,1)} async-done(((bf16[384,1024]{0,1:T(8,128)(2,1)}), bf16[1536,1024]{0,1:T(8,128)(2,1)}) %all-gather.18.cloned.1.call-update) | async-done | bytes 3145744 | tf_op jit(solution)/shard_map/all_gather | solution.py:208
  620.9 58.9 %while.29 = (s32[]{:T(128)}, f32[1536,4,64]{0,2,1:T(8,128)}, f32[1536,4,64]{0,2,1:T(8,128)}, bf16[3,512,4,64]{1,3,2,0:T(8,128)(2,1)}, bf16[3,512,4,64]{1,3,2,0:T...) while((s32[]{:T(128)}, f32[1536,4,64]{0,2,1:T(8,128)}, ...), condition=%wide.region_16.17_spmd.clone, body=%wide.region_14.16_spmd.clone.sunk | while | flops 2043674112 | bytes 148680496 | solution.py:116
  699.3 28.3 %reduce-scatter.23.cloned.1.call-done = bf16[384,1024]{1,0:T(8,128)(2,1)} async-done(((bf16[1536,1024]{1,0:T(8,128)(2,1)}), bf16[384,1024]{1,0:T(8,128)(2,1)}) %reduce-scatter.23.cloned.1.call-update) | async-done | bytes 786448
  755.6 8.5 fusion.114
  797.7 77.6 %all-reduce.7.cloned.1.call-done = f32[4,8,384,128]{3,2,0,1:T(8,128)} async-done(((f32[4,8,384,128]{3,2,0,1:T(8,128)}), f32[4,8,384,128]{3,2,0,1:T(8,128)}) %all-reduce.7.cloned.1.call-update) | async-done | bytes 6291472
  880.1 10.1 pad_maximum_fusion
  890.2 138.1 %shard_map.230 = f32[432,1024]{1,0:T(8,128)} custom-call(f32[3456,1024]{1,0:T(8,128)} %bitcast.255), custom_call_target="tpu_custom_call" | custom-call | tf_op jit(solution)/shard_map/pallas_call | solution.py:446
  1031.5 8.9 all-gather.2
  1057.2 9.6 shard_map.231
  1076.1 13.4 %fusion.104 = (bf16[1,393216]{1,0:T(2,128)(2,1)}, f32[1,393216]{1,0:T(1,128)S(1)}, f32[1,393216]{1,0:T(1,128)}, f32[1,393216]{1,0:T(1,128)}) fusion(f32[1,393216]{1,0:T(1,128)S(1)} %copy-done.24, f32[]{:T(128)} %bitcast.56, f32[]{:T(128)} %bitcast.55, f32[]{:T(128)S(6)} %div.84, f32[1,393216]{1,0:T(1,128)S(1)} %bitcast.263, f32[1,393216]{1,0:T(1,128)S(1)} %bitcast.264, ...), kind=kLoop, calls=%fused_computation.183 | loop fusion | flops 7077888 | bytes 13369357 | tf_op jit(solution)/shard_map/convert_element_type | solution.py:679
  (349 shorter events, 303.2 us)
Async XLA Ops:
  7.2 68.8 %copy-start = (bf16[1,384,576]{1,2,0:T(8,128)(2,1)S(1)}, bf16[1,384,576]{1,2,0:T(8,128)(2,1)}, u32[]{:S(2)}) copy-start(bf16[1,384,576]{1,2,0:T(8,128)(2,1)} %param.18) | copy-start | bytes 1327108
  7.2 62.7 %all-gather.20.cloned.1.call-start = ((), (), s32[]{:S(2)}) async-start(), calls=%async_computation.12 | async-start | bytes 3133440 | tf_op jit(solution)/shard_map/all_gather | solution.py:600
  9.3 161.0 %all-gather.12.cloned.1.call-start = ((), (), s32[]{:S(2)}) async-start(), calls=%async_computation.6 | async-start | bytes 7077888 | tf_op jit(solution)/shard_map/all_gather | solution.py:595
  29.7 169.4 %all-gather.10.cloned.1.call-start = ((), (), s32[]{:S(2)}) async-start(), calls=%async_computation.5 | async-start | bytes 3932160 | tf_op jit(solution)/shard_map/all_gather | solution.py:133
  80.2 223.6 %reduce-scatter.15.cloned.1.call-start = ((), (), s32[]{:S(2)}) async-start(), calls=%async_computation.7 | async-start | bytes 7864320 | tf_op jit(solution)/shard_map/reduce_scatter | solution.py:142
  245.3 60.9 %copy-start.46 = (f32[1024]{0:T(1024)S(1)}, f32[1024]{0:T(1024)}, u32[]{:S(2)}) copy-start(f32[1024]{0:T(1024)} %get-tuple-element.301) | copy-start | bytes 12292
  245.3 60.9 %copy-start.66 = (f32[1024]{0:T(1024)S(1)}, f32[1024]{0:T(1024)}, u32[]{:S(2)}) copy-start(f32[1024]{0:T(1024)} %get-tuple-element.302) | copy-start | bytes 12292
  245.3 90.8 %all-gather.14.cloned.1.call-start = ((), (), s32[]{:S(2)}) async-start(), calls=%async_computation.8 | async-start | bytes 3932160 | tf_op jit(solution)/shard_map/all_gather | solution.py:149
  305.9 271.7 %copy-start.5 = (f32[384,1024]{0,1:T(8,128)}, f32[384,1024]{0,1:T(8,128)S(1)}, u32[]{:S(2)}) copy-start(f32[384,1024]{0,1:T(8,128)S(1)} %get-tuple-element.287) | copy-start | bytes 4718596
  306.0 50.2 %copy-start.48 = (f32[384]{0:T(512)}, f32[384]{0:T(512)S(1)}, u32[]{:S(2)}) copy-start(f32[384]{0:T(512)S(1)} %broadcast_multiply_fusion.5) | copy-start | bytes 4612
  306.2 50.0 %copy-start.55 = (f32[384]{0:T(512)}, f32[384]{0:T(512)S(1)}, u32[]{:S(2)}) copy-start(f32[384]{0:T(512)S(1)} %add_rsqrt_fusion) | copy-start | bytes 4612
  307.5 94.8 %reduce-scatter.19.cloned.1.call-start = ((), (), s32[]{:S(2)}) async-start(), calls=%async_computation.13 | async-start | bytes 3932160
  364.2 119.5 %reduce-scatter.17.cloned.1.call-start = ((), (), s32[]{:S(2)}) async-start(), calls=%async_computation.9 | async-start | bytes 491520 | tf_op jit(solution)/shard_map/reduce_scatter | solution.py:629
  370.7 41.6 %copy-start.1 = (s32[1,6144]{1,0:T(1,128)S(1)}, s32[1,6144]{1,0:T(1,128)}, u32[]{:S(2)}) copy-start(s32[1,6144]{1,0:T(1,128)} %label_ref.1) | copy-start | bytes 73732
  370.7 41.6 %copy-start.2 = (s32[1,4,6144]{2,1,0:T(4,128)S(1)}, s32[1,4,6144]{2,1,0:T(4,128)}, u32[]{:S(2)}) copy-start(s32[1,4,6144]{2,1,0:T(4,128)} %param.20) | copy-start | bytes 294916
  370.7 41.6 %copy-start.3 = (s32[1,4,6144]{2,1,0:T(4,128)S(1)}, s32[1,4,6144]{2,1,0:T(4,128)}, u32[]{:S(2)}) copy-start(s32[1,4,6144]{2,1,0:T(4,128)} %param.21) | copy-start | bytes 294916
  462.4 52.7 %all-gather.16.cloned.1.call-start = ((), (), s32[]{:S(2)}) async-start(), calls=%async_computation.10 | async-start | bytes 3932160 | tf_op jit(solution)/shard_map/all_gather | solution.py:195
  486.4 86.3 %reduce-scatter.21.cloned.1.call-start = ((), (), s32[]{:S(2)}) async-start(), calls=%async_computation.14 | async-start | bytes 3932160
  534.6 40.4 %copy-start.49 = (f32[384]{0:T(512)S(1)}, f32[384]{0:T(512)}, u32[]{:S(2)}) copy-start(f32[384]{0:T(512)} %copy-done.48) | copy-start | bytes 4612
  534.6 40.4 %copy-start.56 = (f32[384]{0:T(512)S(1)}, f32[384]{0:T(512)}, u32[]{:S(2)}) copy-start(f32[384]{0:T(512)} %copy-done.55) | copy-start | bytes 4612
  534.6 74.4 %all-gather.18.cloned.1.call-start = ((), (), s32[]{:S(2)}) async-start(), calls=%async_computation.11 | async-start | bytes 3932160 | tf_op jit(solution)/shard_map/all_gather | solution.py:208
  580.3 147.3 %reduce-scatter.23.cloned.1.call-start = ((), (), s32[]{:S(2)}) async-start(), calls=%async_computation.15 | async-start | bytes 3932160
  689.5 185.8 %all-reduce.7.cloned.1.call-start = ((), (), s32[]{:S(2)}) async-start(), calls=%async_computation.16 | async-start | bytes 12582912
  694.5 35.4 %copy-start.59 = (f32[384]{0:T(512)S(1)}, f32[384]{0:T(512)}, u32[]{:S(2)}) copy-start(f32[384]{0:T(512)} %copy-done.58) | copy-start | bytes 4612
  (73 other events, 650.8 us)
Sparse Core Ops, SparseCore 0:
  10.8 59.1 all-gather.19
  72.7 97.6 all-gather.11
  172.5 26.6 all-gather.9
  245.4 58.3 reduce-scatter.14
  307.6 28.4 all-gather.13
  364.3 37.9 reduce-scatter.18
  462.5 21.1 reduce-scatter.16
  486.5 28.5 all-gather.15
  534.7 37.9 reduce-scatter.20
  580.4 28.4 all-gather.17
  689.6 37.9 reduce-scatter.22
  755.7 119.5 all-reduce.6

commit v2 on v1

--- a/solution.py
+++ b/solution.py
@@ -1,4 +1,3 @@
-import functools
 import math
 from functools import partial
 
@@ -9,7 +8,6 @@
 from jax.experimental.pallas import tpu as pltpu
 from jax.sharding import PartitionSpec as P
 
-MESH = pl.DeviceIdType.MESH
 D = 1024
 DH = 64
 FF = 4096
@@ -17,6 +15,9 @@
 VTOK = 192
 PIN = 576
 POUT = 768
+VMEM = pl.BlockSpec(memory_space=pltpu.VMEM)
+ROOT_HALF = 0.5**0.5
+NORMAL_PEAK = (2.0 * math.pi) ** -0.5
 
 
 clip_norm = 0.005
@@ -30,27 +31,169 @@
 masked_score = -1e30
 
 
-def contract_rows(left_op, right_op):
-    return lax.dot_general(
-        left_op, right_op, (((0,), (0,)), ((), ())), preferred_element_type=jnp.float32
-    )
-
-
-def contract_last(left_op, right_op):
-    return lax.dot_general(
-        left_op, right_op, (((1,), (1,)), ((), ())), preferred_element_type=jnp.float32
-    )
-
-
-def layer_norm(residual, gain_vec, bias_vec):
-    centre = residual - jnp.mean(residual, -1, keepdims=True)
+MESH = pl.DeviceIdType.MESH
+NN = (((1,), (0,)), ((), ()))
+NT = (((1,), (1,)), ((), ()))
+TN = (((0,), (0,)), ((), ()))
+LOW = jnp.bfloat16
+WIDE = jnp.float32
+PIECES = 4
+TILE = 256
+
+
+def dot(left, right, dims=NN):
+    return lax.dot_general(left, right, dims, preferred_element_type=WIDE)
+
+
+def remote(src, dst, send, recv, to):
+    return pltpu.make_async_remote_copy(
+        src_ref=src, dst_ref=dst, send_sem=send, recv_sem=recv, device_id=to, device_id_type=MESH
+    )
+
+
+class Corner:
+    def __init__(self):
+        self.me = lax.axis_index("tensor")
+        self.first, self.last = self.me // 2, lax.rem(self.me, 2)
+        self.mate = self.first * 2 + 1 - self.last
+        self.far = (1 - self.first) * 2 + self.last
+        self.opposite = (1 - self.first) * 2 + 1 - self.last
+
+    def block(self, step):
+        return lax.rem(self.first + 1 - step // 2, 2) * 2 + lax.rem(self.last + 1 - lax.rem(step, 2), 2)
+
+    def greet(self):
+        barrier = pltpu.get_barrier_semaphore()
+        for other in (self.mate, self.far):
+            pl.semaphore_signal(barrier, inc=1, device_id={"tensor": other}, device_id_type=MESH)
+        pl.semaphore_wait(barrier, 2)
+
+
+class Gather:
+    def __init__(self, corner, ref, pieces, sems):
+        self.corner, self.ref, self.pieces, self.sems = corner, ref, pieces, sems
+        self.size = ref.shape[0] // 4
+        self.rows = self.size // pieces
+
+    @staticmethod
+    def scratch(pieces):
+        return [pltpu.SemaphoreType.DMA((pieces,))] * 6
+
+    def part(self, owner, piece):
+        return pl.ds(pl.multiple_of(owner * self.size + piece * self.rows, self.rows), self.rows)
+
+    def copy(self, owner, piece, kind, to):
+        here = self.ref.at[self.part(owner, piece)]
+        return remote(here, here, self.sems[2 * kind].at[piece], self.sems[2 * kind + 1].at[piece], {"tensor": to})
+
+    def start(self, piece):
+        self.copy(self.corner.me, piece, 1, self.corner.far).start()
+        self.copy(self.corner.me, piece, 0, self.corner.mate).start()
+
+    def relay(self, piece):
+        self.copy(self.corner.far, piece, 1, self.corner.far).wait_recv()
+        self.copy(self.corner.far, piece, 2, self.corner.mate).start()
+
+    def finish(self):
+        corner = self.corner
+        for piece in range(self.pieces):
+            self.copy(corner.mate, piece, 0, corner.mate).wait_recv()
+            self.copy(corner.opposite, piece, 2, corner.mate).wait_recv()
+            self.copy(corner.me, piece, 0, corner.mate).wait_send()
+            self.copy(corner.me, piece, 1, corner.far).wait_send()
+            self.copy(corner.far, piece, 2, corner.mate).wait_send()
+
+
+class Scatter:
+    def __init__(self, corner, pieces, mate_out, mate_in, far_out, far_in, mate_send, mate_recv, far_send, far_recv):
+        self.corner, self.pieces = corner, pieces
+        self.mate_out, self.mate_in, self.far_out, self.far_in = mate_out, mate_in, far_out, far_in
+        self.sems = mate_send, mate_recv, far_send, far_recv
+        self.rows = far_out.shape[0] // pieces
+
+    @staticmethod
+    def scratch(rows, width, pieces):
+        return [
+            pltpu.VMEM((2, rows, width), LOW),
+            pltpu.VMEM((2, rows, width), LOW),
+            pltpu.VMEM((rows, width), LOW),
+            pltpu.VMEM((rows, width), LOW),
+            pltpu.SemaphoreType.DMA((2, pieces)),
+            pltpu.SemaphoreType.DMA((2, pieces)),
+            pltpu.SemaphoreType.DMA((pieces,)),
+            pltpu.SemaphoreType.DMA((pieces,)),
+        ]
+
+    def part(self, piece):
+        return pl.ds(piece * self.rows, self.rows)
+
+    def mate_copy(self, half, piece):
+        part = self.part(piece)
+        return remote(
+            self.mate_out.at[half, part],
+            self.mate_in.at[half, part],
+            self.sems[0].at[half, piece],
+            self.sems[1].at[half, piece],
+            {"tensor": self.corner.mate},
+        )
+
+    def far_copy(self, piece):
+        part = self.part(piece)
+        return remote(
+            self.far_out.at[part],
+            self.far_in.at[part],
+            self.sems[2].at[piece],
+            self.sems[3].at[piece],
+            {"tensor": self.corner.far},
+        )
+
+    def give(self, half, ref):
+        for piece in range(self.pieces):
+            part = self.part(piece)
+            self.mate_out[half, part] = ref[part].astype(LOW)
+            self.mate_copy(half, piece).start()
+
+    def cross(self, ref):
+        for piece in range(self.pieces):
+            part = self.part(piece)
+            self.mate_copy(0, piece).wait_recv()
+            self.far_out[part] = (ref[part] + self.mate_in[0, part].astype(WIDE)).astype(LOW)
+            self.far_copy(piece).start()
+
+    def step(self, step, ref):
+        @pl.when(step == 0)
+        def _():
+            self.give(0, ref)
+
+        @pl.when(step == 1)
+        def _():
+            self.cross(ref)
+
+        @pl.when(step == 2)
+        def _():
+            self.give(1, ref)
+
+    def land(self, piece, ref):
+        part = self.part(piece)
+        self.mate_copy(1, piece).wait_recv()
+        self.far_copy(piece).wait_recv()
+        return ref[part] + self.mate_in[1, part].astype(WIDE) + self.far_in[part].astype(WIDE)
+
+    def close(self):
+        for piece in range(self.pieces):
+            self.mate_copy(0, piece).wait_send()
+            self.mate_copy(1, piece).wait_send()
+            self.far_copy(piece).wait_send()
+
+
+def standard(values):
+    centre = values - jnp.mean(values, -1, keepdims=True)
     inverse = lax.rsqrt(jnp.mean(centre * centre, -1, keepdims=True) + norm_eps)
-    scaled = centre * inverse
-    return (scaled * gain_vec + bias_vec, scaled, inverse)
-
-
-def norm_back(grad_out, scaled, inverse, gain_vec):
-    grad_scaled = grad_out * gain_vec
+    return centre * inverse, inverse
+
+
+def norm_back(grad_out, scaled, inverse, gain):
+    grad_scaled = grad_out * gain
     return inverse * (
         grad_scaled
         - jnp.mean(grad_scaled, -1, keepdims=True)
@@ -58,181 +201,416 @@
     )
 
 
-def score_block(q_part, keyset, key_valid):
-    factor = q_part.shape[-1] ** (-0.5)
-    scores = jnp.einsum("qhd,khd->hqk", q_part, keyset, preferred_element_type=jnp.float32) * factor
-    return jnp.where(key_valid[None, None, :], scores, masked_score)
-
-
-def attend_forward(queries, keyset, values, key_valid, block_rows):
-    length = queries.shape[0]
-
-    def one_block(q_part):
-        scores = score_block(q_part, keyset, key_valid)
-        top_score = jnp.max(scores, -1, keepdims=True)
-        weights_exp = jnp.exp(scores - top_score)
-        row_total = jnp.sum(weights_exp, -1, keepdims=True)
-        weights_low = (weights_exp / row_total).astype(jnp.bfloat16)
-        results = jnp.einsum(
-            "hqk,khd->qhd", weights_low, values, preferred_element_type=jnp.float32
-        )
-        return (results, (top_score + jnp.log(row_total))[..., 0])
-
-    q_blocks = queries.reshape(length // block_rows, block_rows, queries.shape[1], queries.shape[2])
-    results, log_total = lax.map(one_block, q_blocks)
-    return (results.reshape(length, queries.shape[1] * queries.shape[2]), log_total)
-
-
-def attend_back(queries, keyset, values, key_valid, attended_grad, log_total, block_rows):
-    length = queries.shape[0]
-    factor = queries.shape[-1] ** (-0.5)
-
-    def one_block(carried, inputs):
-        grad_keys, grad_values = carried
-        q_part, g_part, l_part = inputs
-        scores = score_block(q_part, keyset, key_valid)
-        weights = jnp.exp(scores - l_part[..., None])
-        grad_weights = jnp.einsum(
-            "qhd,khd->hqk", g_part, values, preferred_element_type=jnp.float32
-        )
-        centre = jnp.sum(weights * grad_weights, -1, keepdims=True)
-        grad_scores = (weights * (grad_weights - centre)).astype(jnp.bfloat16)
-        grad_query = (
-            jnp.einsum("hqk,khd->qhd", grad_scores, keyset, preferred_element_type=jnp.float32)
-            * factor
-        )
-        grad_keys = (
-            grad_keys
-            + jnp.einsum("hqk,qhd->khd", grad_scores, q_part, preferred_element_type=jnp.float32)
-            * factor
-        )
-        grad_values = grad_values + jnp.einsum(
-            "hqk,qhd->khd", weights.astype(jnp.bfloat16), g_part, preferred_element_type=jnp.float32
-        )
-        return ((grad_keys, grad_values), grad_query)
-
-    block_shape = (length // block_rows, block_rows, queries.shape[1], queries.shape[2])
-    zeros_kv = jnp.zeros(keyset.shape, jnp.float32)
-    (grad_keys, grad_values), grad_query = lax.scan(
-        one_block,
-        (zeros_kv, zeros_kv),
-        (queries.reshape(block_shape), attended_grad.reshape(block_shape), log_total),
-    )
-    return (
-        grad_query.reshape(length, -1),
-        grad_keys.reshape(length, -1),
-        grad_values.reshape(length, -1),
-    )
-
-
-def layer_forward(embedded, weights, key_valid):
-    qkv_proj, out_proj, up_proj, down_proj, norm_params = weights
-    local_width = out_proj.shape[0]
-    heads_here = local_width // DH
-    normed1, scaled1, inverse1 = layer_norm(embedded, norm_params[0], norm_params[1])
-    normed1_all = lax.all_gather(normed1.astype(jnp.bfloat16), "tensor", axis=0, tiled=True)
-    length = normed1_all.shape[0]
-    block_rows = min(512, length)
-    qkv = jnp.dot(normed1_all, qkv_proj, preferred_element_type=jnp.float32).astype(jnp.bfloat16)
-    queries = qkv[:, :local_width].reshape(length, heads_here, DH)
-    keyset = qkv[:, local_width : 2 * local_width].reshape(length, heads_here, DH)
-    values = qkv[:, 2 * local_width :].reshape(length, heads_here, DH)
-    attended, log_total = attend_forward(queries, keyset, values, key_valid, block_rows)
-    attended = attended.astype(jnp.bfloat16)
-    resid1 = embedded + lax.psum_scatter(
-        jnp.dot(attended, out_proj, preferred_element_type=jnp.float32),
-        "tensor",
-        scatter_dimension=0,
-        tiled=True,
-    )
-    normed2, scaled2, inverse2 = layer_norm(resid1, norm_params[2], norm_params[3])
-    normed2_all = lax.all_gather(normed2.astype(jnp.bfloat16), "tensor", axis=0, tiled=True)
-    hidden_pre = jnp.dot(normed2_all, up_proj, preferred_element_type=jnp.float32)
-    active = jax.nn.gelu(hidden_pre, approximate=False).astype(jnp.bfloat16)
-    resid2 = resid1 + lax.psum_scatter(
-        jnp.dot(active, down_proj, preferred_element_type=jnp.float32).astype(jnp.bfloat16),
-        "tensor",
-        scatter_dimension=0,
-        tiled=True,
-    ).astype(jnp.float32)
-    saved_values = (
-        scaled1,
-        inverse1,
-        normed1_all,
-        queries,
-        keyset,
-        values,
-        log_total,
-        attended,
-        scaled2,
-        inverse2,
-        normed2_all,
-        hidden_pre,
-        active,
-    )
-    return (resid2, saved_values)
-
-
-def layer_backward(resid2_grad, weights, key_valid, saved_values):
-    qkv_proj, out_proj, up_proj, down_proj, norm_params = weights
-    (
-        scaled1,
-        inverse1,
-        normed1_all,
-        queries,
-        keyset,
-        values,
-        log_total,
-        attended,
-        scaled2,
-        inverse2,
-        normed2_all,
-        hidden_pre,
-        active,
-    ) = saved_values
-    length = normed1_all.shape[0]
-    block_rows = min(512, length)
-    down_in = lax.all_gather(resid2_grad.astype(jnp.bfloat16), "tensor", axis=0, tiled=True)
-    down_grad = contract_rows(active, down_in)
-    active_grad = contract_last(down_in, down_proj)
-    gelu_back = jax.vjp(partial(jax.nn.gelu, approximate=False), hidden_pre)[1]
-    hidden_grad = gelu_back(active_grad)[0].astype(jnp.bfloat16)
-    up_grad = contract_rows(normed2_all, hidden_grad)
-    normed2_grad = lax.psum_scatter(
-        contract_last(hidden_grad, up_proj).astype(jnp.bfloat16),
-        "tensor",
-        scatter_dimension=0,
-        tiled=True,
-    ).astype(jnp.float32)
-    resid1_grad = resid2_grad + norm_back(normed2_grad, scaled2, inverse2, norm_params[2])
-    branch_in = lax.all_gather(resid1_grad.astype(jnp.bfloat16), "tensor", axis=0, tiled=True)
-    out_grad = contract_rows(attended, branch_in)
-    attended_grad = contract_last(branch_in, out_proj).astype(jnp.bfloat16).reshape(queries.shape)
-    grad_query, grad_key, grad_value = attend_back(
-        queries, keyset, values, key_valid, attended_grad, log_total, block_rows
-    )
-    qkv_grad = jnp.concatenate([grad_query, grad_key, grad_value], 1).astype(jnp.bfloat16)
-    qkv_weight_grad = contract_rows(normed1_all, qkv_grad)
-    normed1_grad = lax.psum_scatter(
-        contract_last(qkv_grad, qkv_proj).astype(jnp.bfloat16),
-        "tensor",
-        scatter_dimension=0,
-        tiled=True,
-    ).astype(jnp.float32)
-    embed_grad = resid1_grad + norm_back(normed1_grad, scaled1, inverse1, norm_params[0])
-    gain_grad = jnp.stack(
-        [
-            jnp.sum(normed1_grad * scaled1, 0),
-            jnp.sum(normed1_grad, 0),
-            jnp.sum(normed2_grad * scaled2, 0),
-            jnp.sum(normed2_grad, 0),
+def qkv_places(parts, rows, columns):
+    share = rows // parts
+    wide = columns * 2 // 3
+    packed = share * columns // 1024
+    for at in range(parts):
+        for j in range(2):
+            half = share // 2
+            yield (at * packed, half, j * wide, wide, at * share + j * half, 0)
+        for j in range(4):
+            quarter = share // 4
+            yield (at * packed + share // 2, quarter, j * (columns - wide), columns - wide, at * share + j * quarter, wide)
+
+
+def unpack_into(full, packed, parts):
+    for row, rows, col, cols, to_row, to_col in qkv_places(parts, full.shape[0], full.shape[1]):
+        full[to_row : to_row + rows, to_col : to_col + cols] = packed[row : row + rows, col : col + cols]
+
+
+def pack_from(packed, full, parts, base=0):
+    for row, rows, col, cols, to_row, to_col in qkv_places(parts, full.shape[0], full.shape[1]):
+        packed[base + row : base + row + rows, col : col + cols] = full[to_row : to_row + rows, to_col : to_col + cols]
+
+
+def rows_of(block, size):
+    return pl.ds(pl.multiple_of(block * size, size), size)
+
+
+def column_loop(width, body):
+    @pl.loop(0, width // TILE)
+    def _(tile):
+        body(pl.ds(pl.multiple_of(tile * TILE, TILE), TILE))
+
+
+def attend_kernel(parts, q_rows, count_ref, patch_ref, proj_ref, norm_ref, packed_ref, out_ref,
+                  embed_ref, normed1_ref, qkv_ref, attended_ref, log_ref, resid_ref, normed2_ref,
+                  qkv_proj, term, *comm):
+    corner = Corner()
+    corner.greet()
+    scatter = Scatter(corner, PIECES, *comm[:8])
+    gather = Gather(corner, normed2_ref, PIECES, comm[8:])
+    size, width = embed_ref.shape
+    length = patch_ref.shape[0]
+    local = attended_ref.shape[1]
+    unpack_into(qkv_proj, packed_ref, parts)
+
+    @pl.loop(0, 4)
+    def _(block):
+        here = rows_of(block, size)
+        column_loop(width, lambda cols: term.__setitem__((slice(None), cols), dot(patch_ref[here], proj_ref[:, cols])))
+
+        @pl.when(block == corner.me)
+        def _():
+            embed_ref[...] = term[...]
+
+        scaled, inverse = standard(term[...])
+        normed1_ref[here] = (scaled * norm_ref[0:1] + norm_ref[1:2]).astype(LOW)
+
+        def columns(cols):
+            qkv_ref[here, cols] = dot(normed1_ref[here], qkv_proj[:, cols]).astype(LOW)
+
+        column_loop(3 * local, columns)
+
+    valid = lax.broadcasted_iota(jnp.int32, (1, length), 1) < count_ref[0] * VTOK
+    left = lax.broadcasted_iota(jnp.int32, (1, 2 * DH), 1) < DH
+    factor = jnp.array(DH ** (-0.5), LOW)
+
+    @pl.loop(0, length // q_rows)
+    def _(turn):
+        here = rows_of(turn, q_rows)
+        for pair in range(local // (2 * DH)):
+            lanes = slice(pair * 2 * DH, (pair + 1) * 2 * DH)
+            queries = qkv_ref[here, lanes] * factor
+            keyset = qkv_ref[:, local + pair * 2 * DH : local + (pair + 1) * 2 * DH]
+            values = qkv_ref[:, 2 * local + pair * 2 * DH : 2 * local + (pair + 1) * 2 * DH]
+            found = []
+            for side in range(2):
+                mine = left if side == 0 else ~left
+                scores = dot(jnp.where(mine, queries, jnp.zeros_like(queries)), keyset, NT)
+                scores = jnp.where(valid, scores, masked_score)
+                top = jnp.max(scores, -1, keepdims=True)
+                powers = jnp.exp(scores - top)
+                total = jnp.sum(powers, -1, keepdims=True)
+                log_ref[here, pair * 2 + side : pair * 2 + side + 1] = top + jnp.log(total)
+                found.append(dot((powers * (1.0 / total)).astype(LOW), values))
+            attended_ref[here, lanes] = jnp.where(left, found[0], found[1]).astype(LOW)
+
+    @pl.loop(0, 4)
+    def _(step):
+        here = rows_of(corner.block(step), size)
+        column_loop(width, lambda cols: term.__setitem__((slice(None), cols), dot(attended_ref[here], out_ref[:, cols])))
+        scatter.step(step, term)
+
+    for piece in range(PIECES):
+        part = scatter.part(piece)
+        resid = embed_ref[part] + scatter.land(piece, term)
+        resid_ref[part] = resid
+        scaled, inverse = standard(resid)
+        normed2_ref[gather.part(corner.me, piece)] = (scaled * norm_ref[2:3] + norm_ref[3:4]).astype(LOW)
+        gather.start(piece)
+    for piece in range(PIECES):
+        gather.relay(piece)
+    gather.finish()
+    scatter.close()
+
+
+def attend(count, patches, patch_proj, norm, packed, out_proj, parts, collective_id):
+    length, size = patches.shape[0], patches.shape[0] // 4
+    width, local = patch_proj.shape[1], out_proj.shape[0]
+    shape = jax.ShapeDtypeStruct
+    return pl.pallas_call(
+        partial(attend_kernel, parts, 256),
+        out_shape=(
+            shape((size, width), WIDE),
+            shape((length, width), LOW),
+            shape((length, 3 * local), LOW),
+            shape((length, local), LOW),
+            shape((length, local // DH), WIDE),
+            shape((size, width), WIDE),
+            shape((length, width), LOW),
+        ),
+        in_specs=[pl.BlockSpec(memory_space=pltpu.SMEM)] + [VMEM] * 5,
+        out_specs=(VMEM,) * 7,
+        scratch_shapes=[pltpu.VMEM((width, 3 * local), LOW), pltpu.VMEM((size, width), WIDE)]
+        + Scatter.scratch(size, width, PIECES)
+        + Gather.scratch(PIECES),
+        compiler_params=pltpu.CompilerParams(
+            collective_id=collective_id, has_side_effects=True, vmem_limit_bytes=62 * 2**20
+        ),
+    )(count, patches, patch_proj, norm, packed, out_proj)
+
+
+def mlp_kernel(normed2_ref, up_ref, down_ref, resid1_ref, cols_ref, hidden_ref, active_ref, low_ref, table_ref, term, *comm):
+    corner = Corner()
+    corner.greet()
+    scatter = Scatter(corner, PIECES, *comm[:8])
+    gather = Gather(corner, table_ref, PIECES, comm[8:])
+    size, width = resid1_ref.shape
+
+    @pl.loop(0, 4)
+    def _(step):
+        here = rows_of(corner.block(step), size)
+
+        def columns(cols):
+            hidden = dot(normed2_ref[here], up_ref[:, cols])
+            hidden_ref[here, cols] = hidden
+            active_ref[here, cols] = (0.5 * hidden * (1.0 + lax.erf(hidden * ROOT_HALF))).astype(LOW)
+
+        column_loop(up_ref.shape[1], columns)
+        column_loop(width, lambda cols: term.__setitem__((slice(None), cols), dot(active_ref[here], down_ref[:, cols])))
+        scatter.step(step, term)
+
+    for piece in range(PIECES):
+        part = scatter.part(piece)
+        low_ref[part] = (resid1_ref[part] + scatter.land(piece, term)).astype(LOW)
+        table_ref[gather.part(corner.me, piece)] = dot(low_ref[part], cols_ref[...]).astype(LOW)
+        gather.start(piece)
+    for piece in range(PIECES):
+        gather.relay(piece)
+    gather.finish()
+    scatter.close()
+
+
+def mlp(normed2, up_proj, down_proj, resid1, used_cols, collective_id):
+    length, size, width = normed2.shape[0], resid1.shape[0], resid1.shape[1]
+    hidden = up_proj.shape[1]
+    shape = jax.ShapeDtypeStruct
+    return pl.pallas_call(
+        mlp_kernel,
+        out_shape=(
+            shape((length, hidden), WIDE),
+            shape((length, hidden), LOW),
+            shape((size, width), LOW),
+            shape((length, used_cols.shape[1]), LOW),
+        ),
+        in_specs=[VMEM] * 5,
+        out_specs=(VMEM,) * 4,
+        scratch_shapes=[pltpu.VMEM((size, width), WIDE)]
+        + Scatter.scratch(size, width, PIECES)
+        + Gather.scratch(PIECES),
+        compiler_params=pltpu.CompilerParams(
+            collective_id=collective_id, has_side_effects=True, vmem_limit_bytes=62 * 2**20
+        ),
+    )(normed2, up_proj, down_proj, resid1, used_cols)
+
+
+def mlp_back_kernel(table_ref, cols_ref, low_ref, active_ref, hidden_ref, normed2_ref, up_ref, down_ref, resid1_ref, norm_ref,
+                    unpatch_ref, grad_ref, resid_grad_ref, branch_ref, gain_ref,
+                    gauss, down_in, hidden_grad, term, tail, *comm):
+    corner = Corner()
+    corner.greet()
+    small = Scatter(corner, 1, *comm[:8])
+    spread = Gather(corner, gauss, 1, comm[8:14])
+    scatter = Scatter(corner, PIECES, *comm[14:22])
+    gather = Gather(corner, branch_ref, PIECES, comm[22:])
+    size, width = resid1_ref.shape
+    ff = up_ref.shape[1]
+
+    def view(step):
+        return table_ref.at[rows_of(corner.block(step), size)]
+
+    tail[...] = view(0)[...].astype(WIDE)
+    small.give(0, tail)
+    tail[...] = view(1)[...].astype(WIDE)
+    small.cross(tail)
+    tail[...] = view(2)[...].astype(WIDE)
+    small.give(1, tail)
+    tail[...] = view(3)[...].astype(WIDE)
+    own_gauss = small.land(0, tail).astype(LOW)
+    gauss[spread.part(corner.me, 0)] = own_gauss
+    spread.start(0)
+    unpatch_ref[...] = dot(low_ref[...], own_gauss, TN)
+    spread.relay(0)
+    spread.finish()
+    small.close()
+
+    @pl.loop(0, 4)
+    def _(step):
+        here = rows_of(corner.block(step), size)
+        term[...] = dot(gauss[here], cols_ref[...], NT)
+        down_in[here] = term[...].astype(LOW)
+
+        @pl.when(step == 3)
+        def _():
+            resid_grad_ref[...] = term[...]
+
+        def columns(cols):
+            active_grad = dot(down_in[here], down_ref[cols, :], NT)
+            hidden = hidden_ref[here, cols]
+            slope = 0.5 * (1.0 + lax.erf(hidden * ROOT_HALF)) + hidden * (jnp.exp(-0.5 * hidden * hidden) * NORMAL_PEAK)
+            hidden_grad[here, cols] = (active_grad * slope).astype(LOW)
+
+        column_loop(ff, columns)
+
+        def back(cols):
+            term[:, cols] = dot(hidden_grad[here], up_ref[cols, :], NT)
+
+        column_loop(width, back)
+        scatter.step(step, term)
+
+    @pl.loop(0, width // TILE)
+    def _(tile):
+        cols = pl.ds(pl.multiple_of(tile * TILE, TILE), TILE)
+        grad_ref[cols, :] = dot(normed2_ref[:, cols], hidden_grad[...], TN)
+
+    @pl.loop(0, ff // TILE)
+    def _(tile):
+        cols = pl.ds(pl.multiple_of(tile * TILE, TILE), TILE)
+        grad_ref[pl.ds(pl.multiple_of(width + tile * TILE, TILE), TILE), :] = dot(active_ref[:, cols], down_in[...], TN)
+
+    gain_sum, bias_sum = jnp.zeros((1, width), WIDE), jnp.zeros((1, width), WIDE)
+    for piece in range(PIECES):
+        part = scatter.part(piece)
+        grad = scatter.land(piece, term)
+        scaled, inverse = standard(resid1_ref[part])
+        total = resid_grad_ref[part] + norm_back(grad, scaled, inverse, norm_ref[2:3])
+        resid_grad_ref[part] = total
+        branch_ref[gather.part(corner.me, piece)] = total.astype(LOW)
+        gather.start(piece)
+        gain_sum += jnp.sum(grad * scaled, 0, keepdims=True)
+        bias_sum += jnp.sum(grad, 0, keepdims=True)
+    gain_ref[0:1] = gain_sum
+    gain_ref[1:2] = bias_sum
+    for piece in range(PIECES):
+        gather.relay(piece)
+    gather.finish()
+    scatter.close()
+
+
+def mlp_back(table_grad, used_cols, low, active, hidden, normed2, up_proj, down_proj, resid1, norm, collective_id):
+    length, size, width = normed2.shape[0], resid1.shape[0], resid1.shape[1]
+    ff, used = up_proj.shape[1], used_cols.shape[1]
+    shape = jax.ShapeDtypeStruct
+    return pl.pallas_call(
+        mlp_back_kernel,
+        out_shape=(
+            shape((width, used), WIDE),
+            shape((width + ff, width), WIDE),
+            shape((size, width), WIDE),
+            shape((length, width), LOW),
+            shape((2, width), WIDE),
+        ),
+        in_specs=[VMEM] * 10,
+        out_specs=(VMEM,) * 5,
+        scratch_shapes=[
+            pltpu.VMEM((length, used), LOW),
+            pltpu.VMEM((length, width), LOW),
+            pltpu.VMEM((length, ff), LOW),
+            pltpu.VMEM((size, width), WIDE),
+            pltpu.VMEM((size, used), WIDE),
         ]
-    )
-    return (embed_grad, (qkv_weight_grad, out_grad, up_grad, down_grad), gain_grad)
-
-
-NT = (((1,), (1,)), ((), ()))
-NN = (((1,), (0,)), ((), ()))
+        + Scatter.scratch(size, used, 1)
+        + Gather.scratch(1)
+        + Scatter.scratch(size, width, PIECES)
+        + Gather.scratch(PIECES),
+        compiler_params=pltpu.CompilerParams(
+            collective_id=collective_id, has_side_effects=True, vmem_limit_bytes=63 * 2**20
+        ),
+    )(table_grad, used_cols, low, active, hidden, normed2, up_proj, down_proj, resid1, norm)
+
+
+def attend_back_kernel(parts, q_rows, count_ref, branch_ref, out_ref, qkv_ref, log_ref, packed_ref, attended_ref, normed1_ref, embed_ref,
+                       resid_grad_ref, norm_ref, patch_ref, grad_ref, patch_grad_ref, gain_ref,
+                       qkv_proj, attended_grad, qkv_grad, key_grad, value_grad, full_grad, term, embed_grad, *comm):
+    corner = Corner()
+    corner.greet()
+    scatter = Scatter(corner, PIECES, *comm)
+    size, width = embed_ref.shape
+    length, local = attended_ref.shape
+    unpack_into(qkv_proj, packed_ref, parts)
+
+    @pl.loop(0, 4)
+    def _(block):
+        here = rows_of(block, size)
+        attended_grad[here] = dot(branch_ref[here], out_ref[...], NT).astype(LOW)
+
+    key_grad[...] = jnp.zeros_like(key_grad)
+    value_grad[...] = jnp.zeros_like(value_grad)
+    valid = lax.broadcasted_iota(jnp.int32, (1, length), 1) < count_ref[0] * VTOK
+    left = lax.broadcasted_iota(jnp.int32, (1, 2 * DH), 1) < DH
+    factor = jnp.array(DH ** (-0.5), LOW)
+
+    @pl.loop(0, length // q_rows)
+    def _(turn):
+        here = rows_of(turn, q_rows)
+        for pair in range(local // (2 * DH)):
+            lanes = slice(pair * 2 * DH, (pair + 1) * 2 * DH)
+            queries = qkv_ref[here, lanes] * factor
+            grads = attended_grad[here, lanes]
+            keyset = qkv_ref[:, local + pair * 2 * DH : local + (pair + 1) * 2 * DH]
+            values = qkv_ref[:, 2 * local + pair * 2 * DH : 2 * local + (pair + 1) * 2 * DH]
+            found = []
+            for side in range(2):
+                mine = left if side == 0 else ~left
+                own_query = jnp.where(mine, queries, jnp.zeros_like(queries))
+                own_grad = jnp.where(mine, grads, jnp.zeros_like(grads))
+                scores = jnp.where(valid, dot(own_query, keyset, NT), masked_score)
+                probs = jnp.exp(scores - log_ref[here, pair * 2 + side : pair * 2 + side + 1])
+                prob_grad = dot(own_grad, values, NT)
+                value_grad[:, lanes] += dot(probs.astype(LOW), own_grad, TN)
+                centre = jnp.sum(probs * prob_grad, -1, keepdims=True)
+                score_grad = (probs * (prob_grad - centre)).astype(LOW)
+                found.append(dot(score_grad, keyset))
+                key_grad[:, lanes] += dot(score_grad, own_query, TN)
+            qkv_grad[here, lanes] = (jnp.where(left, found[0], found[1]) * (DH ** (-0.5))).astype(LOW)
+
+    qkv_grad[:, local : 2 * local] = key_grad[...].astype(LOW)
+    qkv_grad[:, 2 * local :] = value_grad[...].astype(LOW)
+
+    @pl.loop(0, 4)
+    def _(step):
+        here = rows_of(corner.block(step), size)
+
+        def columns(cols):
+            term[:, cols] = dot(qkv_grad[here], qkv_proj[cols, :], NT)
+
+        column_loop(width, columns)
+        scatter.step(step, term)
+
+    grad_ref[grad_ref.shape[0] - local :, :] = dot(attended_ref[...], branch_ref[...], TN)
+
+    @pl.loop(0, width // TILE)
+    def _(tile):
+        cols = pl.ds(pl.multiple_of(tile * TILE, TILE), TILE)
+        full_grad[cols, :] = dot(normed1_ref[:, cols], qkv_grad[...], TN)
+
+    pack_from(grad_ref, full_grad, parts)
+
+    gain_sum, bias_sum = jnp.zeros((1, width), WIDE), jnp.zeros((1, width), WIDE)
+    for piece in range(PIECES):
+        part = scatter.part(piece)
+        grad = scatter.land(piece, term)
+        scaled, inverse = standard(embed_ref[part])
+        embed_grad[part] = (resid_grad_ref[part] + norm_back(grad, scaled, inverse, norm_ref[0:1])).astype(LOW)
+        gain_sum += jnp.sum(grad * scaled, 0, keepdims=True)
+        bias_sum += jnp.sum(grad, 0, keepdims=True)
+    gain_ref[0:1] = gain_sum
+    gain_ref[1:2] = bias_sum
+    patch_grad_ref[...] = dot(patch_ref[...], embed_grad[...], TN)
+    scatter.close()
+
+
+def attend_back(count, branch, out_proj, qkv, log_total, packed, attended, normed1, embed, resid_grad, norm, patches, parts, collective_id):
+    length, local = attended.shape
+    size, width = embed.shape
+    shape = jax.ShapeDtypeStruct
+    return pl.pallas_call(
+        partial(attend_back_kernel, parts, 256),
+        out_shape=(
+            shape((4 * local, width), WIDE),
+            shape((patches.shape[1], width), WIDE),
+            shape((2, width), WIDE),
+        ),
+        in_specs=[pl.BlockSpec(memory_space=pltpu.SMEM)] + [VMEM] * 11,
+        out_specs=(VMEM,) * 3,
+        scratch_shapes=[
+            pltpu.VMEM((width, 3 * local), LOW),
+            pltpu.VMEM((length, local), LOW),
+            pltpu.VMEM((length, 3 * local), LOW),
+            pltpu.VMEM((length, local), WIDE),
+            pltpu.VMEM((length, local), WIDE),
+            pltpu.VMEM((width, 3 * local), WIDE),
+            pltpu.VMEM((size, width), WIDE),
+            pltpu.VMEM((size, width), LOW),
+        ]
+        + Scatter.scratch(size, width, PIECES),
+        compiler_params=pltpu.CompilerParams(
+            collective_id=collective_id, has_side_effects=True, vmem_limit_bytes=62 * 2**20
+        ),
+    )(count, branch, out_proj, qkv, log_total, packed, attended, normed1, embed, resid_grad, norm, patches)
+
 
 def render_kernel(area, wide, block, split, table_ref, splat_ref, dist_ref, label_ref, loss_ref, grad_ref, flip, picked, hot, spread_grad):
     tokens = table_ref.shape[0]
@@ -309,7 +687,7 @@
     vm = pl.BlockSpec(memory_space=pltpu.VMEM)
     groups = tokens // wide
     return pl.pallas_call(
-        functools.partial(render_kernel, area, wide, block, split),
+        partial(render_kernel, area, wide, block, split),
         out_shape=(jax.ShapeDtypeStruct((8, 128), jnp.float32), jax.ShapeDtypeStruct(table.shape, jnp.bfloat16)),
         in_specs=[vm] * 4, out_specs=(vm, vm),
         scratch_shapes=[pltpu.VMEM((groups * 2 * area, wide), jnp.bfloat16), pltpu.VMEM((groups * 2 * area, block), jnp.float32),
@@ -444,7 +822,7 @@
     half = (lines * chunk, width)
     vmem = pl.BlockSpec(memory_space=pltpu.VMEM)
     return pl.pallas_call(
-        functools.partial(owner_sum_kernel, lines, pieces),
+        partial(owner_sum_kernel, lines, pieces),
         out_shape=jax.ShapeDtypeStruct((chunk, width), jnp.float32),
         in_specs=[vmem],
         out_specs=vmem,
@@ -603,36 +981,28 @@
     up_end = out_end + local_hidden
     patch_rows = PIN * D // 128
     unpatch_rows = D * POUT // 128
-    weights = (
-        unpack_qkv(row_weights[:qkv_rows], qkv_parts),
-        row_weights[qkv_rows:out_end],
-        row_weights[out_end:up_end],
-        row_weights[up_end:],
-        shared_weights[patch_rows + unpatch_rows :].reshape(4, D).astype(jnp.float32),
-    )
+    packed_qkv = row_weights[:qkv_rows]
+    out_proj = row_weights[qkv_rows:out_end]
+    up_proj = row_weights[out_end:up_end]
+    down_proj = row_weights[up_end:]
+    norm = shared_weights[patch_rows + unpatch_rows :].reshape(4, D).astype(jnp.float32)
     patch_proj = shared_weights[:patch_rows].reshape(PIN, D)
     used_cols = shared_weights[patch_rows : patch_rows + unpatch_rows].reshape(D, POUT // 128, 128)[:, 0]
     own_patches = patches[0]
-    row_count = own_patches.shape[0]
-    key_valid = jnp.arange(row_count * groups) < view_counts[0] * VTOK
-    embedded = jnp.dot(own_patches, patch_proj, preferred_element_type=jnp.float32)
-    resid2, saved_values = layer_forward(embedded, weights, key_valid)
-    resid2_low = resid2.astype(jnp.bfloat16)
-    gauss_table = lax.all_gather(
-        jnp.dot(resid2_low, used_cols, preferred_element_type=jnp.float32).astype(jnp.bfloat16),
-        "tensor",
-        axis=0,
-        tiled=True,
-    )
+    all_patches = lax.all_gather(own_patches, "tensor", axis=0, tiled=True)
+    embed, normed1, qkv, attended, log_total, resid1, normed2 = attend(
+        view_counts, all_patches, patch_proj, norm, packed_qkv, out_proj, qkv_parts, 3
+    )
+    hidden, active, resid2_low, gauss_table = mlp(normed2, up_proj, down_proj, resid1, used_cols, 4)
     loss_tile, table_grad = render(gauss_table, splat_index[0], splat_dist[0], alpha_label, PATCH * PATCH)
     loss_part = loss_tile[0, 0]
-    gauss_grad = lax.psum_scatter(table_grad, "tensor", scatter_dimension=0, tiled=True)
-    unpatch_used = contract_rows(resid2_low, gauss_grad)
-    resid2_grad = contract_last(gauss_grad, used_cols)
-    embed_grad, weight_grad, gain_grad = layer_backward(
-        resid2_grad, weights, key_valid, saved_values
-    )
-    patch_grad = contract_rows(own_patches, embed_grad.astype(jnp.bfloat16))
+    unpatch_used, late_grad, resid_grad, branch, gain2_grad = mlp_back(
+        table_grad, used_cols, resid2_low, active, hidden, normed2, up_proj, down_proj, resid1, norm, 5
+    )
+    early_grad, patch_grad, gain1_grad = attend_back(
+        view_counts, branch, out_proj, qkv, log_total, packed_qkv, attended, normed1, embed, resid_grad, norm, own_patches, qkv_parts, 6
+    )
+    gain_grad = jnp.concatenate([gain1_grad, gain2_grad], 0)
     unpatch_grad = jnp.concatenate(
         [unpatch_used, jnp.zeros((D, POUT - unpatch_used.shape[1]), jnp.float32)], 1
     )
@@ -643,8 +1013,7 @@
     lead = split_grad.shape[2]
     shared_stack = pad_first(split_grad, 2, 16 * D // split_grad[0, 0, 0].size).swapaxes(0, 1)
     shared_sum = lax.psum_scatter(shared_stack, "tensor", scatter_dimension=0, tiled=True)
-    qkv_grad, out_grad, up_grad, down_grad = weight_grad
-    row_stack = jnp.concatenate([pack_qkv(qkv_grad, qkv_parts), out_grad, up_grad, down_grad], 0)
+    row_stack = jnp.concatenate([early_grad, late_grad], 0)
     stack = jnp.concatenate(
         [row_stack.reshape(count_dp, share_rows, D), shared_sum.reshape(count_dp, -1, D)], 1
     ).reshape(-1, D)

time: 1110 us -> 882 us (0.79)
  Pallas kernels: 198 us -> 450 us
  waiting for transfers between devices: 489 us -> 251 us
  matrix products: 152 us -> 0 us
  local copies, waits for them, and re-layouts: 113 us -> 67.9 us
  other arithmetic: 110 us -> 75.5 us
    pallas_call x2 -> x6, Pallas kernels: 188 us -> 440 us  [the longest x1 138 us: owner_sum(): pl.pallas_call(partial(owner_sum_kernel, lines, pieces), out_shape=jax.Sh...]
    dot_general x38 -> x0, matrix products: 152 us -> none  [the longest x5 28.7 us: contract_last(): lax.dot_general(left_op, right_op, (((1,), (1,)), ((), ())), preferred_el...]
    all_gather x4 -> x1, waiting for transfers between devices: 110 us -> 17.7 us  [per_device(): all_patches = lax.all_gather(own_patches, 'tensor', axis=0, tiled=True)]
    reduce_scatter x2 -> x0, waiting for transfers between devices: 79.5 us -> none  [the longest x1 58.3 us: layer_forward(): lax.psum_scatter(jnp.dot(attended, out_proj, preferred_element_type=jnp.f...]
    unnamed x16 -> x5, waiting for transfers between devices: 170 us -> 106 us
    convert_element_type x6 -> x0, other arithmetic: 16.1 us -> none  [the longest x3 11 us: one_block(): grad_scores = (weights * (grad_weights - centre)).astype(jnp.bfloat16)]
    reduce_sum x8 -> x0, other arithmetic: 15.6 us -> none  [the longest x3 7.8 us: one_block(): row_total = jnp.sum(weights_exp, -1, keepdims=True)]
    unnamed x151 -> x58, local copies, waits for them, and re-layouts: 29.7 us -> 17.4 us
  transfers between devices with their start and end apart: 12 -> 4, of which waited for: 12 -> 4; matrix products, arithmetic and copies ran while one was open for 9% -> 6% of each run, Pallas kernels for 0% -> 0%
where the time goes in v2:
time: 882 us; the launch traced here: 876 us
  Pallas kernels  450 us (51%)
  waiting for transfers between devices  251 us (28%)
  other arithmetic  75.5 us (9%)
  local copies, waits for them, and re-layouts  67.9 us (8%)
  between operations  22.7 us (3%)
    pallas_call x1, Pallas kernels, owner_sum(): pl.pallas_call(partial(owner_sum_kernel, lines, pieces), out_shape=jax.Sh...  138 us
    unnamed x5, waiting for transfers between devices  106 us
    all_gather x1, waiting for transfers between devices, per_device(): row_weights = lax.all_gather(own_tiles, 'dp', axis=0, tiled=True)  87.6 us
    pallas_call x1, Pallas kernels, attend(): pl.pallas_call(partial(attend_kernel, parts, 256), out_shape=(shape((size...  81.2 us
    pallas_call x1, Pallas kernels, mlp_back(): pl.pallas_call(mlp_back_kernel, out_shape=(shape((width, used), WIDE), sh...  67.6 us
    pallas_call x1, Pallas kernels, attend_back(): pl.pallas_call(partial(attend_back_kernel, parts, 256), out_shape=(shape(...  65.2 us
    pallas_call x1, Pallas kernels, render(): pl.pallas_call(partial(render_kernel, area, wide, block, split), out_shap...  49.4 us
    all_gather x1, waiting for transfers between devices, per_device(): lax.all_gather(own_shared, 'dp', axis=0, tiled=False)[:, :lead]  39.6 us
  transfers between devices with their start and end apart: 4, of which 4 were waited for; matrix products, arithmetic and copies ran while one was open for 6% of the time, Pallas kernels for 0%

profile of v2, /device:TPU:0, one launch (start us, length us, event | category | flops | bytes accessed | tf_op | source)
XLA Modules:
  0.0 876.1 jit_solution(3648620033679932029)
XLA Ops:
  9.3 16.3 %convert_reduce_fusion = bf16[393216]{0:T(1024)(128)(2,1)S(1)} fusion(f32[1,393216]{1,0:T(1,128)S(1)} %copy-done.8), kind=kLoop, calls=%fused_computation.13 | loop fusion | flops 393216 | bytes 2359296 | tf_op jit(solution)/shard_map/convert_element_type | solution.py:967
  30.3 39.6 %all-gather.12.cloned.1.call-done = bf16[10880,128]{1,0:T(8,128)(2,1)} async-done(((bf16[1360,128]{1,0:T(8,128)(2,1)}), bf16[10880,128]{1,0:T(8,128)(2,1)}) %all-gather.12.cloned.1.call-update) | async-done | bytes 2785296 | tf_op jit(solution)/shard_map/all_gather | solution.py:978
  82.7 87.6 %all-gather.8.cloned.1.call-done = bf16[3072,1024]{1,0:T(8,128)(2,1)} async-done(((bf16[384,1024]{1,0:T(8,128)(2,1)}), bf16[3072,1024]{1,0:T(8,128)(2,1)}) %all-gather.8.cloned.1.call-update) | async-done | bytes 6291472 | tf_op jit(solution)/shard_map/all_gather | solution.py:973
  174.9 17.7 %all-gather.10.cloned.1.call-done = bf16[1,1536,576]{2,1,0:T(8,128)(2,1)} async-done(((bf16[1,384,576]{2,1,0:T(8,128)(2,1)}), bf16[1,1536,576]{2,1,0:T(8,128)(2,1)}) %all-gather.10.cloned.1.call-update) | async-done | bytes 1769488 | tf_op jit(solution)/shard_map/all_gather | solution.py:992
  192.5 81.2 %shard_map.229 = (f32[384,1024]{1,0:T(8,128)}, bf16[1536,1024]{1,0:T(8,128)(2,1)}, bf16[1536,768]{1,0:T(8,128)(2,1)}, bf16[1536,256]{1,0:T(8,128)(2,1)}, f32[153...) custom-call(s32[1]{0:T(128)S(6)} %copy.58.count_ref, bf16[1536,576]{1,0:T(8,128)(2,1)} %bitcast.90, ...), custom_call_target="tpu_custom_call" | custom-call | tf_op jit(solution)/shard_map/pallas_call | solution.py:313
  273.7 4.6 fusion.10
  278.3 38.0 %shard_map.230 = (f32[1536,1024]{1,0:T(8,128)}, bf16[1536,1024]{1,0:T(8,128)(2,1)}, bf16[384,1024]{1,0:T(8,128)(2,1)}, bf16[1536,128]{1,0:T(8,128)(2,1)}) custom-call(bf16[1536,1024]{1,0:T(8,128)(2,1)} %get-tuple-element.33.normed2_ref, bf16[1024,1024]{1,0:T(8,128)(2,1)} %get-tuple-element.63.up_ref, bf16[1024,1024]{1,0:T(8,128)(2,1)} %get-tuple-element.62.down_ref, ...), custom_call_target="tpu_custom_call" | custom-call | tf_op jit(solution)/shard_map/pallas_call | solution.py:370
  317.4 49.4 %shard_map.231 = (f32[8,128]{1,0:T(8,128)S(1)}, bf16[1536,128]{1,0:T(8,128)(2,1)S(1)}) custom-call(bf16[1536,128]{1,0:T(8,128)(2,1)S(1)} %copy-done, s32[4,6144]{1,0:T(4,128)S(1)} %bitcast.72, s32[4,6144]{1,0:T(4,128)S(1)} %bitcast.73, s32[1,6144]{1,0:T(1,128)S(1)} %copy-done.2), custom_call_target="tpu_custom_call" | custom-call | tf_op jit(solution)/shard_map/pallas_call | solution.py:689
  367.6 67.6 %shard_map.232 = (f32[1024,128]{1,0:T(8,128)}, f32[2048,1024]{1,0:T(8,128)}, f32[384,1024]{1,0:T(8,128)}, bf16[1536,1024]{1,0:T(8,128)(2,1)}, f32[2,1024]{1,0:T(2,128)}) custom-call(bf16[1536,128]{1,0:T(8,128)(2,1)} %copy-done.1, bf16[1024,128]{1,0:T(8,128)(2,1)} %bitcast.84, bf16[384,1024]{1,0:T(8,128)(2,1)} %get-tuple-element.37.low_ref, ...), custom_call_target="tpu_custom_call" | custom-call | tf_op jit(solution)/shard_map/pallas_call | solution.py:476
  435.2 65.2 %shard_map.233 = (f32[1024,1024]{1,0:T(8,128)}, f32[576,1024]{1,0:T(8,128)}, f32[2,1024]{1,0:T(2,128)}) custom-call(s32[1]{0:T(128)S(6)} %copy.58.count_ref, bf16[1536,1024]{1,0:T(8,128)(2,1)} %get-tuple-element.40.branch_ref, bf16[256,1024]{1,0:T(8,128)(2,1)} %slice.86.out_ref, bf16[1536,768]{1,0:T(8,128)(2,1)} %get-tuple-element.41.qkv_ref, ...), custom_call_target="tpu_custom_call" | custom-call | tf_op jit(solution)/shard_map/pallas_call | solution.py:589
  503.1 4.5 reshape.182
  509.5 6.4 pad_maximum_fusion.2
  515.9 5.6 reshape.184
  521.5 6.0 pad_bitcast_fusion
  530.0 12.4 %pad_maximum_fusion.1 = f32[3072,1024]{1,0:T(8,128)} fusion(f32[2048,1024]{1,0:T(8,128)} %get-tuple-element.48, f32[1024,1024]{1,0:T(8,128)} %get-tuple-element.47), kind=kLoop, calls=%fused_computation.1 | loop fusion | flops 3145728 | bytes 25165824 | tf_op jit(solution)/shard_map/concatenate | solution.py:1016
  542.4 105.8 %all-reduce.7.cloned.1.call-done = f32[4,8,384,128]{3,2,0,1:T(8,128)} async-done(((f32[4,8,384,128]{3,2,0,1:T(8,128)}), f32[4,8,384,128]{3,2,0,1:T(8,128)}) %all-reduce.7.cloned.1.call-update) | async-done | bytes 6291472
  650.7 10.1 %pad_maximum_fusion = f32[8,432,1024]{2,1,0:T(8,128)} fusion(f32[8,48,1024]{2,1,0:T(8,128)S(1)} %reshape.185, f32[8,384,1024]{2,1,0:T(8,128)} %bitcast.75), kind=kLoop, calls=%fused_computation | loop fusion | flops 3538944 | bytes 28311552 | tf_op jit(solution)/shard_map/concatenate | solution.py:1017
  660.7 138.4 %shard_map.234 = f32[432,1024]{1,0:T(8,128)} custom-call(f32[3456,1024]{1,0:T(8,128)} %bitcast.74), custom_call_target="tpu_custom_call" | custom-call | tf_op jit(solution)/shard_map/pallas_call | solution.py:824
  814.7 10.4 %shard_map.235 = f32[8,128]{1,0:T(8,128)} custom-call(f32[8,128]{1,0:T(8,128)} %pad.18.mine_ref), custom_call_target="tpu_custom_call" | custom-call | tf_op jit(solution)/shard_map/pallas_call | solution.py:887
  829.8 4.2 copy.51
  834.0 2.8 copy.52
  836.7 8.3 all-gather.3
  847.9 12.9 %fusion.8 = (bf16[1,393216]{1,0:T(2,128)(2,1)}, f32[1,393216]{1,0:T(1,128)S(1)}, f32[1,393216]{1,0:T(1,128)}, f32[1,393216]{1,0:T(1,128)}) fusion(f32[1,393216]{1,0:T(1,128)S(1)} %copy-done.9, f32[]{:T(128)} %bitcast.36, f32[]{:T(128)} %bitcast.35, f32[]{:T(128)S(6)} %div.44, f32[1,393216]{1,0:T(1,128)S(1)} %bitcast.77, f32[1,393216]{1,0:T(1,128)} %bitcast.78, ...), kind=kLoop, calls=%fused_computation.39 | loop fusion | flops 7077888 | bytes 13369357 | tf_op jit(solution)/shard_map/convert_element_type | solution.py:1048
  860.9 3.5 multiply_add_fusion
  (113 shorter events, 54.8 us)
Async XLA Ops:
  7.2 2.1 copy-start.8
  7.2 62.7 %all-gather.12.cloned.1.call-start = ((), (), s32[]{:S(2)}) async-start(), calls=%async_computation.2 | async-start | bytes 3133440 | tf_op jit(solution)/shard_map/all_gather | solution.py:978
  9.3 161.1 %all-gather.8.cloned.1.call-start = ((), (), s32[]{:S(2)}) async-start(), calls=%async_computation | async-start | bytes 7077888 | tf_op jit(solution)/shard_map/all_gather | solution.py:973
  28.1 164.5 %all-gather.10.cloned.1.call-start = ((), (), s32[]{:S(2)}) async-start(), calls=%async_computation.1 | async-start | bytes 2457600 | tf_op jit(solution)/shard_map/all_gather | solution.py:992
  29.1 619.1 %all-reduce.7.cloned.1.call-start = ((), (), s32[]{:S(2)}) async-start(), calls=%async_computation.3 | async-start | bytes 12582912
  75.5 2.7 slice-start.2
  278.3 38.0 %copy-start.2 = (s32[1,6144]{1,0:T(1,128)S(1)}, s32[1,6144]{1,0:T(1,128)}, u32[]{:S(2)}) copy-start(s32[1,6144]{1,0:T(1,128)} %label_ref.1) | copy-start | bytes 73732
  278.3 38.0 %copy-start.3 = (s32[1,4,6144]{2,1,0:T(4,128)S(1)}, s32[1,4,6144]{2,1,0:T(4,128)}, u32[]{:S(2)}) copy-start(s32[1,4,6144]{2,1,0:T(4,128)} %param.16) | copy-start | bytes 294916
  278.3 38.0 %copy-start.4 = (s32[1,4,6144]{2,1,0:T(4,128)S(1)}, s32[1,4,6144]{2,1,0:T(4,128)}, u32[]{:S(2)}) copy-start(s32[1,4,6144]{2,1,0:T(4,128)} %param.17) | copy-start | bytes 294916
  435.2 65.2 %copy-start.23 = (f32[2,1024]{1,0:T(2,128)S(1)}, f32[2,1024]{1,0:T(2,128)}, u32[]{:S(2)}) copy-start(f32[2,1024]{1,0:T(2,128)} %get-tuple-element.52) | copy-start | bytes 24580
  435.2 66.0 %copy-start.21 = (f32[1024,128]{1,0:T(8,128)S(1)}, f32[1024,128]{1,0:T(8,128)}, u32[]{:S(2)}) copy-start(f32[1024,128]{1,0:T(8,128)} %get-tuple-element.50) | copy-start | bytes 1572868
  503.1 4.5 copy-start.15
  507.6 1.9 copy-start.6
  806.3 1.8 copy-start.5
  808.2 2.5 slice-start
  836.7 11.2 %copy-start.10 = (f32[1,1,512,768]{3,1,2,0:T(1,128)S(1)}, f32[1,1,512,768]{3,1,2,0:T(1,128)}, u32[]{:S(2)}) copy-start(f32[1,1,512,768]{3,1,2,0:T(1,128)} %copy.51) | copy-start | bytes 4718596
  845.0 2.9 copy-start.9
  847.9 12.9 %copy-start.17 = (f32[1,393216]{1,0:T(1,128)S(1)}, f32[1,393216]{1,0:T(1,128)}, u32[]{:S(2)}) copy-start(f32[1,393216]{1,0:T(1,128)} %param.23) | copy-start | bytes 4718596
  860.9 3.6 copy-start.11
  860.9 3.6 copy-start.12
  860.9 3.6 copy-start.14
  860.9 3.6 copy-start.19
  860.9 3.6 copy-start.20
  864.5 1.6 copy-start.18
  (9 other events, 9.5 us)
Sparse Core Ops, SparseCore 0:
  10.8 59.1 all-gather.11
  72.7 97.6 all-gather.7
  172.5 20.0 all-gather.9
  527.6 120.6 all-reduce.6

commit v3 on v2

--- a/solution.py
+++ b/solution.py
@@ -234,17 +234,21 @@
         body(pl.ds(pl.multiple_of(tile * TILE, TILE), TILE))
 
 
-def attend_kernel(parts, q_rows, count_ref, patch_ref, proj_ref, norm_ref, packed_ref, out_ref,
-                  embed_ref, normed1_ref, qkv_ref, attended_ref, log_ref, resid_ref, normed2_ref,
-                  qkv_proj, term, *comm):
+def attend_kernel(parts, q_rows, count_ref, patch_ref, proj_ref, norm_ref, packed_ref, out_ref, *rest):
     corner = Corner()
     corner.greet()
+    attend_body(parts, q_rows, corner, None, count_ref, patch_ref, proj_ref, norm_ref, packed_ref, out_ref, *rest)
+
+
+def attend_body(parts, q_rows, corner, progress, count_ref, patch_ref, proj_ref, norm_ref, packed_ref, out_ref,
+                embed_ref, normed1_ref, qkv_ref, attended_ref, log_ref, resid_ref, normed2_ref,
+                qkv_proj, term, *comm):
+    progress = progress or (lambda *_: None)
     scatter = Scatter(corner, PIECES, *comm[:8])
     gather = Gather(corner, normed2_ref, PIECES, comm[8:])
     size, width = embed_ref.shape
     length = patch_ref.shape[0]
     local = attended_ref.shape[1]
-    unpack_into(qkv_proj, packed_ref, parts)
 
     @pl.loop(0, 4)
     def _(block):
@@ -257,6 +261,13 @@
 
         scaled, inverse = standard(term[...])
         normed1_ref[here] = (scaled * norm_ref[0:1] + norm_ref[1:2]).astype(LOW)
+
+    progress("weights")
+    unpack_into(qkv_proj, packed_ref, parts)
+
+    @pl.loop(0, 4)
+    def _(block):
+        here = rows_of(block, size)
 
         def columns(cols):
             qkv_ref[here, cols] = dot(normed1_ref[here], qkv_proj[:, cols]).astype(LOW)
@@ -286,6 +297,9 @@
                 log_ref[here, pair * 2 + side : pair * 2 + side + 1] = top + jnp.log(total)
                 found.append(dot((powers * (1.0 / total)).astype(LOW), values))
             attended_ref[here, lanes] = jnp.where(left, found[0], found[1]).astype(LOW)
+        progress("turn", turn)
+
+    progress("out")
 
     @pl.loop(0, 4)
     def _(step):
@@ -300,6 +314,7 @@
         scaled, inverse = standard(resid)
         normed2_ref[gather.part(corner.me, piece)] = (scaled * norm_ref[2:3] + norm_ref[3:4]).astype(LOW)
         gather.start(piece)
+        progress("land", piece)
     for piece in range(PIECES):
         gather.relay(piece)
     gather.finish()
@@ -330,6 +345,334 @@
             collective_id=collective_id, has_side_effects=True, vmem_limit_bytes=62 * 2**20
         ),
     )(count, patches, patch_proj, norm, packed, out_proj)
+
+
+class Lines:
+    def __init__(self, lines):
+        self.lines = lines
+        self.me = lax.axis_index("dp")
+        self.line, self.side = self.me // 2, lax.rem(self.me, 2)
+        self.pair = {"dp": self.line * 2 + 1 - self.side}
+        self.above = {"dp": lax.rem(self.line + 1, lines) * 2 + self.side}
+        self.below = {"dp": lax.rem(self.line + lines - 1, lines) * 2 + self.side}
+        self.has_below, self.has_above = self.line > 0, self.line < lines - 1
+
+    def signal(self, barrier):
+        pl.semaphore_signal(barrier, inc=1, device_id=self.pair, device_id_type=MESH)
+
+        @pl.when(self.has_below)
+        def _():
+            pl.semaphore_signal(barrier, inc=1, device_id=self.below, device_id_type=MESH)
+
+        @pl.when(self.has_above)
+        def _():
+            pl.semaphore_signal(barrier, inc=1, device_id=self.above, device_id_type=MESH)
+
+        return 1 + jnp.minimum(self.line, 1) + jnp.minimum(self.lines - 1 - self.line, 1)
+
+
+class LineGather:
+    def __init__(self, spot, ref, base, chunk, pieces, late_own, sems):
+        self.spot, self.ref, self.base, self.chunk, self.pieces, self.late_own = spot, ref, base, chunk, pieces, late_own
+        self.sems = sems
+        self.rows = chunk // pieces
+        self.steps = (spot.lines - 1) * pieces
+
+    @staticmethod
+    def scratch(lines, pieces):
+        return [pltpu.SemaphoreType.DMA((lines * pieces,))] * 6
+
+    def copy(self, kind, line, side, piece, to):
+        start = self.base + (line * 2 + side) * self.chunk + piece * self.rows
+        here = self.ref.at[pl.ds(pl.multiple_of(start, 16), self.rows)]
+        at = line * self.pieces + piece
+        return remote(here, here, self.sems[2 * kind].at[at], self.sems[2 * kind + 1].at[at], to)
+
+    def up(self, line, piece):
+        return self.copy(0, line, self.spot.side, piece, self.spot.above)
+
+    def down(self, line, piece):
+        return self.copy(1, line, self.spot.side, piece, self.spot.below)
+
+    def across(self, line, piece):
+        return self.copy(2, line, self.spot.side, piece, self.spot.pair)
+
+    def crossed(self, line, piece):
+        return self.copy(2, line, 1 - self.spot.side, piece, self.spot.pair)
+
+    def own(self, copy):
+        @pl.loop(0, self.pieces)
+        def _(piece):
+            copy(self.spot.line, piece).start()
+
+    def begin(self):
+        spot = self.spot
+        first = spot.line == 0 if self.late_own else spot.line >= 0
+
+        @pl.when(first & spot.has_above)
+        def _():
+            self.own(self.up)
+
+        @pl.when(spot.has_below)
+        def _():
+            self.own(self.down)
+
+        @pl.when(first)
+        def _():
+            self.own(self.across)
+
+    def step(self, at):
+        spot = self.spot
+        piece = lax.rem(at, self.pieces)
+
+        @pl.when(at < spot.line * self.pieces)
+        def _():
+            line = at // self.pieces
+            self.up(line, piece).wait_recv()
+
+            @pl.when(spot.has_above)
+            def _():
+                self.up(line, piece).start()
+
+            self.across(line, piece).start()
+
+        if self.late_own:
+
+            @pl.when((at == spot.line * self.pieces - 1) & spot.has_above)
+            def _():
+                self.own(self.up)
+
+            @pl.when((at == self.pieces - 1) & spot.has_below)
+            def _():
+                self.own(self.across)
+
+        @pl.when(at < (spot.lines - 1 - spot.line) * self.pieces)
+        def _():
+            line = spot.line + 1 + at // self.pieces
+            self.down(line, piece).wait_recv()
+
+            @pl.when(spot.has_below)
+            def _():
+                self.down(line, piece).start()
+
+            self.across(line, piece).start()
+
+    def wait_crossed(self, line, pieces=None):
+        @pl.loop(0, pieces or self.pieces)
+        def _(piece):
+            self.crossed(line, piece).wait_recv()
+
+    def close(self):
+        spot = self.spot
+
+        @pl.loop(0, spot.lines * self.pieces)
+        def _(at):
+            line, piece = at // self.pieces, lax.rem(at, self.pieces)
+            self.across(line, piece).wait_send()
+
+            @pl.when((line <= spot.line) & spot.has_above)
+            def _():
+                self.up(line, piece).wait_send()
+
+            @pl.when((line >= spot.line) & spot.has_below)
+            def _():
+                self.down(line, piece).wait_send()
+
+
+WINDOW = 48
+FRONT = 80
+PADDED = 1616
+ROW_START = (0, 160, 336, 496)
+USED_START = (None, None, None, 0, 128, 352, 576, 800)
+
+
+def shared_offsets(me, quarter):
+    chunk = SHARED_LANES
+    rows = jnp.where(me == 0, 0, jnp.where(me == 1, 160, jnp.where(me == 2, 336, 496)))
+    used = (me - 4) * 224 + 128
+    return (
+        FRONT + 8 * rows - me * chunk + 8 * WINDOW * quarter,
+        FRONT + 8 * rows - me * chunk + 8 * 32 * quarter,
+        FRONT + PATCH_LANES - me * chunk + 6 * 48 * quarter,
+        FRONT + PATCH_LANES + 6 * used - me * chunk + 6 * 64 * quarter,
+        FRONT + PATCH_LANES + 6 * D - me * chunk,
+    )
+
+
+def shared_walk(me, quarter, take, phases=range(5)):
+    rows, last_rows, first_used, used, norm = shared_offsets(me, quarter)
+    for j in range(8):
+        if 0 in phases:
+            take(me < 3, 0, WINDOW, j, rows + j, 8)
+        if 1 in phases:
+            take((me == 3) & (quarter < 3), 0, 32, j, last_rows + j, 8)
+    if 2 in phases:
+        for j in range(3):
+            take((me == 3) & (quarter < 3), 32, 16, j, first_used + 6 * 16 * j, 6)
+    if 3 in phases:
+        for j in range(2):
+            take(me > 3, 0, 32, j, used + 6 * 32 * j, 6)
+    if 4 in phases:
+        for j in range(8):
+            take((me == 7) & (quarter == 0), 32, 8, j, norm + j, 8)
+
+
+def window_pieces(kind, row):
+    found = []
+    if kind == 0:
+        for me in range(3):
+            at = row - ROW_START[me]
+            if 0 <= at < 4 * WINDOW:
+                found.append((me, at // WINDOW, at % WINDOW, None))
+        at = row - ROW_START[3]
+        if 0 <= at < 96:
+            found.append((3, at // 32, at % 32, None))
+    else:
+        if row < 144:
+            found.append((3, row // 48, 32, row % 48 // 16))
+        for me in range(4, 8):
+            at = row - USED_START[me]
+            if 0 <= at < 256:
+                found.append((me, at // 64, at % 32, at % 64 // 32))
+    return found
+
+SHARED_LANES = 1348
+PATCH_LANES = PIN * D // 128
+CHUNK_PIECES = 4
+
+
+def forward_kernel(lines, q_rows, count_ref, row_ref, shared_ref, own_patch_ref,
+                   weight_ref, used_ref, norm_ref,
+                   embed_ref, normed1_ref, qkv_ref, attended_ref, log_ref, resid_ref, normed2_ref,
+                   patches, proj, windows, *rest):
+    body, extra = rest[:2 + 14], rest[2 + 14:]
+    corner, spot = Corner(), Lines(lines)
+    barrier = pltpu.get_barrier_semaphore()
+    for other in (corner.mate, corner.far):
+        pl.semaphore_signal(barrier, inc=1, device_id={"tensor": other}, device_id_type=MESH)
+    pl.semaphore_wait(barrier, 2 + spot.signal(barrier))
+    parts = lines // 2
+    chunk = weight_ref.shape[0] // (2 * lines)
+    size, inputs = own_patch_ref.shape
+    window = LineGather(spot, windows, corner.me * (2 * lines * WINDOW), WINDOW, 1, False, extra[0:6])
+    weights = LineGather(spot, weight_ref, 0, chunk, CHUNK_PIECES, True, extra[6:12])
+    spread = Gather(corner, windows, 2, extra[12:18])
+    given = Gather(corner, patches, 1, extra[18:24])
+
+    patches[given.part(corner.me, 0)] = own_patch_ref[...]
+    given.start(0)
+    base = pl.multiple_of((corner.me * 2 * lines + spot.me) * WINDOW, 16)
+    windows[pl.ds(base, WINDOW)] = jnp.zeros((WINDOW, windows.shape[1]), LOW)
+
+    def take(condition, row, rows, j, start, stride):
+        @pl.when(condition)
+        def _():
+            windows[pl.ds(pl.multiple_of(base + row, 16), rows), j * 128 : (j + 1) * 128] = shared_ref[
+                pl.ds(start, rows, stride)
+            ].astype(LOW)
+
+    shared_walk(spot.me, corner.me, take)
+    window.begin()
+    own = pl.multiple_of(spot.me * chunk, 16)
+
+    @pl.when(spot.me < parts)
+    def _():
+        for row, rows, col, cols, at, at_col in qkv_places(1, chunk * 4 // 3, D * 3 // 4):
+            for j in range(cols // 128):
+                weight_ref[pl.ds(pl.multiple_of(own + row, 16), rows), col + j * 128 : col + (j + 1) * 128] = row_ref[
+                    pl.ds(6 * at + at_col // 128 + j, rows, 6)
+                ].astype(LOW)
+
+    @pl.when(spot.me >= parts)
+    def _():
+        for j in range(8):
+            weight_ref[pl.ds(own, chunk), j * 128 : (j + 1) * 128] = row_ref[pl.ds(j, chunk, 8)].astype(LOW)
+
+    weights.begin()
+    for at in range(window.steps):
+        window.step(at)
+    for line in range(lines):
+        window.wait_crossed(line)
+    for piece in range(2):
+        spread.start(piece)
+    given.relay(0)
+    for at in range(2):
+        weights.step(at)
+    spread.relay(0)
+    weights.step(2)
+    spread.relay(1)
+    weights.step(3)
+    given.finish()
+    spread.finish()
+
+    def source(me, quarter, row, rows, j):
+        start = (quarter * 2 * lines + me) * WINDOW + row
+        return windows[start : start + rows] if j is None else windows[start : start + rows, j * 128 : (j + 1) * 128]
+
+    for row in range(0, proj.shape[0], 16):
+        proj[row : row + 16] = sum(source(me, t, at, 16, j) for me, t, at, j in window_pieces(0, row))
+    for row in range(0, used_ref.shape[0], 16):
+        used_ref[row : row + 16] = sum(source(me, t, at, 16, j) for me, t, at, j in window_pieces(1, row))
+    norm_ref[...] = source(2 * lines - 1, 0, 32, 8, None).astype(WIDE)
+
+    def progress(place, at=None):
+        if place == "weights":
+            weights.wait_crossed(0)
+        if place == "turn":
+            @pl.when(at >= 2)
+            def _():
+                weights.step(at + 2)
+        if place == "out":
+            weights.wait_crossed(1)
+        if place == "land":
+            weights.step(8 + at)
+
+    attend_body(parts, q_rows, corner, progress, count_ref, patches, proj, norm_ref,
+                weight_ref.at[pl.ds(0, D * 3 // 4)], weight_ref.at[pl.ds(D * 3 // 4, D // 4)],
+                embed_ref, normed1_ref, qkv_ref, attended_ref, log_ref, resid_ref, normed2_ref, *body)
+    for line in range(2, lines):
+        weights.wait_crossed(line)
+    weights.close()
+    window.close()
+
+
+def forward(count, row_lanes, shared_lanes, own_patches, lines, collective_id):
+    size, inputs = own_patches.shape
+    length, width, local = 4 * size, D, D // 4
+    shape = jax.ShapeDtypeStruct
+    return pl.pallas_call(
+        partial(forward_kernel, lines, 256),
+        out_shape=(
+            shape((3 * D, D), LOW),
+            shape((D, 128), LOW),
+            shape((8, D), WIDE),
+            shape((size, width), WIDE),
+            shape((length, width), LOW),
+            shape((length, 3 * local), LOW),
+            shape((length, local), LOW),
+            shape((length, local // DH), WIDE),
+            shape((size, width), WIDE),
+            shape((length, width), LOW),
+        ),
+        in_specs=[pl.BlockSpec(memory_space=pltpu.SMEM)] + [VMEM] * 3,
+        out_specs=(VMEM,) * 10,
+        scratch_shapes=[
+            pltpu.VMEM((length, inputs), LOW),
+            pltpu.VMEM((inputs, width), LOW),
+            pltpu.VMEM((8 * lines * WINDOW, width), LOW),
+            pltpu.VMEM((width, 3 * local), LOW),
+            pltpu.VMEM((size, width), WIDE),
+        ]
+        + Scatter.scratch(size, width, PIECES)
+        + Gather.scratch(PIECES)
+        + LineGather.scratch(lines, 1)
+        + LineGather.scratch(lines, CHUNK_PIECES)
+        + Gather.scratch(2)
+        + Gather.scratch(1),
+        compiler_params=pltpu.CompilerParams(
+            collective_id=collective_id, has_side_effects=True, vmem_limit_bytes=63 * 2**20
+        ),
+    )(count, row_lanes, shared_lanes, own_patches)
 
 
 def mlp_kernel(normed2_ref, up_ref, down_ref, resid1_ref, cols_ref, hidden_ref, active_ref, low_ref, table_ref, term, *comm):
@@ -964,35 +1307,44 @@
     local_hidden = FF // groups
     qkv_parts = count_dp // 4
     share_rows = row_master.shape[1] // D
-    own_row = row_master[0].astype(jnp.bfloat16)
-    own_tiles = jnp.where(
-        my_dp < qkv_parts,
-        pack_qkv(own_row.reshape(-1, 3 * local_width), 1),
-        own_row.reshape(share_rows, D),
-    )
-    row_weights = lax.all_gather(own_tiles, "dp", axis=0, tiled=True)
-    own_flat = shared_master.astype(jnp.bfloat16)
-    own_shared = by_lanes(own_flat, ())
-    lead = own_shared.shape[0]
-    own_shared = pad_first(own_shared, 0, 2048 // own_shared[0].size)
-    shared_weights = lax.all_gather(own_shared, "dp", axis=0, tiled=False)[:, :lead].reshape(-1, 128)
-    qkv_rows = 3 * local_width
-    out_end = qkv_rows + local_width
-    up_end = out_end + local_hidden
-    patch_rows = PIN * D // 128
-    unpatch_rows = D * POUT // 128
-    packed_qkv = row_weights[:qkv_rows]
-    out_proj = row_weights[qkv_rows:out_end]
-    up_proj = row_weights[out_end:up_end]
-    down_proj = row_weights[up_end:]
-    norm = shared_weights[patch_rows + unpatch_rows :].reshape(4, D).astype(jnp.float32)
-    patch_proj = shared_weights[:patch_rows].reshape(PIN, D)
-    used_cols = shared_weights[patch_rows : patch_rows + unpatch_rows].reshape(D, POUT // 128, 128)[:, 0]
     own_patches = patches[0]
-    all_patches = lax.all_gather(own_patches, "tensor", axis=0, tiled=True)
-    embed, normed1, qkv, attended, log_total, resid1, normed2 = attend(
-        view_counts, all_patches, patch_proj, norm, packed_qkv, out_proj, qkv_parts, 3
-    )
+    if count_dp == 8:
+        shared_lanes = jnp.pad(
+            shared_master.reshape(SHARED_LANES, 128), ((FRONT, PADDED - FRONT - SHARED_LANES), (0, 0))
+        )
+        weights, used_cols, norm, embed, normed1, qkv, attended, log_total, resid1, normed2 = forward(
+            view_counts, row_master.reshape(-1, 128), shared_lanes, own_patches, count_dp // 2, 7
+        )
+        packed_qkv, out_proj, up_proj, down_proj = jnp.split(weights, (3 * local_width, D, D + local_hidden))
+    else:
+        own_row = row_master[0].astype(jnp.bfloat16)
+        own_tiles = jnp.where(
+            my_dp < qkv_parts,
+            pack_qkv(own_row.reshape(-1, 3 * local_width), 1),
+            own_row.reshape(share_rows, D),
+        )
+        weights = lax.all_gather(own_tiles, "dp", axis=0, tiled=True)
+        own_flat = shared_master.astype(jnp.bfloat16)
+        own_shared = by_lanes(own_flat, ())
+        lead = own_shared.shape[0]
+        own_shared = pad_first(own_shared, 0, 2048 // own_shared[0].size)
+        shared_weights = lax.all_gather(own_shared, "dp", axis=0, tiled=False)[:, :lead].reshape(-1, 128)
+        qkv_rows = 3 * local_width
+        out_end = qkv_rows + local_width
+        up_end = out_end + local_hidden
+        patch_rows = PIN * D // 128
+        unpatch_rows = D * POUT // 128
+        packed_qkv = weights[:qkv_rows]
+        out_proj = weights[qkv_rows:out_end]
+        up_proj = weights[out_end:up_end]
+        down_proj = weights[up_end:]
+        norm = shared_weights[patch_rows + unpatch_rows :].reshape(4, D).astype(jnp.float32)
+        patch_proj = shared_weights[:patch_rows].reshape(PIN, D)
+        used_cols = shared_weights[patch_rows : patch_rows + unpatch_rows].reshape(D, POUT // 128, 128)[:, 0]
+        all_patches = lax.all_gather(own_patches, "tensor", axis=0, tiled=True)
+        embed, normed1, qkv, attended, log_total, resid1, normed2 = attend(
+            view_counts, all_patches, patch_proj, norm, packed_qkv, out_proj, qkv_parts, 3
+        )
     hidden, active, resid2_low, gauss_table = mlp(normed2, up_proj, down_proj, resid1, used_cols, 4)
     loss_tile, table_grad = render(gauss_table, splat_index[0], splat_dist[0], alpha_label, PATCH * PATCH)
     loss_part = loss_tile[0, 0]

time: 882 us -> 779 us (0.88)
  waiting for transfers between devices: 251 us -> 126 us
  Pallas kernels: 450 us -> 505 us
  other arithmetic: 75.5 us -> 56.2 us
  local copies, waits for them, and re-layouts: 67.9 us -> 52.1 us
    all_gather x3 -> x0, waiting for transfers between devices: 145 us -> none  [the longest x1 87.6 us: per_device(): row_weights = lax.all_gather(own_tiles, 'dp', axis=0, tiled=True)]
    pallas_call x1, Pallas kernels: 81.2 us -> 136 us  [forward(): pl.pallas_call(partial(forward_kernel, lines, 256), out_shape=(shape((3 *...]
    unnamed x5 -> x2, waiting for transfers between devices: 106 us -> 126 us
    convert_element_type x2 -> x0, other arithmetic: 17 us -> none  [the longest x1 16.3 us: per_device(): own_row = row_master[0].astype(jnp.bfloat16)]
    slice x11 -> x0, local copies, waits for them, and re-layouts: 14.6 us -> none  [the longest x1 4.6 us: per_device(): down_proj = row_weights[up_end:]]
    split x0 -> x3, local copies, waits for them, and re-layouts: none -> 9.24 us  [per_device(): jnp.split(weights, (3 * local_width, D, D + local_hidden))]
  transfers between devices with their start and end apart: 4 -> 1, of which waited for: 4 -> 1; matrix products, arithmetic and copies ran while one was open for 6% -> 2% of each run, Pallas kernels for 0% -> 0%
where the time goes in v3:
time: 779 us; the launch traced here: 772 us
  Pallas kernels  505 us (65%)
  waiting for transfers between devices  126 us (16%)
  other arithmetic  56.2 us (7%)
  local copies, waits for them, and re-layouts  52.1 us (7%)
  between operations  23 us (3%)
  blocking collectives  9.31 us (1%)
    pallas_call x1, Pallas kernels, owner_sum(): pl.pallas_call(partial(owner_sum_kernel, lines, pieces), out_shape=jax.Sh...  138 us
    pallas_call x1, Pallas kernels, forward(): pl.pallas_call(partial(forward_kernel, lines, 256), out_shape=(shape((3 *...  136 us
    unnamed x2, waiting for transfers between devices  126 us
    pallas_call x1, Pallas kernels, mlp_back(): pl.pallas_call(mlp_back_kernel, out_shape=(shape((width, used), WIDE), sh...  67.8 us
    pallas_call x1, Pallas kernels, attend_back(): pl.pallas_call(partial(attend_back_kernel, parts, 256), out_shape=(shape(...  64.9 us
    pallas_call x1, Pallas kernels, render(): pl.pallas_call(partial(render_kernel, area, wide, block, split), out_shap...  49.3 us
    pallas_call x1, Pallas kernels, mlp(): pl.pallas_call(mlp_kernel, out_shape=(shape((length, hidden), WIDE), shap...  39.2 us
  transfers between devices with their start and end apart: 1, of which 1 were waited for; matrix products, arithmetic and copies ran while one was open for 2% of the time, Pallas kernels for 0%

profile of v3, /device:TPU:0, one launch (start us, length us, event | category | flops | bytes accessed | tf_op | source)
XLA Modules:
  0.0 771.6 jit_solution(13579526345002800722)
XLA Ops:
  11.9 135.8 %shard_map.229 = (bf16[3072,1024]{1,0:T(8,128)(2,1)}, bf16[1024,128]{1,0:T(8,128)(2,1)}, f32[8,1024]{1,0:T(8,128)}, f32[384,1024]{1,0:T(8,128)}, bf16[1536,1024]...) custom-call(s32[1]{0:T(128)S(6)} %copy.44.count_ref, ...), custom_call_target="tpu_custom_call" | custom-call | tf_op jit(solution)/shard_map/pallas_call | solution.py:643
  149.6 2.7 split.15.packed_ref
  152.3 4.7 fusion.9
  157.0 39.2 %shard_map.230 = (f32[1536,1024]{1,0:T(8,128)}, bf16[1536,1024]{1,0:T(8,128)(2,1)}, bf16[384,1024]{1,0:T(8,128)(2,1)}, bf16[1536,128]{1,0:T(8,128)(2,1)}) custom-call(bf16[1536,1024]{1,0:T(8,128)(2,1)} %get-tuple-element.36.normed2_ref, bf16[1024,1024]{1,0:T(8,128)(2,1)} %get-tuple-element.69.up_ref, bf16[1024,1024]{1,0:T(8,128)(2,1)} %get-tuple-element.68.down_ref, ...), custom_call_target="tpu_custom_call" | custom-call | tf_op jit(solution)/shard_map/pallas_call | solution.py:713
  197.2 49.3 %shard_map.231 = (f32[8,128]{1,0:T(8,128)S(1)}, bf16[1536,128]{1,0:T(8,128)(2,1)S(1)}) custom-call(bf16[1536,128]{1,0:T(8,128)(2,1)S(1)} %copy-done, s32[4,6144]{1,0:T(4,128)S(1)} %bitcast.53, s32[4,6144]{1,0:T(4,128)S(1)} %bitcast.54, s32[1,6144]{1,0:T(1,128)S(1)} %copy-done.2), custom_call_target="tpu_custom_call" | custom-call | tf_op jit(solution)/shard_map/pallas_call | solution.py:1032
  247.3 67.8 %shard_map.232 = (f32[1024,128]{1,0:T(8,128)}, f32[2048,1024]{1,0:T(8,128)}, f32[384,1024]{1,0:T(8,128)}, bf16[1536,1024]{1,0:T(8,128)(2,1)}, f32[2,1024]{1,0:T(2,128)}) custom-call(bf16[1536,128]{1,0:T(8,128)(2,1)} %copy-done.1, bf16[1024,128]{1,0:T(8,128)(2,1)} %get-tuple-element.39.cols_ref, bf16[384,1024]{1,0:T(8,128)(2,1)} %get-tuple-element.42.low_ref, ...), custom_call_target="tpu_custom_call" | custom-call | tf_op jit(solution)/shard_map/pallas_call | solution.py:819
  315.0 64.9 %shard_map.233 = (f32[1024,1024]{1,0:T(8,128)}, f32[576,1024]{1,0:T(8,128)}, f32[2,1024]{1,0:T(2,128)}) custom-call(s32[1]{0:T(128)S(6)} %copy.44.count_ref, bf16[1536,1024]{1,0:T(8,128)(2,1)} %get-tuple-element.46.branch_ref, bf16[256,1024]{1,0:T(8,128)(2,1)} %split.14.out_ref, bf16[1536,768]{1,0:T(8,128)(2,1)} %get-tuple-element.47.qkv_ref, ...), custom_call_target="tpu_custom_call" | custom-call | tf_op jit(solution)/shard_map/pallas_call | solution.py:932
  380.0 2.3 copy.37
  384.2 4.4 reshape.145
  388.6 6.7 pad_maximum_fusion.2
  395.3 5.6 reshape.147
  400.9 6.0 pad_bitcast_fusion
  409.5 11.8 %pad_maximum_fusion.1 = f32[3072,1024]{1,0:T(8,128)} fusion(f32[2048,1024]{1,0:T(8,128)} %get-tuple-element.54, f32[1024,1024]{1,0:T(8,128)} %get-tuple-element.53), kind=kLoop, calls=%fused_computation.1 | loop fusion | flops 3145728 | bytes 25165824 | tf_op jit(solution)/shard_map/concatenate | solution.py:1368
  421.3 126.3 %all-reduce.7.cloned.1.call-done = f32[4,8,384,128]{3,2,0,1:T(8,128)} async-done(((f32[4,8,384,128]{3,2,0,1:T(8,128)}), f32[4,8,384,128]{3,2,0,1:T(8,128)}) %all-reduce.7.cloned.1.call-update) | async-done | bytes 6291472
  547.5 2.2 constant_dynamic-slice_fusion
  549.9 10.0 %pad_maximum_fusion = f32[8,432,1024]{2,1,0:T(8,128)} fusion(f32[8,48,1024]{2,1,0:T(8,128)S(1)} %reshape.148, f32[8,384,1024]{2,1,0:T(8,128)} %bitcast.56), kind=kLoop, calls=%fused_computation | loop fusion | flops 3538944 | bytes 28311552 | tf_op jit(solution)/shard_map/concatenate | solution.py:1369
  560.0 138.1 %shard_map.234 = f32[432,1024]{1,0:T(8,128)} custom-call(f32[3456,1024]{1,0:T(8,128)} %bitcast.55), custom_call_target="tpu_custom_call" | custom-call | tf_op jit(solution)/shard_map/pallas_call | solution.py:1167
  701.4 9.3 %all-gather.1 = f32[4,337,128]{2,1,0:T(8,128)} all-gather(f32[1,337,128]{2,1,0:T(8,128)S(1)} %get-tuple-element.74), channel_id=2, replica_groups=mesh['dp'=8,'tensor'=4] {'tensor'}, dimensions={0}, use_global_device_ids=true | all-gather | bytes 862720 | tf_op jit(solution)/shard_map/all_gather | solution.py:1376
  714.4 2.8 copy.39
  725.2 9.6 %shard_map.235 = f32[8,128]{1,0:T(8,128)} custom-call(f32[8,128]{1,0:T(8,128)} %pad.18.mine_ref), custom_call_target="tpu_custom_call" | custom-call | tf_op jit(solution)/shard_map/pallas_call | solution.py:1230
  739.7 3.2 fusion.5
  742.9 2.4 multiply_add_fusion.2
  745.3 13.4 %fusion.7 = (bf16[1,393216]{1,0:T(2,128)(2,1)}, f32[1,393216]{1,0:T(1,128)S(1)}, f32[1,393216]{1,0:T(1,128)}, f32[1,393216]{1,0:T(1,128)}) fusion(f32[1,393216]{1,0:T(1,128)S(1)} %copy-done.7, f32[]{:T(128)} %bitcast.29, f32[]{:T(128)} %bitcast.28, f32[]{:T(128)S(6)} %div.44, f32[1,393216]{1,0:T(1,128)S(1)} %bitcast.59, f32[1,393216]{1,0:T(1,128)S(1)} %bitcast.60, ...), kind=kLoop, calls=%fused_computation.33 | loop fusion | flops 7077888 | bytes 13369357 | tf_op jit(solution)/shard_map/convert_element_type | solution.py:1400
  758.7 3.5 multiply_add_fusion
  (72 shorter events, 26.7 us)
Async XLA Ops:
  7.2 540.4 %all-reduce.7.cloned.1.call-start = ((), (), s32[]{:S(2)}) async-start(), calls=%async_computation | async-start | bytes 12582912
  157.0 39.2 %copy-start.2 = (s32[1,6144]{1,0:T(1,128)S(1)}, s32[1,6144]{1,0:T(1,128)}, u32[]{:S(2)}) copy-start(s32[1,6144]{1,0:T(1,128)} %label_ref.1) | copy-start | bytes 73732
  157.0 39.2 %copy-start.3 = (s32[1,4,6144]{2,1,0:T(4,128)S(1)}, s32[1,4,6144]{2,1,0:T(4,128)}, u32[]{:S(2)}) copy-start(s32[1,4,6144]{2,1,0:T(4,128)} %param.16) | copy-start | bytes 294916
  157.0 39.2 %copy-start.4 = (s32[1,4,6144]{2,1,0:T(4,128)S(1)}, s32[1,4,6144]{2,1,0:T(4,128)}, u32[]{:S(2)}) copy-start(s32[1,4,6144]{2,1,0:T(4,128)} %param.17) | copy-start | bytes 294916
  196.2 1.0 copy-start
  246.5 0.7 copy-start.1
  380.0 2.3 copy-start.16
  380.0 2.3 copy-start.17
  380.0 2.3 copy-start.15
  406.9 1.3 copy-start.18
  699.6 1.1 copy-start.6
  699.6 1.1 slice-start
  700.8 10.0 %slice-start.2 = ((f32[1,384,1024]{2,1,0:T(8,128)}), f32[1,256,1024]{2,1,0:T(8,128)S(1)}, s32[]{:S(2)}) async-start(f32[1,384,1024]{2,1,0:T(8,128)} %copy-done.6), calls=%async_computation.3 | async-start | bytes 2097152 | tf_op jit(solution)/shard_map/slice | solution.py:1256
  711.6 1.0 slice-start.1
  717.1 2.0 copy-start.5
  720.2 19.3 %copy-start.10 = (f32[4,337,128]{2,1,0:T(8,128)S(1)}, f32[4,337,128]{2,1,0:T(8,128)}, u32[]{:S(2)}) copy-start(f32[4,337,128]{2,1,0:T(8,128)} %all-gather.1) | copy-start | bytes 2070532
  739.6 5.6 copy-start.8
  739.7 5.6 copy-start.13
  739.7 5.6 copy-start.14
  742.9 15.9 %copy-start.11 = (f32[172544]{0:T(1024)}, f32[172544]{0:T(1024)S(1)}, u32[]{:S(2)}) copy-start(f32[172544]{0:T(1024)S(1)} %get-tuple-element.61) | copy-start | bytes 2070532
  742.9 2.4 copy-start.7
  745.3 13.5 %copy-start.12 = (f32[1,393216]{1,0:T(1,128)S(1)}, f32[1,393216]{1,0:T(1,128)}, u32[]{:S(2)}) copy-start(f32[1,393216]{1,0:T(1,128)} %param.23) | copy-start | bytes 4718596
  758.7 3.6 copy-start.9
Sparse Core Ops, SparseCore 0:
  407.1 140.3 all-reduce.6

commit v4 on v3

--- a/solution.py
+++ b/solution.py
@@ -953,6 +953,409 @@
             collective_id=collective_id, has_side_effects=True, vmem_limit_bytes=62 * 2**20
         ),
     )(count, branch, out_proj, qkv, log_total, packed, attended, normed1, embed, resid_grad, norm, patches)
+
+
+class LineSum:
+    def __init__(self, spot, pieces, low, source, buffers, sems):
+        self.spot, self.pieces, self.low, self.source = spot, pieces, low, source
+        self.pair_out, self.pair_in, self.part, self.line_in, self.low_out, self.low_in = buffers
+        self.p_send, self.p_recv, self.l_send, self.up_recv, self.down_recv = sems
+        self.count = spot.lines * pieces
+        self.rows = self.part.shape[0] // self.count
+
+    @staticmethod
+    def scratch(lines, rows, pieces, width, low):
+        half = (lines * rows, width)
+        kept = half if low else (rows, width)
+        kind = LOW if low else WIDE
+        return [
+            pltpu.VMEM(half, LOW),
+            pltpu.VMEM(half, LOW),
+            pltpu.VMEM(half, WIDE),
+            pltpu.VMEM(half, WIDE),
+            pltpu.VMEM(half if low else (16, 128), LOW),
+            pltpu.VMEM(kept, kind),
+        ] + [pltpu.SemaphoreType.DMA((lines * pieces,))] * 5
+
+    def target(self, step):
+        turn = lax.rem(step, self.spot.lines)
+        odd = lax.rem(turn, 2)
+        return (1 - odd) * (self.spot.lines - 1 - turn // 2) + odd * (turn // 2)
+
+    def slot(self, step):
+        return pl.ds(pl.multiple_of(step * self.rows, 16), self.rows)
+
+    def pair_copy(self, step):
+        slot = self.slot(step)
+        return remote(self.pair_out.at[slot], self.pair_in.at[slot], self.p_send.at[step], self.p_recv.at[step], self.spot.pair)
+
+    def line_copy(self, step, to, recv):
+        slot = self.slot(step)
+        return remote(self.part.at[slot], self.line_in.at[slot], self.l_send.at[step], recv.at[step], to)
+
+    def low_copy(self, step, to, recv):
+        slot = self.slot(step)
+        return remote(self.low_out.at[slot], self.low_in.at[slot], self.l_send.at[step], recv.at[step], to)
+
+    def last_copy(self, step):
+        here = pl.ds(pl.multiple_of(step // self.spot.lines * self.rows, 16), self.rows)
+        return remote(self.part.at[self.slot(step)], self.low_in.at[here], self.l_send.at[step], self.down_recv.at[step], self.spot.below)
+
+    def begin(self, step):
+        self.pair_out[self.slot(step)] = self.source(self.target(step), 1 - self.spot.side, step // self.spot.lines).astype(LOW)
+        self.pair_copy(step).start()
+
+    def add(self, step, low):
+        slot = self.slot(step)
+        self.part[slot] += self.low_in[slot].astype(WIDE) if low else self.line_in[slot]
+
+    def travel(self, step, rising):
+        spot, slot = self.spot, self.slot(step)
+        to, recv = (spot.above, self.up_recv) if rising else (spot.below, self.down_recv)
+        last = spot.lines - 1
+        from_end = spot.line == (1 if rising else last - 1)
+        at_end = spot.line == (0 if rising else last)
+        target = self.target(step)
+        if self.low:
+
+            @pl.when(at_end)
+            def _():
+                self.low_out[slot] = self.part[slot].astype(LOW)
+                self.low_copy(step, to, recv).start()
+
+            @pl.when(from_end)
+            def _():
+                self.low_copy(step, to, recv).wait_recv()
+                self.add(step, True)
+
+            @pl.when(jnp.logical_not(at_end | from_end))
+            def _():
+                self.line_copy(step, to, recv).wait_recv()
+                self.add(step, False)
+
+            @pl.when(jnp.logical_not(at_end))
+            def _():
+                self.line_copy(step, to, recv).start()
+        else:
+
+            @pl.when(jnp.logical_not(at_end))
+            def _():
+                self.line_copy(step, to, recv).wait_recv()
+                self.add(step, False)
+
+            if rising:
+                self.line_copy(step, to, recv).start()
+            else:
+
+                @pl.when(target == spot.line - 1)
+                def _():
+                    self.last_copy(step).start()
+
+                @pl.when(target < spot.line - 1)
+                def _():
+                    self.line_copy(step, to, recv).start()
+
+    def advance(self, step):
+        spot = self.spot
+
+        @pl.when(step < self.count)
+        def _():
+            slot = self.slot(step)
+            self.pair_copy(step).wait_recv()
+            own = self.source(self.target(step), spot.side, step // spot.lines)
+            self.part[slot] = own + self.pair_in[slot].astype(WIDE)
+
+        rising = step - spot.line
+
+        @pl.when((rising >= 0) & (rising < self.count) & (self.target(rising) > spot.line))
+        def _():
+            self.travel(rising, True)
+
+        falling = step - (spot.lines - 1 - spot.line)
+
+        @pl.when((falling >= 0) & (falling < self.count) & (self.target(falling) < spot.line))
+        def _():
+            self.travel(falling, False)
+
+    def close(self, step, give):
+        spot, slot = self.spot, self.slot(step)
+        target = self.target(step)
+        last = spot.lines - 1
+        self.pair_copy(step).wait_send()
+
+        @pl.when(target > spot.line)
+        def _():
+            if self.low:
+
+                @pl.when(spot.line == 0)
+                def _():
+                    self.low_copy(step, spot.above, self.up_recv).wait_send()
+
+                @pl.when(spot.line > 0)
+                def _():
+                    self.line_copy(step, spot.above, self.up_recv).wait_send()
+            else:
+                self.line_copy(step, spot.above, self.up_recv).wait_send()
+
+        @pl.when(target < spot.line)
+        def _():
+            if self.low:
+
+                @pl.when(spot.line == last)
+                def _():
+                    self.low_copy(step, spot.below, self.down_recv).wait_send()
+
+                @pl.when(spot.line < last)
+                def _():
+                    self.line_copy(step, spot.below, self.down_recv).wait_send()
+            else:
+                self.line_copy(step, spot.below, self.down_recv).wait_send()
+
+        @pl.when(target == spot.line)
+        def _():
+            if self.low:
+
+                @pl.when(spot.line == 1)
+                def _():
+                    self.low_copy(step, spot.above, self.up_recv).wait_recv()
+                    self.add(step, True)
+
+                @pl.when(spot.line > 1)
+                def _():
+                    self.line_copy(step, spot.above, self.up_recv).wait_recv()
+                    self.add(step, False)
+
+                @pl.when(spot.line == last - 1)
+                def _():
+                    self.low_copy(step, spot.below, self.down_recv).wait_recv()
+                    self.add(step, True)
+
+                @pl.when(spot.line < last - 1)
+                def _():
+                    self.line_copy(step, spot.below, self.down_recv).wait_recv()
+                    self.add(step, False)
+            else:
+
+                @pl.when(spot.has_below)
+                def _():
+                    self.line_copy(step, spot.above, self.up_recv).wait_recv()
+                    self.add(step, False)
+
+                @pl.when(spot.has_above)
+                def _():
+                    self.last_copy(step).wait_recv()
+                    here = pl.ds(pl.multiple_of(step // spot.lines * self.rows, 16), self.rows)
+                    self.part[slot] += self.low_in[here]
+
+            give(step // spot.lines, self.part[slot])
+
+
+SUM_PIECES = 6
+
+
+def share_kernel(lines, early_ref, late_ref, patch_ref, used_ref, gain_ref, loss_ref, label_ref,
+                 row_ref, shared_ref, total_ref,
+                 term, windows, mine, slots, rows_out, *comm):
+    corner, spot = Corner(), Lines(lines)
+    pairs, width = 2 * lines, early_ref.shape[1]
+    quarters = 4
+    count = pairs * quarters
+    me = spot.me * quarters + corner.me
+    barrier = pltpu.get_barrier_semaphore()
+
+    def peer(step):
+        other = lax.rem(me + step, count)
+        return {"dp": other // quarters, "tensor": lax.rem(other, quarters)}
+
+    @pl.loop(1, count)
+    def _(step):
+        pl.semaphore_signal(barrier, inc=1, device_id=peer(step), device_id_type=MESH)
+
+    pl.semaphore_wait(barrier, count - 1)
+    chunk = (early_ref.shape[0] + late_ref.shape[0]) // pairs
+    rows = chunk // SUM_PIECES
+    edge = early_ref.shape[0]
+
+    def weight_term(line, side, piece):
+        start = (line * 2 + side) * chunk + piece * rows
+        inside = start < edge
+        first = early_ref[pl.ds(pl.multiple_of(jnp.where(inside, start, 0), 8), rows)]
+        second = late_ref[pl.ds(pl.multiple_of(jnp.where(inside, 0, start - edge), 8), rows)]
+        return jnp.where(inside, first, second)
+
+    def shared_term(line, side, piece):
+        return mine[pl.ds(pl.multiple_of((line * 2 + side) * WINDOW, 16), WINDOW)]
+
+    weights = LineSum(spot, SUM_PIECES, True, weight_term, comm[0:6], comm[6:11])
+    shared = LineSum(spot, 1, False, shared_term, comm[11:17], comm[17:22])
+    scatter = Scatter(corner, PIECES, *comm[22:30])
+    gather = Gather(corner, windows, 1, comm[30:36])
+    own_sem, send_sem, recv_sem = comm[36:39]
+
+    @pl.loop(0, weights.count)
+    def _(step):
+        weights.begin(step)
+
+    @pl.loop(0, 4)
+    def _(step):
+        block = corner.block(step)
+        term[...] = jnp.zeros_like(term)
+
+        def rows_at(start, size):
+            return pl.ds(pl.multiple_of(start, 16), size)
+
+        for owner in range(3):
+            at = owner * WINDOW
+            term[at : at + WINDOW] = patch_ref[rows_at(ROW_START[owner] + block * WINDOW, WINDOW)]
+
+        @pl.when(block < 3)
+        def _():
+            at = 3 * WINDOW
+            term[at : at + 16] = patch_ref[rows_at(ROW_START[3] + block * 32, 16)]
+
+            @pl.when(block < 2)
+            def _():
+                term[at + 16 : at + 32] = patch_ref[rows_at(ROW_START[3] + block * 32 + 16, 16)]
+
+            for j in range(3):
+                term[at + 32 : at + 48, j * 128 : (j + 1) * 128] = used_ref[rows_at(block * 48 + 16 * j, 16)]
+
+        for owner in range(4, 8):
+            at = owner * WINDOW
+            for j in range(2):
+
+                @pl.when((block < 3) | (owner < 7) | (j < 1))
+                def _():
+                    term[at : at + 32, j * 128 : (j + 1) * 128] = used_ref[rows_at(USED_START[owner] + block * 64 + 32 * j, 32)]
+
+        @pl.when(block == 0)
+        def _():
+            term[7 * WINDOW + 32 : 7 * WINDOW + 40] = gain_ref[...]
+
+        scatter.step(step, term)
+
+    @pl.loop(0, 8)
+    def _(step):
+        weights.advance(step)
+
+    for piece in range(PIECES):
+        mine[scatter.part(piece)] = scatter.land(piece, term)
+    for step in range(lines):
+        shared.begin(step)
+
+    @pl.loop(8, weights.count + lines - 1)
+    def _(step):
+        weights.advance(step)
+
+    for step in range(2 * lines - 1):
+        shared.advance(step)
+
+    def keep_window(piece, value):
+        windows[gather.part(corner.me, 0)] = value
+
+    @pl.loop(0, lines)
+    def _(step):
+        shared.close(step, keep_window)
+
+    gather.start(0)
+
+    def keep_rows(piece, value):
+        rows_out[pl.ds(pl.multiple_of(piece * rows, rows), rows)] = value
+
+    @pl.loop(0, weights.count)
+    def _(step):
+        weights.close(step, keep_rows)
+
+    gather.relay(0)
+
+    @pl.when(spot.me < lines // 2)
+    def _():
+        for row, height, col, cols, at, at_col in qkv_places(1, chunk * 4 // 3, width * 3 // 4):
+            for j in range(cols // 128):
+                row_ref[pl.ds(6 * at + at_col // 128 + j, height, 6)] = rows_out[
+                    row : row + height, col + j * 128 : col + (j + 1) * 128
+                ]
+
+    @pl.when(spot.me >= lines // 2)
+    def _():
+        for j in range(8):
+            row_ref[pl.ds(j, chunk, 8)] = rows_out[:, j * 128 : (j + 1) * 128]
+
+    squares = jnp.sum(rows_out[...] * rows_out[...], 0, keepdims=True)
+    gather.finish()
+    shared_ref[...] = jnp.zeros_like(shared_ref)
+    for phase in range(5):
+        for quarter in range(4):
+
+            def take(condition, row, height, j, start, stride):
+                @pl.when(condition)
+                def _():
+                    at = quarter * WINDOW + row
+                    shared_ref[pl.ds(start, height, stride)] = windows[at : at + height, j * 128 : (j + 1) * 128]
+
+            shared_walk(spot.me, quarter, take, (phase,))
+    kept = shared_ref[FRONT : FRONT + PADDED - FRONT]
+    place = lax.broadcasted_iota(jnp.int32, kept.shape, 0)
+    kept = jnp.where((place < SHARED_LANES) & (corner.me == 0), kept, 0.0)
+    square = jnp.sum(jnp.sum(squares, 1, keepdims=True)) + jnp.sum(kept * kept)
+    counted = jnp.sum(jnp.where(label_ref[...] < 2, 1.0, 0.0))
+    line = lax.broadcasted_iota(jnp.int32, total_ref.shape, 0)
+    slots[me] = jnp.where(line == 0, square, jnp.where(line == 1, loss_ref[...], jnp.where(line == 2, counted, 0.0)))
+
+    def send(step):
+        return remote(slots.at[me], slots.at[me], send_sem.at[step], recv_sem.at[step], peer(step))
+
+    def arrive(step):
+        source = lax.rem(me - step + count, count)
+        return remote(slots.at[source], slots.at[source], send_sem.at[step], recv_sem.at[step], peer(step))
+
+    @pl.loop(1, count)
+    def _(step):
+        send(step).start()
+
+    @pl.loop(1, count)
+    def _(step):
+        arrive(step).wait_recv()
+
+    total_ref[...] = jnp.sum(slots[...], 0)
+
+    @pl.loop(1, count)
+    def _(step):
+        send(step).wait_send()
+
+    scatter.close()
+
+
+def share(early, late, patch_grad, used_grad, gains, loss_tile, labels, lines, collective_id):
+    width = early.shape[1]
+    chunk = (early.shape[0] + late.shape[0]) // (2 * lines)
+    count = 8 * lines
+    shape = jax.ShapeDtypeStruct
+    return pl.pallas_call(
+        partial(share_kernel, lines),
+        out_shape=(shape((chunk * width // 128, 128), WIDE), shape((PADDED, 128), WIDE), shape((8, 128), WIDE)),
+        in_specs=[VMEM] * 7,
+        out_specs=(VMEM,) * 3,
+        scratch_shapes=[
+            pltpu.VMEM((2 * lines * WINDOW, width), WIDE),
+            pltpu.VMEM((4 * WINDOW, width), WIDE),
+            pltpu.VMEM((2 * lines * WINDOW, width), WIDE),
+            pltpu.VMEM((count, 8, 128), WIDE),
+            pltpu.VMEM((chunk, width), WIDE),
+        ]
+        + LineSum.scratch(lines, chunk, SUM_PIECES, width, True)
+        + LineSum.scratch(lines, WINDOW, 1, width, False)
+        + Scatter.scratch(2 * lines * WINDOW, width, PIECES)
+        + Gather.scratch(1)
+        + [
+            pltpu.SemaphoreType.DMA(()),
+            pltpu.SemaphoreType.DMA((count,)),
+            pltpu.SemaphoreType.DMA((count,)),
+        ],
+        compiler_params=pltpu.CompilerParams(
+            collective_id=collective_id, has_side_effects=True, vmem_limit_bytes=63 * 2**20
+        ),
+    )(early, late, patch_grad, used_grad, gains, loss_tile, labels)
 
 
 def render_kernel(area, wide, block, split, table_ref, splat_ref, dist_ref, label_ref, loss_ref, grad_ref, flip, picked, hot, spread_grad):
@@ -1282,6 +1685,28 @@
         first_hat / (jnp.sqrt(second_hat) + adam_eps) + decay_rate * master
     )
     return (master_new, first_new, second_new)
+
+
+def adam_kernel(total_ref, count_ref, *refs):
+    norm_value = jnp.sqrt(total_ref[0, 0:1]) / total_ref[2, 0:1]
+    factor = clip_norm / jnp.maximum(norm_value, clip_norm) / total_ref[2, 0:1]
+    step_float = jnp.full((1, 1), count_ref[0], jnp.int32).astype(WIDE)
+    grad, master, first, second, ema = (ref[...] for ref in refs[:5])
+    new, first_new, second_new = adam_update(master, first, second, grad * factor.reshape(1, 1), step_float)
+    for ref, value in zip(refs[5:], (new, first_new, second_new, ema_rate * ema + (1.0 - ema_rate) * new, new.astype(LOW))):
+        ref[...] = value
+
+
+def adam(totals, step_count, grad, master, first, second, ema, block):
+    size = master.shape[1]
+    spec = pl.BlockSpec((1, block), lambda at: (0, at))
+    return pl.pallas_call(
+        adam_kernel,
+        grid=(size // block,),
+        out_shape=tuple(jax.ShapeDtypeStruct(master.shape, kind) for kind in (WIDE,) * 4 + (LOW,)),
+        in_specs=[pl.BlockSpec((8, 128), lambda at: (0, 0)), pl.BlockSpec(memory_space=pltpu.SMEM)] + [spec] * 5,
+        out_specs=(spec,) * 5,
+    )(totals, step_count, grad, master, first, second, ema)
 
 
 def per_device(
@@ -1355,49 +1780,56 @@
         view_counts, branch, out_proj, qkv, log_total, packed_qkv, attended, normed1, embed, resid_grad, norm, own_patches, qkv_parts, 6
     )
     gain_grad = jnp.concatenate([gain1_grad, gain2_grad], 0)
-    unpatch_grad = jnp.concatenate(
-        [unpatch_used, jnp.zeros((D, POUT - unpatch_used.shape[1]), jnp.float32)], 1
-    )
-    shared_grad = jnp.concatenate(
-        [patch_grad.reshape(-1), unpatch_grad.reshape(-1), gain_grad.reshape(-1)]
-    )
-    split_grad = by_lanes(shared_grad, (count_dp, groups))
-    lead = split_grad.shape[2]
-    shared_stack = pad_first(split_grad, 2, 16 * D // split_grad[0, 0, 0].size).swapaxes(0, 1)
-    shared_sum = lax.psum_scatter(shared_stack, "tensor", scatter_dimension=0, tiled=True)
-    row_stack = jnp.concatenate([early_grad, late_grad], 0)
-    stack = jnp.concatenate(
-        [row_stack.reshape(count_dp, share_rows, D), shared_sum.reshape(count_dp, -1, D)], 1
-    ).reshape(-1, D)
-    own_share = sum_to_owners(stack, count_dp)
-    own_rows = own_share[:share_rows]
-    row_share = jnp.where(my_dp < qkv_parts, unpack_qkv(own_rows, 1).reshape(-1), own_rows.reshape(-1))
-    shared_part = own_share[share_rows:].reshape((-1,) + split_grad.shape[3:])[:lead]
-    shared_share = lax.all_gather(shared_part, "tensor", axis=0, tiled=False).reshape(-1)
-    own_squares = jnp.sum(row_share * row_share) + jnp.sum(shared_part * shared_part)
-    pixel_part = jnp.sum((alpha_label < 2).astype(jnp.float32))
-    scalars = jnp.stack([own_squares, loss_part, pixel_part]).reshape(3, 1)
-    totals = total_over_all(jnp.pad(jnp.broadcast_to(scalars, (3, 128)), ((0, 5), (0, 0))), 2)
+    if count_dp == 8:
+        gains = jnp.pad(gain_grad, ((0, 4), (0, 0)))
+        row_lanes, shared_kept, totals = share(
+            early_grad, late_grad, patch_grad, unpatch_used, gains, loss_tile, alpha_label, count_dp // 2, 8
+        )
+        row_share = row_lanes.reshape(-1)
+        shared_share = shared_kept[FRONT : FRONT + SHARED_LANES].reshape(-1)
+    else:
+        unpatch_grad = jnp.concatenate(
+            [unpatch_used, jnp.zeros((D, POUT - unpatch_used.shape[1]), jnp.float32)], 1
+        )
+        shared_grad = jnp.concatenate(
+            [patch_grad.reshape(-1), unpatch_grad.reshape(-1), gain_grad.reshape(-1)]
+        )
+        split_grad = by_lanes(shared_grad, (count_dp, groups))
+        lead = split_grad.shape[2]
+        shared_stack = pad_first(split_grad, 2, 16 * D // split_grad[0, 0, 0].size).swapaxes(0, 1)
+        shared_sum = lax.psum_scatter(shared_stack, "tensor", scatter_dimension=0, tiled=True)
+        row_stack = jnp.concatenate([early_grad, late_grad], 0)
+        stack = jnp.concatenate(
+            [row_stack.reshape(count_dp, share_rows, D), shared_sum.reshape(count_dp, -1, D)], 1
+        ).reshape(-1, D)
+        own_share = sum_to_owners(stack, count_dp)
+        own_rows = own_share[:share_rows]
+        row_share = jnp.where(my_dp < qkv_parts, unpack_qkv(own_rows, 1).reshape(-1), own_rows.reshape(-1))
+        shared_part = own_share[share_rows:].reshape((-1,) + split_grad.shape[3:])[:lead]
+        shared_share = lax.all_gather(shared_part, "tensor", axis=0, tiled=False).reshape(-1)
+        own_squares = jnp.sum(row_share * row_share) + jnp.sum(shared_part * shared_part)
+        pixel_part = jnp.sum((alpha_label < 2).astype(jnp.float32))
+        scalars = jnp.stack([own_squares, loss_part, pixel_part]).reshape(3, 1)
+        totals = total_over_all(jnp.pad(jnp.broadcast_to(scalars, (3, 128)), ((0, 5), (0, 0))), 2)
     square_total, loss_total, pixel_total = totals[0, 0], totals[1, 0], totals[2, 0]
     norm_value = jnp.sqrt(square_total) / pixel_total
     factor = clip_norm / jnp.maximum(norm_value, clip_norm) / pixel_total
     step_float = step_count[0].astype(jnp.float32)
-    row_new, row_first_new, row_second_new = adam_update(
-        row_master[0], row_first[0], row_second[0], row_share * factor, step_float
+    row_new, row_first_new, row_second_new, row_ema_new, row_copy = adam(
+        totals, step_count, row_share[None], row_master, row_first, row_second, row_ema, row_master.shape[1] // 6
     )
     shared_new, shared_first_new, shared_second_new = adam_update(
         shared_master, shared_first, shared_second, shared_share * factor, step_float
     )
-    row_ema_new = ema_rate * row_ema[0] + (1.0 - ema_rate) * row_new
     shared_ema_new = ema_rate * shared_ema + (1.0 - ema_rate) * shared_new
     return (
         norm_value.reshape(1),
         (loss_total / pixel_total).reshape(1),
-        row_new[None],
-        row_first_new[None],
-        row_second_new[None],
-        row_ema_new[None],
-        row_new.astype(jnp.bfloat16)[None],
+        row_new,
+        row_first_new,
+        row_second_new,
+        row_ema_new,
+        row_copy,
         shared_new,
         shared_first_new,
         shared_second_new,

time: 779 us -> 538 us (0.69)
  waiting for transfers between devices: 126 us -> 0 us
  other arithmetic: 56.2 us -> 5.49 us
  local copies, waits for them, and re-layouts: 52.1 us -> 16.9 us
  between operations: 23 us -> 7.81 us
  blocking collectives: 9.31 us -> 0 us
    unnamed x2 -> x0, waiting for transfers between devices: 126 us -> none
    concatenate x3 -> x1, other arithmetic: 28.6 us -> 1.32 us  [per_device(): gain_grad = jnp.concatenate([gain1_grad, gain2_grad], 0)]
    convert_element_type x1 -> x0, other arithmetic: 13.4 us -> none  [per_device(): row_new.astype(jnp.bfloat16)[None]]
    reshape x7 -> x0, local copies, waits for them, and re-layouts: 12.9 us -> none  [the longest x1 5.57 us: by_lanes(): flat.reshape(outer + ((size // 128, 128) if size % 128 == 0 else (size,)))]
    unnamed x45 -> x21, local copies, waits for them, and re-layouts: 14.3 us -> 4.35 us
    all_gather x1 -> x0, blocking collectives: 9.31 us -> none  [per_device(): lax.all_gather(shared_part, 'tensor', axis=0, tiled=False).reshape(-1)]
  transfers between devices with their start and end apart: 1 -> 0, of which waited for: 1 -> 0; matrix products, arithmetic and copies ran while one was open for 2% -> 0% of each run, Pallas kernels for 0% -> 0%
where the time goes in v4:
time: 538 us; the launch traced here: 537 us
  Pallas kernels  507 us (94%)
  local copies, waits for them, and re-layouts  16.9 us (3%)
  between operations  7.81 us (1%)
  other arithmetic  5.49 us (1%)
    pallas_call x1, Pallas kernels, share(): pl.pallas_call(partial(share_kernel, lines), out_shape=(shape((chunk * wi...  142 us
    pallas_call x1, Pallas kernels, forward(): pl.pallas_call(partial(forward_kernel, lines, 256), out_shape=(shape((3 *...  136 us
    pallas_call x1, Pallas kernels, mlp_back(): pl.pallas_call(mlp_back_kernel, out_shape=(shape((width, used), WIDE), sh...  67.7 us
    pallas_call x1, Pallas kernels, attend_back(): pl.pallas_call(partial(attend_back_kernel, parts, 256), out_shape=(shape(...  65 us
    pallas_call x1, Pallas kernels, render(): pl.pallas_call(partial(render_kernel, area, wide, block, split), out_shap...  49.3 us
    pallas_call x1, Pallas kernels, mlp(): pl.pallas_call(mlp_kernel, out_shape=(shape((length, hidden), WIDE), shap...  39.2 us

profile of v4, /device:TPU:0, one launch (start us, length us, event | category | flops | bytes accessed | tf_op | source)
XLA Modules:
  0.0 537.0 jit_solution(8654436028725613765)
XLA Ops:
  2.0 2.0 copy.26
  4.0 2.0 pad.8.shared_ref
  6.1 135.5 %shard_map.229 = (bf16[3072,1024]{1,0:T(8,128)(2,1)}, bf16[1024,128]{1,0:T(8,128)(2,1)}, f32[8,1024]{1,0:T(8,128)}, f32[384,1024]{1,0:T(8,128)}, bf16[1536,1024]...) custom-call(s32[1]{0:T(128)S(6)} %copy.27.count_ref, ...), custom_call_target="tpu_custom_call" | custom-call | tf_op jit(solution)/shard_map/pallas_call | solution.py:643
  141.6 1.9 split.14.out_ref
  143.5 2.7 split.15.packed_ref
  146.1 4.6 fusion.5
  150.8 39.2 %shard_map.230 = (f32[1536,1024]{1,0:T(8,128)}, bf16[1536,1024]{1,0:T(8,128)(2,1)}, bf16[384,1024]{1,0:T(8,128)(2,1)}, bf16[1536,128]{1,0:T(8,128)(2,1)}) custom-call(bf16[1536,1024]{1,0:T(8,128)(2,1)} %get-tuple-element.44.normed2_ref, bf16[1024,1024]{1,0:T(8,128)(2,1)} %get-tuple-element.81.up_ref, bf16[1024,1024]{1,0:T(8,128)(2,1)} %get-tuple-element.80.down_ref, ...), custom_call_target="tpu_custom_call" | custom-call | tf_op jit(solution)/shard_map/pallas_call | solution.py:713
  189.9 0.0 copy-done.2
  189.9 0.0 copy-done.3
  190.0 0.0 copy-done.4
  190.0 1.0 copy-done
  191.0 49.3 %shard_map.231 = (f32[8,128]{1,0:T(8,128)S(1)}, bf16[1536,128]{1,0:T(8,128)(2,1)S(1)}) custom-call(bf16[1536,128]{1,0:T(8,128)(2,1)S(1)} %copy-done, s32[4,6144]{1,0:T(4,128)S(1)} %bitcast.20, s32[4,6144]{1,0:T(4,128)S(1)} %bitcast.21, s32[1,6144]{1,0:T(1,128)S(1)} %copy-done.2), custom_call_target="tpu_custom_call" | custom-call | tf_op jit(solution)/shard_map/pallas_call | solution.py:1435
  240.2 0.0 copy-start.1
  240.3 0.7 copy-done.1
  241.0 0.6 copy-done.5
  241.6 67.7 %shard_map.232 = (f32[1024,128]{1,0:T(8,128)}, f32[2048,1024]{1,0:T(8,128)}, f32[384,1024]{1,0:T(8,128)}, bf16[1536,1024]{1,0:T(8,128)(2,1)}, f32[2,1024]{1,0:T(2,128)}) custom-call(bf16[1536,128]{1,0:T(8,128)(2,1)} %copy-done.1, bf16[1024,128]{1,0:T(8,128)(2,1)} %get-tuple-element.47.cols_ref, bf16[384,1024]{1,0:T(8,128)(2,1)} %get-tuple-element.50.low_ref, ...), custom_call_target="tpu_custom_call" | custom-call | tf_op jit(solution)/shard_map/pallas_call | solution.py:819
  309.3 65.0 %shard_map.233 = (f32[1024,1024]{1,0:T(8,128)}, f32[576,1024]{1,0:T(8,128)}, f32[2,1024]{1,0:T(2,128)}) custom-call(s32[1]{0:T(128)S(6)} %copy.27.count_ref, bf16[1536,1024]{1,0:T(8,128)(2,1)} %get-tuple-element.54.branch_ref, bf16[256,1024]{1,0:T(8,128)(2,1)} %split.14.out_ref, bf16[1536,768]{1,0:T(8,128)(2,1)} %get-tuple-element.55.qkv_ref, ...), custom_call_target="tpu_custom_call" | custom-call | tf_op jit(solution)/shard_map/pallas_call | solution.py:932
  374.3 1.3 select_maximum_fusion.gain_ref
  375.6 141.8 %shard_map.234 = (f32[3072,128]{1,0:T(8,128)}, f32[1616,128]{1,0:T(8,128)}, f32[8,128]{1,0:T(8,128)}) custom-call(f32[1024,1024]{1,0:T(8,128)} %get-tuple-element.61.early_ref, f32[2048,1024]{1,0:T(8,128)} %get-tuple-element.62.late_ref, f32[576,1024]{1,0:T(8,128)} %get-tuple-element.63.patch_ref, f32[1024,128]{1,0:T(8,128)} %get-tuple-element.64.used_ref, ...), custom_call_target="tpu_custom_call" | custom-call | tf_op jit(solution)/shard_map/pallas_call | solution.py:1334
  517.4 1.3 fusion.6
  522.1 0.0 copy-start.8
  522.2 3.1 fusion.2
  525.3 1.1 multiply_add_fusion
  526.3 8.4 %shard_map.235 = (f32[1,393216]{1,0:T(1,128)}, f32[1,393216]{1,0:T(1,128)}, f32[1,393216]{1,0:T(1,128)}, f32[1,393216]{1,0:T(1,128)}, bf16[1,393216]{1,0:T(2,128)(2,1)}) custom-call(f32[8,128]{1,0:T(8,128)} %get-tuple-element.68.total_ref, s32[1]{0:T(128)S(6)} %copy.28.count_ref, f32[1,393216]{1,0:T(1,128)} %bitcast.26, f32[1,393216]{1,0:T(1,128)} %refs_1_.1, ...), custom_call_target="tpu_custom_call" | custom-call | tf_op jit(solution)/shard_map/pallas_call | solution.py:1703
  (12 shorter events, 0.0 us)
Async XLA Ops:
  150.8 39.2 %copy-start.2 = (s32[1,6144]{1,0:T(1,128)S(1)}, s32[1,6144]{1,0:T(1,128)}, u32[]{:S(2)}) copy-start(s32[1,6144]{1,0:T(1,128)} %label_ref.3) | copy-start | bytes 73732
  150.8 39.2 %copy-start.3 = (s32[1,4,6144]{2,1,0:T(4,128)S(1)}, s32[1,4,6144]{2,1,0:T(4,128)}, u32[]{:S(2)}) copy-start(s32[1,4,6144]{2,1,0:T(4,128)} %param.16) | copy-start | bytes 294916
  150.8 39.2 %copy-start.4 = (s32[1,4,6144]{2,1,0:T(4,128)S(1)}, s32[1,4,6144]{2,1,0:T(4,128)}, u32[]{:S(2)}) copy-start(s32[1,4,6144]{2,1,0:T(4,128)} %param.17) | copy-start | bytes 294916
  190.0 1.0 copy-start
  240.2 0.7 copy-start.1
  241.0 0.6 copy-start.5
  309.3 65.0 %copy-start.9 = (f32[2,1024]{1,0:T(2,128)S(1)}, f32[2,1024]{1,0:T(2,128)}, u32[]{:S(2)}) copy-start(f32[2,1024]{1,0:T(2,128)} %get-tuple-element.66) | copy-start | bytes 24580
  375.6 146.5 %copy-start.7 = (f32[172544]{0:T(1024)S(1)}, f32[172544]{0:T(1024)}, u32[]{:S(2)}) copy-start(f32[172544]{0:T(1024)} %param.24) | copy-start | bytes 2070532
  522.1 3.1 copy-start.8
  525.3 9.4 %copy-start.6 = (f32[172544]{0:T(1024)}, f32[172544]{0:T(1024)S(1)}, u32[]{:S(2)}) copy-start(f32[172544]{0:T(1024)S(1)} %get-tuple-element.77) | copy-start | bytes 2070532

commit v5 on v4

--- a/solution.py
+++ b/solution.py
@@ -16,6 +16,7 @@
 PIN = 576
 POUT = 768
 VMEM = pl.BlockSpec(memory_space=pltpu.VMEM)
+HBM = pl.BlockSpec(memory_space=pl.ANY)
 ROOT_HALF = 0.5**0.5
 NORMAL_PEAK = (2.0 * math.pi) ** -0.5
 
@@ -70,8 +71,8 @@
 
 
 class Gather:
-    def __init__(self, corner, ref, pieces, sems):
-        self.corner, self.ref, self.pieces, self.sems = corner, ref, pieces, sems
+    def __init__(self, corner, ref, pieces, sems, short=None):
+        self.corner, self.ref, self.pieces, self.sems, self.short = corner, ref, pieces, sems, short
         self.size = ref.shape[0] // 4
         self.rows = self.size // pieces
 
@@ -79,29 +80,43 @@
     def scratch(pieces):
         return [pltpu.SemaphoreType.DMA((pieces,))] * 6
 
-    def part(self, owner, piece):
-        return pl.ds(pl.multiple_of(owner * self.size + piece * self.rows, self.rows), self.rows)
-
-    def copy(self, owner, piece, kind, to):
-        here = self.ref.at[self.part(owner, piece)]
-        return remote(here, here, self.sems[2 * kind].at[piece], self.sems[2 * kind + 1].at[piece], {"tensor": to})
+    def part(self, owner, piece, rows=None):
+        return pl.ds(pl.multiple_of(owner * self.size + piece * self.rows, self.rows), rows or self.rows)
+
+    def run(self, act, owner, piece, kind, to):
+        def go(rows):
+            here = self.ref.at[self.part(owner, piece, rows)]
+            sems = self.sems[2 * kind].at[piece], self.sems[2 * kind + 1].at[piece]
+            getattr(remote(here, here, *sems, {"tensor": to}), act)()
+
+        by_half(self.short, piece < self.pieces // 2, self.rows, go)
 
     def start(self, piece):
-        self.copy(self.corner.me, piece, 1, self.corner.far).start()
-        self.copy(self.corner.me, piece, 0, self.corner.mate).start()
+        self.run("start", self.corner.me, piece, 1, self.corner.far)
+        self.run("start", self.corner.me, piece, 0, self.corner.mate)
 
     def relay(self, piece):
-        self.copy(self.corner.far, piece, 1, self.corner.far).wait_recv()
-        self.copy(self.corner.far, piece, 2, self.corner.mate).start()
+        self.run("wait_recv", self.corner.far, piece, 1, self.corner.far)
+        self.run("start", self.corner.far, piece, 2, self.corner.mate)
 
     def finish(self):
         corner = self.corner
         for piece in range(self.pieces):
-            self.copy(corner.mate, piece, 0, corner.mate).wait_recv()
-            self.copy(corner.opposite, piece, 2, corner.mate).wait_recv()
-            self.copy(corner.me, piece, 0, corner.mate).wait_send()
-            self.copy(corner.me, piece, 1, corner.far).wait_send()
-            self.copy(corner.far, piece, 2, corner.mate).wait_send()
+            self.run("wait_recv", corner.mate, piece, 0, corner.mate)
+            self.run("wait_recv", corner.opposite, piece, 2, corner.mate)
+            self.run("wait_send", corner.me, piece, 0, corner.mate)
+            self.run("wait_send", corner.me, piece, 1, corner.far)
+            self.run("wait_send", corner.far, piece, 2, corner.mate)
+
+
+def by_half(short, first, rows, go):
+    if short is None:
+        go(rows)
+    elif isinstance(first, bool):
+        go(rows if first else short)
+    else:
+        pl.when(first)(lambda: go(rows))
+        pl.when(jnp.logical_not(first))(lambda: go(short))
 
 
 class Scatter:
@@ -234,18 +249,26 @@
         body(pl.ds(pl.multiple_of(tile * TILE, TILE), TILE))
 
 
-def attend_kernel(parts, q_rows, count_ref, patch_ref, proj_ref, norm_ref, packed_ref, out_ref, *rest):
+def attend_kernel(parts, q_rows, count_ref, patch_ref, proj_ref, norm_ref, weight_ref, *rest):
     corner = Corner()
     corner.greet()
-    attend_body(parts, q_rows, corner, None, count_ref, patch_ref, proj_ref, norm_ref, packed_ref, out_ref, *rest)
-
-
-def attend_body(parts, q_rows, corner, progress, count_ref, patch_ref, proj_ref, norm_ref, packed_ref, out_ref,
+    attend_body(parts, q_rows, corner, None, count_ref, patch_ref, proj_ref, norm_ref, weight_ref, *rest)
+
+
+def attend_body(parts, q_rows, corner, progress, count_ref, patch_ref, proj_ref, norm_ref, weight_ref,
                 embed_ref, normed1_ref, qkv_ref, attended_ref, log_ref, resid_ref, normed2_ref,
-                qkv_proj, term, *comm):
+                qkv_proj, term, held, held_sem, *comm):
     progress = progress or (lambda *_: None)
     scatter = Scatter(corner, PIECES, *comm[:8])
     gather = Gather(corner, normed2_ref, PIECES, comm[8:])
+    packed_rows = held.shape[0] * 3 // 4
+    packed_ref, out_ref = held.at[pl.ds(0, packed_rows)], held.at[pl.ds(packed_rows, held.shape[0] - packed_rows)]
+
+    def hold(start, target, at):
+        copy = pltpu.make_async_copy(weight_ref.at[pl.ds(start, target.shape[0])], target, held_sem.at[at])
+        copy.start()
+        copy.wait()
+
     size, width = embed_ref.shape
     length = patch_ref.shape[0]
     local = attended_ref.shape[1]
@@ -261,8 +284,10 @@
 
         scaled, inverse = standard(term[...])
         normed1_ref[here] = (scaled * norm_ref[0:1] + norm_ref[1:2]).astype(LOW)
+        progress("embed", block)
 
     progress("weights")
+    hold(0, packed_ref, 0)
     unpack_into(qkv_proj, packed_ref, parts)
 
     @pl.loop(0, 4)
@@ -300,12 +325,14 @@
         progress("turn", turn)
 
     progress("out")
+    hold(packed_rows, out_ref, 1)
 
     @pl.loop(0, 4)
     def _(step):
         here = rows_of(corner.block(step), size)
         column_loop(width, lambda cols: term.__setitem__((slice(None), cols), dot(attended_ref[here], out_ref[:, cols])))
         scatter.step(step, term)
+        progress("give", step)
 
     for piece in range(PIECES):
         part = scatter.part(piece)
@@ -321,9 +348,9 @@
     scatter.close()
 
 
-def attend(count, patches, patch_proj, norm, packed, out_proj, parts, collective_id):
+def attend(count, patches, patch_proj, norm, weights, parts, collective_id):
     length, size = patches.shape[0], patches.shape[0] // 4
-    width, local = patch_proj.shape[1], out_proj.shape[0]
+    width, local = patch_proj.shape[1], patch_proj.shape[1] // 4
     shape = jax.ShapeDtypeStruct
     return pl.pallas_call(
         partial(attend_kernel, parts, 256),
@@ -336,15 +363,20 @@
             shape((size, width), WIDE),
             shape((length, width), LOW),
         ),
-        in_specs=[pl.BlockSpec(memory_space=pltpu.SMEM)] + [VMEM] * 5,
+        in_specs=[pl.BlockSpec(memory_space=pltpu.SMEM)] + [VMEM] * 3 + [HBM],
         out_specs=(VMEM,) * 7,
-        scratch_shapes=[pltpu.VMEM((width, 3 * local), LOW), pltpu.VMEM((size, width), WIDE)]
+        scratch_shapes=[
+            pltpu.VMEM((width, 3 * local), LOW),
+            pltpu.VMEM((size, width), WIDE),
+            pltpu.VMEM((4 * local, width), LOW),
+            pltpu.SemaphoreType.DMA((2,)),
+        ]
         + Scatter.scratch(size, width, PIECES)
         + Gather.scratch(PIECES),
         compiler_params=pltpu.CompilerParams(
             collective_id=collective_id, has_side_effects=True, vmem_limit_bytes=62 * 2**20
         ),
-    )(count, patches, patch_proj, norm, packed, out_proj)
+    )(count, patches, patch_proj, norm, weights)
 
 
 class Lines:
@@ -372,9 +404,9 @@
 
 
 class LineGather:
-    def __init__(self, spot, ref, base, chunk, pieces, late_own, sems):
+    def __init__(self, spot, ref, base, chunk, pieces, late_own, sems, short=None):
         self.spot, self.ref, self.base, self.chunk, self.pieces, self.late_own = spot, ref, base, chunk, pieces, late_own
-        self.sems = sems
+        self.sems, self.short = sems, short
         self.rows = chunk // pieces
         self.steps = (spot.lines - 1) * pieces
 
@@ -382,44 +414,53 @@
     def scratch(lines, pieces):
         return [pltpu.SemaphoreType.DMA((lines * pieces,))] * 6
 
-    def copy(self, kind, line, side, piece, to):
-        start = self.base + (line * 2 + side) * self.chunk + piece * self.rows
-        here = self.ref.at[pl.ds(pl.multiple_of(start, 16), self.rows)]
-        at = line * self.pieces + piece
-        return remote(here, here, self.sems[2 * kind].at[at], self.sems[2 * kind + 1].at[at], to)
-
-    def up(self, line, piece):
-        return self.copy(0, line, self.spot.side, piece, self.spot.above)
-
-    def down(self, line, piece):
-        return self.copy(1, line, self.spot.side, piece, self.spot.below)
-
-    def across(self, line, piece):
-        return self.copy(2, line, self.spot.side, piece, self.spot.pair)
-
-    def crossed(self, line, piece):
-        return self.copy(2, line, 1 - self.spot.side, piece, self.spot.pair)
-
-    def own(self, copy):
-        @pl.loop(0, self.pieces)
+    def run(self, act, kind, line, piece, crossed=False):
+        spot = self.spot
+        side = 1 - spot.side if crossed else spot.side
+        to = (spot.above, spot.below, spot.pair)[kind]
+
+        def go(rows):
+            start = self.base + (line * 2 + side) * self.chunk + piece * self.rows
+            here = self.ref.at[pl.ds(pl.multiple_of(start, 16), rows)]
+            at = line * self.pieces + piece
+            getattr(remote(here, here, self.sems[2 * kind].at[at], self.sems[2 * kind + 1].at[at], to), act)()
+
+        by_half(self.short, line < spot.lines // 2, self.rows, go)
+
+    def own(self, kind, first=0, last=None):
+        @pl.loop(first, self.pieces if last is None else last)
         def _(piece):
-            copy(self.spot.line, piece).start()
+            self.run("start", kind, self.spot.line, piece)
+
+    def early(self):
+        return jnp.where(self.spot.line == 0, self.pieces, jnp.minimum(self.spot.line, self.pieces - 1))
 
     def begin(self):
         spot = self.spot
-        first = spot.line == 0 if self.late_own else spot.line >= 0
-
-        @pl.when(first & spot.has_above)
-        def _():
-            self.own(self.up)
+        if self.late_own:
+
+            @pl.when(spot.line == 0)
+            def _():
+                self.own(0)
+
+            return
+
+        @pl.when(spot.has_above)
+        def _():
+            self.own(0)
 
         @pl.when(spot.has_below)
         def _():
-            self.own(self.down)
-
-        @pl.when(first)
-        def _():
-            self.own(self.across)
+            self.own(1)
+
+        self.own(2)
+
+    def follow(self):
+        @pl.when(self.spot.has_below)
+        def _():
+            self.own(1)
+
+        self.own(2, 0, self.early())
 
     def step(self, at):
         spot = self.spot
@@ -428,39 +469,39 @@
         @pl.when(at < spot.line * self.pieces)
         def _():
             line = at // self.pieces
-            self.up(line, piece).wait_recv()
+            self.run("wait_recv", 0, line, piece)
 
             @pl.when(spot.has_above)
             def _():
-                self.up(line, piece).start()
-
-            self.across(line, piece).start()
+                self.run("start", 0, line, piece)
+
+            self.run("start", 2, line, piece)
 
         if self.late_own:
 
             @pl.when((at == spot.line * self.pieces - 1) & spot.has_above)
             def _():
-                self.own(self.up)
+                self.own(0)
 
             @pl.when((at == self.pieces - 1) & spot.has_below)
             def _():
-                self.own(self.across)
+                self.own(2, self.early())
 
         @pl.when(at < (spot.lines - 1 - spot.line) * self.pieces)
         def _():
             line = spot.line + 1 + at // self.pieces
-            self.down(line, piece).wait_recv()
+            self.run("wait_recv", 1, line, piece)
 
             @pl.when(spot.has_below)
             def _():
-                self.down(line, piece).start()
-
-            self.across(line, piece).start()
-
-    def wait_crossed(self, line, pieces=None):
-        @pl.loop(0, pieces or self.pieces)
+                self.run("start", 1, line, piece)
+
+            self.run("start", 2, line, piece)
+
+    def wait_crossed(self, line):
+        @pl.loop(0, self.pieces)
         def _(piece):
-            self.crossed(line, piece).wait_recv()
+            self.run("wait_recv", 2, line, piece, True)
 
     def close(self):
         spot = self.spot
@@ -468,18 +509,19 @@
         @pl.loop(0, spot.lines * self.pieces)
         def _(at):
             line, piece = at // self.pieces, lax.rem(at, self.pieces)
-            self.across(line, piece).wait_send()
+            self.run("wait_send", 2, line, piece)
 
             @pl.when((line <= spot.line) & spot.has_above)
             def _():
-                self.up(line, piece).wait_send()
+                self.run("wait_send", 0, line, piece)
 
             @pl.when((line >= spot.line) & spot.has_below)
             def _():
-                self.down(line, piece).wait_send()
+                self.run("wait_send", 1, line, piece)
 
 
 WINDOW = 48
+SHORT = 16
 FRONT = 80
 PADDED = 1616
 ROW_START = (0, 160, 336, 496)
@@ -510,11 +552,11 @@
         for j in range(3):
             take((me == 3) & (quarter < 3), 32, 16, j, first_used + 6 * 16 * j, 6)
     if 3 in phases:
-        for j in range(2):
-            take(me > 3, 0, 32, j, used + 6 * 32 * j, 6)
+        for j in range(4):
+            take(me > 3, 0, SHORT, j, used + 6 * SHORT * j, 6)
     if 4 in phases:
-        for j in range(8):
-            take((me == 7) & (quarter == 0), 32, 8, j, norm + j, 8)
+        for j in range(4):
+            take((me == 7) & (quarter == 0), 0, SHORT, 4 + j, norm + j, 4)
 
 
 def window_pieces(kind, row):
@@ -533,7 +575,7 @@
         for me in range(4, 8):
             at = row - USED_START[me]
             if 0 <= at < 256:
-                found.append((me, at // 64, at % 32, at % 64 // 32))
+                found.append((me, at // 64, 0, at % 64 // 16))
     return found
 
 SHARED_LANES = 1348
@@ -544,8 +586,8 @@
 def forward_kernel(lines, q_rows, count_ref, row_ref, shared_ref, own_patch_ref,
                    weight_ref, used_ref, norm_ref,
                    embed_ref, normed1_ref, qkv_ref, attended_ref, log_ref, resid_ref, normed2_ref,
-                   patches, proj, windows, *rest):
-    body, extra = rest[:2 + 14], rest[2 + 14:]
+                   patches, proj, windows, own_chunk, own_sem, *rest):
+    body, extra = rest[:4 + 14], rest[4 + 14:]
     corner, spot = Corner(), Lines(lines)
     barrier = pltpu.get_barrier_semaphore()
     for other in (corner.mate, corner.far):
@@ -554,9 +596,9 @@
     parts = lines // 2
     chunk = weight_ref.shape[0] // (2 * lines)
     size, inputs = own_patch_ref.shape
-    window = LineGather(spot, windows, corner.me * (2 * lines * WINDOW), WINDOW, 1, False, extra[0:6])
+    window = LineGather(spot, windows, corner.me * (2 * lines * WINDOW), WINDOW, 1, False, extra[0:6], SHORT)
     weights = LineGather(spot, weight_ref, 0, chunk, CHUNK_PIECES, True, extra[6:12])
-    spread = Gather(corner, windows, 2, extra[12:18])
+    spread = Gather(corner, windows, 2 * lines, extra[12:18], SHORT)
     given = Gather(corner, patches, 1, extra[18:24])
 
     patches[given.part(corner.me, 0)] = own_patch_ref[...]
@@ -573,37 +615,70 @@
 
     shared_walk(spot.me, corner.me, take)
     window.begin()
+    spread.start(spot.me)
     own = pl.multiple_of(spot.me * chunk, 16)
 
     @pl.when(spot.me < parts)
     def _():
         for row, rows, col, cols, at, at_col in qkv_places(1, chunk * 4 // 3, D * 3 // 4):
             for j in range(cols // 128):
-                weight_ref[pl.ds(pl.multiple_of(own + row, 16), rows), col + j * 128 : col + (j + 1) * 128] = row_ref[
+                own_chunk[row : row + rows, col + j * 128 : col + (j + 1) * 128] = row_ref[
                     pl.ds(6 * at + at_col // 128 + j, rows, 6)
                 ].astype(LOW)
 
     @pl.when(spot.me >= parts)
     def _():
         for j in range(8):
-            weight_ref[pl.ds(own, chunk), j * 128 : (j + 1) * 128] = row_ref[pl.ds(j, chunk, 8)].astype(LOW)
-
+            own_chunk[:, j * 128 : (j + 1) * 128] = row_ref[pl.ds(j, chunk, 8)].astype(LOW)
+
+    kept = pltpu.make_async_copy(own_chunk, weight_ref.at[pl.ds(own, chunk)], own_sem)
+    kept.start()
+    kept.wait()
     weights.begin()
-    for at in range(window.steps):
-        window.step(at)
-    for line in range(lines):
-        window.wait_crossed(line)
-    for piece in range(2):
-        spread.start(piece)
+
+    def passed(stage, act):
+        if stage == 0:
+            act(spot.me, None)
+            act(spot.line * 2 + 1 - spot.side, spot.line)
+            return
+        for near in (True, False):
+            for there, line in (
+                (stage - 1 < spot.line, stage - 1),
+                (stage - 1 < lines - 1 - spot.line, spot.line + stage),
+            ):
+
+                @pl.when(there)
+                def _():
+                    act(line * 2 + (spot.side if near else 1 - spot.side), None if near else line)
+
+    def send_on(owner, line):
+        if line is not None:
+            window.wait_crossed(line)
+        spread.start(owner)
+
+    def relay_on(owner, line):
+        spread.relay(owner)
+
+    window.wait_crossed(spot.line)
+    spread.start(spot.line * 2 + 1 - spot.side)
+    window.step(0)
+    passed(1, send_on)
+    window.step(1)
+    passed(2, send_on)
+    window.step(2)
+    weights.follow()
+    weights.step(0)
+    passed(3, send_on)
+    weights.step(1)
     given.relay(0)
-    for at in range(2):
-        weights.step(at)
-    spread.relay(0)
+    passed(0, relay_on)
     weights.step(2)
-    spread.relay(1)
+    passed(1, relay_on)
     weights.step(3)
+    passed(2, relay_on)
+    passed(3, relay_on)
+    spread.finish()
     given.finish()
-    spread.finish()
 
     def source(me, quarter, row, rows, j):
         start = (quarter * 2 * lines + me) * WINDOW + row
@@ -613,23 +688,38 @@
         proj[row : row + 16] = sum(source(me, t, at, 16, j) for me, t, at, j in window_pieces(0, row))
     for row in range(0, used_ref.shape[0], 16):
         used_ref[row : row + 16] = sum(source(me, t, at, 16, j) for me, t, at, j in window_pieces(1, row))
-    norm_ref[...] = source(2 * lines - 1, 0, 32, 8, None).astype(WIDE)
+    ends = source(2 * lines - 1, 0, 0, SHORT, None)[:, D // 2 :].astype(WIDE)
+    norm_ref[...] = jnp.zeros_like(norm_ref)
+    for row in range(8):
+        norm_ref[row // 2 : row // 2 + 1, row % 2 * D // 2 : (row % 2 + 1) * D // 2] = ends[row : row + 1]
 
     def progress(place, at=None):
+        if place == "embed":
+
+            @pl.when(at == 2)
+            def _():
+                weights.step(4)
+
         if place == "weights":
+            weights.step(5)
             weights.wait_crossed(0)
         if place == "turn":
-            @pl.when(at >= 2)
-            def _():
-                weights.step(at + 2)
+
+            @pl.when(lax.rem(at, 2) == 1)
+            def _():
+                weights.step(6 + at // 2)
+
+        if place == "give":
+
+            @pl.when(at < 3)
+            def _():
+                weights.step(9 + at)
+
         if place == "out":
             weights.wait_crossed(1)
-        if place == "land":
-            weights.step(8 + at)
 
     attend_body(parts, q_rows, corner, progress, count_ref, patches, proj, norm_ref,
-                weight_ref.at[pl.ds(0, D * 3 // 4)], weight_ref.at[pl.ds(D * 3 // 4, D // 4)],
-                embed_ref, normed1_ref, qkv_ref, attended_ref, log_ref, resid_ref, normed2_ref, *body)
+                weight_ref, embed_ref, normed1_ref, qkv_ref, attended_ref, log_ref, resid_ref, normed2_ref, *body)
     for line in range(2, lines):
         weights.wait_crossed(line)
     weights.close()
@@ -655,19 +745,23 @@
             shape((length, width), LOW),
         ),
         in_specs=[pl.BlockSpec(memory_space=pltpu.SMEM)] + [VMEM] * 3,
-        out_specs=(VMEM,) * 10,
+        out_specs=(HBM,) + (VMEM,) * 9,
         scratch_shapes=[
             pltpu.VMEM((length, inputs), LOW),
             pltpu.VMEM((inputs, width), LOW),
             pltpu.VMEM((8 * lines * WINDOW, width), LOW),
+            pltpu.VMEM((3 * D // (2 * lines), width), LOW),
+            pltpu.SemaphoreType.DMA(()),
             pltpu.VMEM((width, 3 * local), LOW),
             pltpu.VMEM((size, width), WIDE),
+            pltpu.VMEM((4 * local, width), LOW),
+            pltpu.SemaphoreType.DMA((2,)),
         ]
         + Scatter.scratch(size, width, PIECES)
         + Gather.scratch(PIECES)
         + LineGather.scratch(lines, 1)
         + LineGather.scratch(lines, CHUNK_PIECES)
-        + Gather.scratch(2)
+        + Gather.scratch(2 * lines)
         + Gather.scratch(1),
         compiler_params=pltpu.CompilerParams(
             collective_id=collective_id, has_side_effects=True, vmem_limit_bytes=63 * 2**20
@@ -675,12 +769,37 @@
     )(count, row_lanes, shared_lanes, own_patches)
 
 
-def mlp_kernel(normed2_ref, up_ref, down_ref, resid1_ref, cols_ref, hidden_ref, active_ref, low_ref, table_ref, term, *comm):
+class Moves:
+    def __init__(self, sems, *pairs):
+        self.copies = [pltpu.make_async_copy(src, dst, sems.at[at]) for at, (src, dst) in enumerate(pairs)]
+
+    def start(self, *which):
+        for at in which or range(len(self.copies)):
+            self.copies[at].start()
+
+    def wait(self, *which):
+        for at in which or range(len(self.copies)):
+            self.copies[at].wait()
+
+
+def mlp_kernel(normed2_ref, weight_ref, resid1_ref, cols_ref, hidden_out, active_out, low_ref, table_ref,
+               term, up_ref, down_ref, hidden_ref, active_ref, load_sem, hidden_sem, active_sem, *comm):
+    first, ff = up_ref.shape[0], down_ref.shape[0]
+    loads = Moves(load_sem, (weight_ref.at[pl.ds(first, first)], up_ref), (weight_ref.at[pl.ds(2 * first, ff)], down_ref))
+    loads.start()
     corner = Corner()
     corner.greet()
     scatter = Scatter(corner, PIECES, *comm[:8])
     gather = Gather(corner, table_ref, PIECES, comm[8:])
     size, width = resid1_ref.shape
+    loads.wait()
+
+    def stores(step):
+        here = rows_of(corner.block(step), size)
+        return (
+            pltpu.make_async_copy(hidden_ref.at[here], hidden_out.at[here], hidden_sem.at[step]),
+            pltpu.make_async_copy(active_ref.at[here], active_out.at[here], active_sem.at[step]),
+        )
 
     @pl.loop(0, 4)
     def _(step):
@@ -692,6 +811,8 @@
             active_ref[here, cols] = (0.5 * hidden * (1.0 + lax.erf(hidden * ROOT_HALF))).astype(LOW)
 
         column_loop(up_ref.shape[1], columns)
+        for copy in stores(step):
+            copy.start()
         column_loop(width, lambda cols: term.__setitem__((slice(None), cols), dot(active_ref[here], down_ref[:, cols])))
         scatter.step(step, term)
 
@@ -704,11 +825,14 @@
         gather.relay(piece)
     gather.finish()
     scatter.close()
-
-
-def mlp(normed2, up_proj, down_proj, resid1, used_cols, collective_id):
+    for step in range(4):
+        for copy in stores(step):
+            copy.wait()
+
+
+def mlp(normed2, weights, resid1, used_cols, collective_id):
     length, size, width = normed2.shape[0], resid1.shape[0], resid1.shape[1]
-    hidden = up_proj.shape[1]
+    hidden = FF // 4
     shape = jax.ShapeDtypeStruct
     return pl.pallas_call(
         mlp_kernel,
@@ -718,20 +842,40 @@
             shape((size, width), LOW),
             shape((length, used_cols.shape[1]), LOW),
         ),
-        in_specs=[VMEM] * 5,
-        out_specs=(VMEM,) * 4,
-        scratch_shapes=[pltpu.VMEM((size, width), WIDE)]
+        in_specs=[VMEM, HBM, VMEM, VMEM],
+        out_specs=(HBM, HBM, VMEM, VMEM),
+        scratch_shapes=[
+            pltpu.VMEM((size, width), WIDE),
+            pltpu.VMEM((width, hidden), LOW),
+            pltpu.VMEM((hidden, width), LOW),
+            pltpu.VMEM((length, hidden), WIDE),
+            pltpu.VMEM((length, hidden), LOW),
+            pltpu.SemaphoreType.DMA((2,)),
+            pltpu.SemaphoreType.DMA((4,)),
+            pltpu.SemaphoreType.DMA((4,)),
+        ]
         + Scatter.scratch(size, width, PIECES)
         + Gather.scratch(PIECES),
         compiler_params=pltpu.CompilerParams(
             collective_id=collective_id, has_side_effects=True, vmem_limit_bytes=62 * 2**20
         ),
-    )(normed2, up_proj, down_proj, resid1, used_cols)
-
-
-def mlp_back_kernel(table_ref, cols_ref, low_ref, active_ref, hidden_ref, normed2_ref, up_ref, down_ref, resid1_ref, norm_ref,
-                    unpatch_ref, grad_ref, resid_grad_ref, branch_ref, gain_ref,
-                    gauss, down_in, hidden_grad, term, tail, *comm):
+    )(normed2, weights, resid1, used_cols)
+
+
+def mlp_back_kernel(table_ref, cols_ref, low_ref, active_in, hidden_in, normed2_in, weight_ref, resid1_ref, norm_ref,
+                    unpatch_ref, grad_out, resid_grad_ref, branch_ref, gain_ref,
+                    gauss, down_in, hidden_grad, term, tail, active_ref, hidden_ref, normed2_ref, up_ref, down_ref, grad_ref,
+                    load_sem, store_sem, *comm):
+    first = up_ref.shape[0]
+    loads = Moves(
+        load_sem,
+        (weight_ref.at[pl.ds(2 * first, down_ref.shape[0])], down_ref),
+        (hidden_in, hidden_ref),
+        (weight_ref.at[pl.ds(first, first)], up_ref),
+        (normed2_in, normed2_ref),
+        (active_in, active_ref),
+    )
+    loads.start()
     corner = Corner()
     corner.greet()
     small = Scatter(corner, 1, *comm[:8])
@@ -758,6 +902,7 @@
     spread.relay(0)
     spread.finish()
     small.close()
+    loads.wait(0, 1, 2)
 
     @pl.loop(0, 4)
     def _(step):
@@ -783,15 +928,23 @@
         column_loop(width, back)
         scatter.step(step, term)
 
+    def store(tile):
+        part = pl.ds(pl.multiple_of(tile * TILE, TILE), TILE)
+        return pltpu.make_async_copy(grad_ref.at[part], grad_out.at[part], store_sem.at[tile])
+
+    loads.wait(3, 4)
+
     @pl.loop(0, width // TILE)
     def _(tile):
         cols = pl.ds(pl.multiple_of(tile * TILE, TILE), TILE)
         grad_ref[cols, :] = dot(normed2_ref[:, cols], hidden_grad[...], TN)
+        store(tile).start()
 
     @pl.loop(0, ff // TILE)
     def _(tile):
         cols = pl.ds(pl.multiple_of(tile * TILE, TILE), TILE)
         grad_ref[pl.ds(pl.multiple_of(width + tile * TILE, TILE), TILE), :] = dot(active_ref[:, cols], down_in[...], TN)
+        store(width // TILE + tile).start()
 
     gain_sum, bias_sum = jnp.zeros((1, width), WIDE), jnp.zeros((1, width), WIDE)
     for piece in range(PIECES):
@@ -811,10 +964,14 @@
     gather.finish()
     scatter.close()
 
-
-def mlp_back(table_grad, used_cols, low, active, hidden, normed2, up_proj, down_proj, resid1, norm, collective_id):
+    @pl.loop(0, (width + ff) // TILE)
+    def _(tile):
+        store(tile).wait()
+
+
+def mlp_back(table_grad, used_cols, low, active, hidden, normed2, weights, resid1, norm, collective_id):
     length, size, width = normed2.shape[0], resid1.shape[0], resid1.shape[1]
-    ff, used = up_proj.shape[1], used_cols.shape[1]
+    ff, used = hidden.shape[1], used_cols.shape[1]
     shape = jax.ShapeDtypeStruct
     return pl.pallas_call(
         mlp_back_kernel,
@@ -825,14 +982,22 @@
             shape((length, width), LOW),
             shape((2, width), WIDE),
         ),
-        in_specs=[VMEM] * 10,
-        out_specs=(VMEM,) * 5,
+        in_specs=[VMEM] * 3 + [HBM] * 4 + [VMEM] * 2,
+        out_specs=(VMEM, HBM, VMEM, VMEM, VMEM),
         scratch_shapes=[
             pltpu.VMEM((length, used), LOW),
             pltpu.VMEM((length, width), LOW),
             pltpu.VMEM((length, ff), LOW),
             pltpu.VMEM((size, width), WIDE),
             pltpu.VMEM((size, used), WIDE),
+            pltpu.VMEM((length, ff), LOW),
+            pltpu.VMEM((length, ff), WIDE),
+            pltpu.VMEM((length, width), LOW),
+            pltpu.VMEM((width, ff), LOW),
+            pltpu.VMEM((ff, width), LOW),
+            pltpu.VMEM((width + ff, width), WIDE),
+            pltpu.SemaphoreType.DMA((5,)),
+            pltpu.SemaphoreType.DMA(((width + ff) // TILE,)),
         ]
         + Scatter.scratch(size, used, 1)
         + Gather.scratch(1)
@@ -841,17 +1006,22 @@
         compiler_params=pltpu.CompilerParams(
             collective_id=collective_id, has_side_effects=True, vmem_limit_bytes=63 * 2**20
         ),
-    )(table_grad, used_cols, low, active, hidden, normed2, up_proj, down_proj, resid1, norm)
-
-
-def attend_back_kernel(parts, q_rows, count_ref, branch_ref, out_ref, qkv_ref, log_ref, packed_ref, attended_ref, normed1_ref, embed_ref,
+    )(table_grad, used_cols, low, active, hidden, normed2, weights, resid1, norm)
+
+
+def attend_back_kernel(parts, q_rows, count_ref, branch_ref, weight_ref, qkv_ref, log_ref, attended_ref, normed1_in, embed_ref,
                        resid_grad_ref, norm_ref, patch_ref, grad_ref, patch_grad_ref, gain_ref,
-                       qkv_proj, attended_grad, qkv_grad, key_grad, value_grad, full_grad, term, embed_grad, *comm):
+                       qkv_proj, attended_grad, qkv_grad, key_grad, value_grad, full_grad, term, embed_grad,
+                       held, normed1_ref, load_sem, *comm):
+    loads = Moves(load_sem, (weight_ref.at[pl.ds(0, held.shape[0])], held), (normed1_in, normed1_ref))
+    loads.start()
     corner = Corner()
     corner.greet()
     scatter = Scatter(corner, PIECES, *comm)
     size, width = embed_ref.shape
     length, local = attended_ref.shape
+    packed_ref, out_ref = held.at[pl.ds(0, 3 * local)], held.at[pl.ds(3 * local, local)]
+    loads.wait(0)
     unpack_into(qkv_proj, packed_ref, parts)
 
     @pl.loop(0, 4)
@@ -903,6 +1073,7 @@
         scatter.step(step, term)
 
     grad_ref[grad_ref.shape[0] - local :, :] = dot(attended_ref[...], branch_ref[...], TN)
+    loads.wait(1)
 
     @pl.loop(0, width // TILE)
     def _(tile):
@@ -925,7 +1096,7 @@
     scatter.close()
 
 
-def attend_back(count, branch, out_proj, qkv, log_total, packed, attended, normed1, embed, resid_grad, norm, patches, parts, collective_id):
+def attend_back(count, branch, weights, qkv, log_total, attended, normed1, embed, resid_grad, norm, patches, parts, collective_id):
     length, local = attended.shape
     size, width = embed.shape
     shape = jax.ShapeDtypeStruct
@@ -936,7 +1107,7 @@
             shape((patches.shape[1], width), WIDE),
             shape((2, width), WIDE),
         ),
-        in_specs=[pl.BlockSpec(memory_space=pltpu.SMEM)] + [VMEM] * 11,
+        in_specs=[pl.BlockSpec(memory_space=pltpu.SMEM), VMEM, HBM] + [VMEM] * 3 + [HBM] + [VMEM] * 4,
         out_specs=(VMEM,) * 3,
         scratch_shapes=[
             pltpu.VMEM((width, 3 * local), LOW),
@@ -947,12 +1118,15 @@
             pltpu.VMEM((width, 3 * local), WIDE),
             pltpu.VMEM((size, width), WIDE),
             pltpu.VMEM((size, width), LOW),
+            pltpu.VMEM((4 * local, width), LOW),
+            pltpu.VMEM((length, width), LOW),
+            pltpu.SemaphoreType.DMA((2,)),
         ]
         + Scatter.scratch(size, width, PIECES),
         compiler_params=pltpu.CompilerParams(
             collective_id=collective_id, has_side_effects=True, vmem_limit_bytes=62 * 2**20
         ),
-    )(count, branch, out_proj, qkv, log_total, packed, attended, normed1, embed, resid_grad, norm, patches)
+    )(count, branch, weights, qkv, log_total, attended, normed1, embed, resid_grad, norm, patches)
 
 
 class LineSum:
@@ -1222,15 +1396,19 @@
 
         for owner in range(4, 8):
             at = owner * WINDOW
-            for j in range(2):
-
-                @pl.when((block < 3) | (owner < 7) | (j < 1))
+            for j in range(4):
+
+                @pl.when((block < 3) | (owner < 7) | (j < 2))
                 def _():
-                    term[at : at + 32, j * 128 : (j + 1) * 128] = used_ref[rows_at(USED_START[owner] + block * 64 + 32 * j, 32)]
+                    term[at : at + SHORT, j * 128 : (j + 1) * 128] = used_ref[
+                        rows_at(USED_START[owner] + block * 64 + SHORT * j, SHORT)
+                    ]
 
         @pl.when(block == 0)
         def _():
-            term[7 * WINDOW + 32 : 7 * WINDOW + 40] = gain_ref[...]
+            for row in range(8):
+                at = 7 * WINDOW + row
+                term[at : at + 1, width // 2 :] = gain_ref[row // 2 : row // 2 + 1, row % 2 * width // 2 : (row % 2 + 1) * width // 2]
 
         scatter.step(step, term)
 
@@ -1729,7 +1907,6 @@
     my_dp = lax.axis_index("dp")
     count_dp = lax.axis_size("dp")
     local_width = D // groups
-    local_hidden = FF // groups
     qkv_parts = count_dp // 4
     share_rows = row_master.shape[1] // D
     own_patches = patches[0]
@@ -1740,7 +1917,6 @@
         weights, used_cols, norm, embed, normed1, qkv, attended, log_total, resid1, normed2 = forward(
             view_counts, row_master.reshape(-1, 128), shared_lanes, own_patches, count_dp // 2, 7
         )
-        packed_qkv, out_proj, up_proj, down_proj = jnp.split(weights, (3 * local_width, D, D + local_hidden))
     else:
         own_row = row_master[0].astype(jnp.bfloat16)
         own_tiles = jnp.where(
@@ -1754,30 +1930,23 @@
         lead = own_shared.shape[0]
         own_shared = pad_first(own_shared, 0, 2048 // own_shared[0].size)
         shared_weights = lax.all_gather(own_shared, "dp", axis=0, tiled=False)[:, :lead].reshape(-1, 128)
-        qkv_rows = 3 * local_width
-        out_end = qkv_rows + local_width
-        up_end = out_end + local_hidden
         patch_rows = PIN * D // 128
         unpatch_rows = D * POUT // 128
-        packed_qkv = weights[:qkv_rows]
-        out_proj = weights[qkv_rows:out_end]
-        up_proj = weights[out_end:up_end]
-        down_proj = weights[up_end:]
         norm = shared_weights[patch_rows + unpatch_rows :].reshape(4, D).astype(jnp.float32)
         patch_proj = shared_weights[:patch_rows].reshape(PIN, D)
         used_cols = shared_weights[patch_rows : patch_rows + unpatch_rows].reshape(D, POUT // 128, 128)[:, 0]
         all_patches = lax.all_gather(own_patches, "tensor", axis=0, tiled=True)
         embed, normed1, qkv, attended, log_total, resid1, normed2 = attend(
-            view_counts, all_patches, patch_proj, norm, packed_qkv, out_proj, qkv_parts, 3
+            view_counts, all_patches, patch_proj, norm, weights, qkv_parts, 3
         )
-    hidden, active, resid2_low, gauss_table = mlp(normed2, up_proj, down_proj, resid1, used_cols, 4)
+    hidden, active, resid2_low, gauss_table = mlp(normed2, weights, resid1, used_cols, 4)
     loss_tile, table_grad = render(gauss_table, splat_index[0], splat_dist[0], alpha_label, PATCH * PATCH)
     loss_part = loss_tile[0, 0]
     unpatch_used, late_grad, resid_grad, branch, gain2_grad = mlp_back(
-        table_grad, used_cols, resid2_low, active, hidden, normed2, up_proj, down_proj, resid1, norm, 5
+        table_grad, used_cols, resid2_low, active, hidden, normed2, weights, resid1, norm, 5
     )
     early_grad, patch_grad, gain1_grad = attend_back(
-        view_counts, branch, out_proj, qkv, log_total, packed_qkv, attended, normed1, embed, resid_grad, norm, own_patches, qkv_parts, 6
+        view_counts, branch, weights, qkv, log_total, attended, normed1, embed, resid_grad, norm, own_patches, qkv_parts, 6
     )
     gain_grad = jnp.concatenate([gain1_grad, gain2_grad], 0)
     if count_dp == 8:

time: 538 us -> 506 us (0.941)
  Pallas kernels: 507 us -> 484 us
  local copies, waits for them, and re-layouts: 16.9 us -> 7.78 us
    pallas_call x1, Pallas kernels: 136 us -> 124 us  [forward(): pl.pallas_call(partial(forward_kernel, lines, 256), out_shape=(shape((3 *...]
    split x3 -> x0, local copies, waits for them, and re-layouts: 9.16 us -> none  [per_device(): jnp.split(weights, (3 * local_width, D, D + local_hidden))]
    pallas_call x1, Pallas kernels: 67.7 us -> 60.6 us  [mlp_back(): pl.pallas_call(mlp_back_kernel, out_shape=(shape((width, used), WIDE), sh...]
where the time goes in v5:
time: 506 us; the launch traced here: 505 us
  Pallas kernels  484 us (96%)
  between operations  7.95 us (2%)
  local copies, waits for them, and re-layouts  7.78 us (2%)
  other arithmetic  5.47 us (1%)
    pallas_call x1, Pallas kernels, share(): pl.pallas_call(partial(share_kernel, lines), out_shape=(shape((chunk * wi...  143 us
    pallas_call x1, Pallas kernels, forward(): pl.pallas_call(partial(forward_kernel, lines, 256), out_shape=(shape((3 *...  124 us
    pallas_call x1, Pallas kernels, attend_back(): pl.pallas_call(partial(attend_back_kernel, parts, 256), out_shape=(shape(...  63.7 us
    pallas_call x1, Pallas kernels, mlp_back(): pl.pallas_call(mlp_back_kernel, out_shape=(shape((width, used), WIDE), sh...  60.6 us
    pallas_call x1, Pallas kernels, render(): pl.pallas_call(partial(render_kernel, area, wide, block, split), out_shap...  49.3 us
    pallas_call x1, Pallas kernels, mlp(): pl.pallas_call(mlp_kernel, out_shape=(shape((length, hidden), WIDE), shap...  35.9 us

profile of v5, /device:TPU:0, one launch (start us, length us, event | category | flops | bytes accessed | tf_op | source)
XLA Modules:
  0.0 505.4 jit_solution(11640006871631024417)
XLA Ops:
  0.6 2.0 copy.26
  3.3 2.0 pad.8.shared_ref
  5.3 123.7 %shard_map.229 = (bf16[3072,1024]{1,0:T(8,128)(2,1)}, bf16[1024,128]{1,0:T(8,128)(2,1)}, f32[8,1024]{1,0:T(8,128)}, f32[384,1024]{1,0:T(8,128)}, bf16[1536,1024]...) custom-call(s32[1]{0:T(128)S(6)} %copy.27.count_ref, ...), custom_call_target="tpu_custom_call" | custom-call | tf_op jit(solution)/shard_map/pallas_call | solution.py:733
  129.1 0.0 copy-start.2
  129.1 0.0 copy-start.3
  129.1 0.0 copy-start.4
  129.1 35.9 %shard_map.230 = (f32[1536,1024]{1,0:T(8,128)}, bf16[1536,1024]{1,0:T(8,128)(2,1)}, bf16[384,1024]{1,0:T(8,128)(2,1)}, bf16[1536,128]{1,0:T(8,128)(2,1)}) custom-call(bf16[1536,1024]{1,0:T(8,128)(2,1)} %get-tuple-element.44.normed2_ref.normed2_in, bf16[3072,1024]{1,0:T(8,128)(2,1)} %get-tuple-element.45.weight_ref, ...), custom_call_target="tpu_custom_call" | custom-call | tf_op jit(solution)/shard_map/pallas_call | solution.py:837
  165.0 0.0 copy-done.2
  165.0 1.0 copy-done
  166.0 49.3 %shard_map.231 = (f32[8,128]{1,0:T(8,128)S(1)}, bf16[1536,128]{1,0:T(8,128)(2,1)S(1)}) custom-call(bf16[1536,128]{1,0:T(8,128)(2,1)S(1)} %copy-done, s32[4,6144]{1,0:T(4,128)S(1)} %bitcast.20, s32[4,6144]{1,0:T(4,128)S(1)} %bitcast.21, s32[1,6144]{1,0:T(1,128)S(1)} %copy-done.2), custom_call_target="tpu_custom_call" | custom-call | tf_op jit(solution)/shard_map/pallas_call | solution.py:1613
  215.3 0.0 copy-start.1
  215.3 0.7 copy-done.1
  216.1 0.6 copy-done.5
  216.7 60.6 %shard_map.232 = (f32[1024,128]{1,0:T(8,128)}, f32[2048,1024]{1,0:T(8,128)}, f32[384,1024]{1,0:T(8,128)}, bf16[1536,1024]{1,0:T(8,128)(2,1)}, f32[2,1024]{1,0:T(2,128)}) custom-call(bf16[1536,128]{1,0:T(8,128)(2,1)} %copy-done.1, bf16[1024,128]{1,0:T(8,128)(2,1)} %get-tuple-element.47.cols_ref, bf16[384,1024]{1,0:T(8,128)(2,1)} %get-tuple-element.50.low_ref, ...), custom_call_target="tpu_custom_call" | custom-call | tf_op jit(solution)/shard_map/pallas_call | solution.py:976
  277.3 0.0 copy-start.9
  277.3 63.7 %shard_map.233 = (f32[1024,1024]{1,0:T(8,128)}, f32[576,1024]{1,0:T(8,128)}, f32[2,1024]{1,0:T(2,128)}) custom-call(s32[1]{0:T(128)S(6)} %copy.27.count_ref, bf16[1536,1024]{1,0:T(8,128)(2,1)} %get-tuple-element.54.branch_ref, bf16[3072,1024]{1,0:T(8,128)(2,1)} %get-tuple-element.45.weight_ref, bf16[1536,768]{1,0:T(8,128)(2,1)} %get-tuple-element.55.qkv_ref, ...), custom_call_target="tpu_custom_call" | custom-call | tf_op jit(solution)/shard_map/pallas_call | solution.py:1103
  341.0 1.3 select_maximum_fusion.gain_ref
  342.3 142.7 %shard_map.234 = (f32[3072,128]{1,0:T(8,128)}, f32[1616,128]{1,0:T(8,128)}, f32[8,128]{1,0:T(8,128)}) custom-call(f32[1024,1024]{1,0:T(8,128)} %get-tuple-element.61.early_ref, f32[2048,1024]{1,0:T(8,128)} %get-tuple-element.62.late_ref, f32[576,1024]{1,0:T(8,128)} %get-tuple-element.63.patch_ref, f32[1024,128]{1,0:T(8,128)} %get-tuple-element.64.used_ref, ...), custom_call_target="tpu_custom_call" | custom-call | tf_op jit(solution)/shard_map/pallas_call | solution.py:1512
  485.0 1.4 fusion.5
  489.3 0.0 copy-start.8
  489.3 3.1 fusion.2
  492.4 0.0 copy-done.8
  492.4 1.0 multiply_add_fusion
  493.4 8.4 %shard_map.235 = (f32[1,393216]{1,0:T(1,128)}, f32[1,393216]{1,0:T(1,128)}, f32[1,393216]{1,0:T(1,128)}, f32[1,393216]{1,0:T(1,128)}, bf16[1,393216]{1,0:T(2,128)(2,1)}) custom-call(f32[8,128]{1,0:T(8,128)} %get-tuple-element.68.total_ref, s32[1]{0:T(128)S(6)} %copy.28.count_ref, f32[1,393216]{1,0:T(1,128)} %bitcast.26, f32[1,393216]{1,0:T(1,128)} %refs_1_.1, ...), custom_call_target="tpu_custom_call" | custom-call | tf_op jit(solution)/shard_map/pallas_call | solution.py:1881
  (9 shorter events, 0.0 us)
Async XLA Ops:
  129.1 35.9 %copy-start.2 = (s32[1,6144]{1,0:T(1,128)S(1)}, s32[1,6144]{1,0:T(1,128)}, u32[]{:S(2)}) copy-start(s32[1,6144]{1,0:T(1,128)} %label_ref.3) | copy-start | bytes 73732
  129.1 35.9 %copy-start.3 = (s32[1,4,6144]{2,1,0:T(4,128)S(1)}, s32[1,4,6144]{2,1,0:T(4,128)}, u32[]{:S(2)}) copy-start(s32[1,4,6144]{2,1,0:T(4,128)} %param.16) | copy-start | bytes 294916
  129.1 35.9 %copy-start.4 = (s32[1,4,6144]{2,1,0:T(4,128)S(1)}, s32[1,4,6144]{2,1,0:T(4,128)}, u32[]{:S(2)}) copy-start(s32[1,4,6144]{2,1,0:T(4,128)} %param.17) | copy-start | bytes 294916
  165.0 1.0 copy-start
  215.3 0.7 copy-start.1
  216.1 0.6 copy-start.5
  277.3 63.7 %copy-start.9 = (f32[2,1024]{1,0:T(2,128)S(1)}, f32[2,1024]{1,0:T(2,128)}, u32[]{:S(2)}) copy-start(f32[2,1024]{1,0:T(2,128)} %get-tuple-element.66) | copy-start | bytes 24580
  342.3 146.9 %copy-start.7 = (f32[172544]{0:T(1024)S(1)}, f32[172544]{0:T(1024)}, u32[]{:S(2)}) copy-start(f32[172544]{0:T(1024)} %param.24) | copy-start | bytes 2070532
  489.3 3.1 copy-start.8
  492.4 9.4 %copy-start.6 = (f32[172544]{0:T(1024)}, f32[172544]{0:T(1024)S(1)}, u32[]{:S(2)}) copy-start(f32[172544]{0:T(1024)S(1)} %get-tuple-element.77) | copy-start | bytes 2070532

commit v6 on v5

--- a/solution.py
+++ b/solution.py
@@ -526,6 +526,12 @@
 PADDED = 1616
 ROW_START = (0, 160, 336, 496)
 USED_START = (None, None, None, 0, 128, 352, 576, 800)
+
+
+def window_row(owner):
+    if isinstance(owner, int):
+        return owner * WINDOW if owner < 4 else 4 * WINDOW + (owner - 4) * SHORT
+    return jnp.minimum(owner, 4) * WINDOW + jnp.maximum(owner - 4, 0) * SHORT
 
 
 def shared_offsets(me, quarter):
@@ -862,10 +868,10 @@
     )(normed2, weights, resid1, used_cols)
 
 
-def mlp_back_kernel(table_ref, cols_ref, low_ref, active_in, hidden_in, normed2_in, weight_ref, resid1_ref, norm_ref,
-                    unpatch_ref, grad_out, resid_grad_ref, branch_ref, gain_ref,
+def mlp_back_kernel(table_ref, cols_ref, low_ref, active_in, hidden_in, normed2_in, weight_ref, resid1_ref, norm_ref, attended_ref,
+                    unpatch_ref, grad_out, rounded_out, resid_grad_ref, branch_ref, gain_ref,
                     gauss, down_in, hidden_grad, term, tail, active_ref, hidden_ref, normed2_ref, up_ref, down_ref, grad_ref,
-                    load_sem, store_sem, *comm):
+                    rounded_ref, load_sem, store_sem, *comm):
     first = up_ref.shape[0]
     loads = Moves(
         load_sem,
@@ -928,23 +934,32 @@
         column_loop(width, back)
         scatter.step(step, term)
 
-    def store(tile):
+    def stores(tile):
         part = pl.ds(pl.multiple_of(tile * TILE, TILE), TILE)
-        return pltpu.make_async_copy(grad_ref.at[part], grad_out.at[part], store_sem.at[tile])
+        return (
+            pltpu.make_async_copy(grad_ref.at[part], grad_out.at[part], store_sem.at[0, tile]),
+            pltpu.make_async_copy(rounded_ref.at[part], rounded_out.at[part], store_sem.at[1, tile]),
+        )
+
+    def keep(tile, value):
+        part = pl.ds(pl.multiple_of(tile * TILE, TILE), TILE)
+        grad_ref[part, :] = value
+        rounded_ref[part, :] = value.astype(LOW)
+        for copy in stores(tile):
+            copy.start()
 
     loads.wait(3, 4)
+    tiles = attended_ref.shape[1] // TILE
 
     @pl.loop(0, width // TILE)
     def _(tile):
         cols = pl.ds(pl.multiple_of(tile * TILE, TILE), TILE)
-        grad_ref[cols, :] = dot(normed2_ref[:, cols], hidden_grad[...], TN)
-        store(tile).start()
+        keep(tiles + tile, dot(normed2_ref[:, cols], hidden_grad[...], TN))
 
     @pl.loop(0, ff // TILE)
     def _(tile):
         cols = pl.ds(pl.multiple_of(tile * TILE, TILE), TILE)
-        grad_ref[pl.ds(pl.multiple_of(width + tile * TILE, TILE), TILE), :] = dot(active_ref[:, cols], down_in[...], TN)
-        store(width // TILE + tile).start()
+        keep(tiles + width // TILE + tile, dot(active_ref[:, cols], down_in[...], TN))
 
     gain_sum, bias_sum = jnp.zeros((1, width), WIDE), jnp.zeros((1, width), WIDE)
     for piece in range(PIECES):
@@ -964,26 +979,32 @@
     gather.finish()
     scatter.close()
 
-    @pl.loop(0, (width + ff) // TILE)
+    for tile in range(tiles):
+        keep(tile, dot(attended_ref[:, tile * TILE : (tile + 1) * TILE], branch_ref[...], TN))
+
+    @pl.loop(0, grad_ref.shape[0] // TILE)
     def _(tile):
-        store(tile).wait()
-
-
-def mlp_back(table_grad, used_cols, low, active, hidden, normed2, weights, resid1, norm, collective_id):
+        for copy in stores(tile):
+            copy.wait()
+
+
+def mlp_back(table_grad, used_cols, low, active, hidden, normed2, weights, resid1, norm, attended, collective_id):
     length, size, width = normed2.shape[0], resid1.shape[0], resid1.shape[1]
     ff, used = hidden.shape[1], used_cols.shape[1]
+    total = attended.shape[1] + width + ff
     shape = jax.ShapeDtypeStruct
     return pl.pallas_call(
         mlp_back_kernel,
         out_shape=(
             shape((width, used), WIDE),
-            shape((width + ff, width), WIDE),
+            shape((total, width), WIDE),
+            shape((total, width), LOW),
             shape((size, width), WIDE),
             shape((length, width), LOW),
             shape((2, width), WIDE),
         ),
-        in_specs=[VMEM] * 3 + [HBM] * 4 + [VMEM] * 2,
-        out_specs=(VMEM, HBM, VMEM, VMEM, VMEM),
+        in_specs=[VMEM] * 3 + [HBM] * 4 + [VMEM] * 3,
+        out_specs=(VMEM, HBM, HBM, VMEM, VMEM, VMEM),
         scratch_shapes=[
             pltpu.VMEM((length, used), LOW),
             pltpu.VMEM((length, width), LOW),
@@ -995,9 +1016,10 @@
             pltpu.VMEM((length, width), LOW),
             pltpu.VMEM((width, ff), LOW),
             pltpu.VMEM((ff, width), LOW),
-            pltpu.VMEM((width + ff, width), WIDE),
+            pltpu.VMEM((total, width), WIDE),
+            pltpu.VMEM((total, width), LOW),
             pltpu.SemaphoreType.DMA((5,)),
-            pltpu.SemaphoreType.DMA(((width + ff) // TILE,)),
+            pltpu.SemaphoreType.DMA((2, total // TILE)),
         ]
         + Scatter.scratch(size, used, 1)
         + Gather.scratch(1)
@@ -1006,20 +1028,257 @@
         compiler_params=pltpu.CompilerParams(
             collective_id=collective_id, has_side_effects=True, vmem_limit_bytes=63 * 2**20
         ),
-    )(table_grad, used_cols, low, active, hidden, normed2, weights, resid1, norm)
-
-
-def attend_back_kernel(parts, q_rows, count_ref, branch_ref, weight_ref, qkv_ref, log_ref, attended_ref, normed1_in, embed_ref,
-                       resid_grad_ref, norm_ref, patch_ref, grad_ref, patch_grad_ref, gain_ref,
-                       qkv_proj, attended_grad, qkv_grad, key_grad, value_grad, full_grad, term, embed_grad,
-                       held, normed1_ref, load_sem, *comm):
+    )(table_grad, used_cols, low, active, hidden, normed2, weights, resid1, norm, attended)
+
+
+class LineSum:
+    def __init__(self, spot, pieces, low, source, buffers, sems, first=0, turns=4, stored=None):
+        self.spot, self.pieces, self.low, self.source = spot, pieces, low, source
+        self.first, self.turns, self.stored = first, turns, stored
+        self.pair_out, self.pair_in, self.part, self.line_in, self.low_out, self.low_in = buffers
+        self.p_send, self.p_recv, self.l_send, self.up_recv, self.down_recv = sems
+        self.count = turns * pieces
+        self.rows = self.part.shape[0] // self.count
+
+    @staticmethod
+    def scratch(turns, rows, pieces, width, low, stored=False):
+        half = (turns * rows, width)
+        kept = half if low else (rows, width)
+        kind = LOW if low else WIDE
+        return [
+            pltpu.VMEM((16, 128) if stored else half, LOW),
+            pltpu.VMEM(half, LOW),
+            pltpu.VMEM(half, WIDE),
+            pltpu.VMEM(half, WIDE),
+            pltpu.VMEM(half if low else (16, 128), LOW),
+            pltpu.VMEM(kept, kind),
+        ] + [pltpu.SemaphoreType.DMA((turns * pieces,))] * 5
+
+    def target(self, step):
+        turn = lax.rem(step, self.turns)
+        if self.turns == 4:
+            odd = lax.rem(turn, 2)
+            return (1 - odd) * (3 - turn // 2) + odd * (turn // 2)
+        if self.turns == 3:
+            return self.first + 2 - 2 * jnp.minimum(turn, 1) + turn - jnp.minimum(turn, 1)
+        return self.first + turn
+
+    def stored_rows(self, step, side):
+        start = ((self.target(step) - self.first) * 2 + side) * self.pieces + step // self.turns
+        return pl.ds(pl.multiple_of(start * self.rows, 16), self.rows)
+
+    def slot(self, step):
+        return pl.ds(pl.multiple_of(step * self.rows, 16), self.rows)
+
+    def pair_copy(self, step):
+        slot = self.slot(step)
+        if self.stored:
+            sent = self.stored[1].at[self.stored_rows(step, 1 - self.spot.side)]
+            return remote(sent, self.pair_in.at[slot], self.p_send.at[step], self.p_recv.at[step], self.spot.pair)
+        return remote(self.pair_out.at[slot], self.pair_in.at[slot], self.p_send.at[step], self.p_recv.at[step], self.spot.pair)
+
+    def line_copy(self, step, to, recv):
+        slot = self.slot(step)
+        return remote(self.part.at[slot], self.line_in.at[slot], self.l_send.at[step], recv.at[step], to)
+
+    def low_copy(self, step, to, recv):
+        slot = self.slot(step)
+        return remote(self.low_out.at[slot], self.low_in.at[slot], self.l_send.at[step], recv.at[step], to)
+
+    def last_copy(self, step):
+        here = pl.ds(pl.multiple_of(step // self.turns * self.rows, 16), self.rows)
+        return remote(self.part.at[self.slot(step)], self.low_in.at[here], self.l_send.at[step], self.down_recv.at[step], self.spot.below)
+
+    def own_copy(self, step):
+        own = self.stored[0].at[self.stored_rows(step, self.spot.side)]
+        return pltpu.make_async_copy(own, self.part.at[self.slot(step)], self.stored[2].at[step])
+
+    def begin(self, step):
+        if self.stored:
+            self.pair_copy(step).start()
+            self.own_copy(step).start()
+            return
+        self.pair_out[self.slot(step)] = self.source(self.target(step), 1 - self.spot.side, step // self.turns).astype(LOW)
+        self.pair_copy(step).start()
+
+    def add(self, step, low):
+        slot = self.slot(step)
+        self.part[slot] += self.low_in[slot].astype(WIDE) if low else self.line_in[slot]
+
+    def travel(self, step, rising):
+        spot, slot = self.spot, self.slot(step)
+        to, recv = (spot.above, self.up_recv) if rising else (spot.below, self.down_recv)
+        last = spot.lines - 1
+        from_end = spot.line == (1 if rising else last - 1)
+        at_end = spot.line == (0 if rising else last)
+        target = self.target(step)
+        if self.low:
+
+            @pl.when(at_end)
+            def _():
+                self.low_out[slot] = self.part[slot].astype(LOW)
+                self.low_copy(step, to, recv).start()
+
+            @pl.when(from_end)
+            def _():
+                self.low_copy(step, to, recv).wait_recv()
+                self.add(step, True)
+
+            @pl.when(jnp.logical_not(at_end | from_end))
+            def _():
+                self.line_copy(step, to, recv).wait_recv()
+                self.add(step, False)
+
+            @pl.when(jnp.logical_not(at_end))
+            def _():
+                self.line_copy(step, to, recv).start()
+        else:
+
+            @pl.when(jnp.logical_not(at_end))
+            def _():
+                self.line_copy(step, to, recv).wait_recv()
+                self.add(step, False)
+
+            if rising:
+                self.line_copy(step, to, recv).start()
+            else:
+
+                @pl.when(target == spot.line - 1)
+                def _():
+                    self.last_copy(step).start()
+
+                @pl.when(target < spot.line - 1)
+                def _():
+                    self.line_copy(step, to, recv).start()
+
+    def advance(self, step):
+        spot = self.spot
+
+        @pl.when(step < self.count)
+        def _():
+            slot = self.slot(step)
+            self.pair_copy(step).wait_recv()
+            if self.stored:
+                self.own_copy(step).wait()
+                self.part[slot] += self.pair_in[slot].astype(WIDE)
+                return
+            own = self.source(self.target(step), spot.side, step // self.turns)
+            self.part[slot] = own + self.pair_in[slot].astype(WIDE)
+
+        rising = step - spot.line
+
+        @pl.when((rising >= 0) & (rising < self.count) & (self.target(rising) > spot.line))
+        def _():
+            self.travel(rising, True)
+
+        falling = step - (spot.lines - 1 - spot.line)
+
+        @pl.when((falling >= 0) & (falling < self.count) & (self.target(falling) < spot.line))
+        def _():
+            self.travel(falling, False)
+
+    def close(self, step, give):
+        spot, slot = self.spot, self.slot(step)
+        target = self.target(step)
+        last = spot.lines - 1
+        self.pair_copy(step).wait_send()
+
+        @pl.when(target > spot.line)
+        def _():
+            if self.low:
+
+                @pl.when(spot.line == 0)
+                def _():
+                    self.low_copy(step, spot.above, self.up_recv).wait_send()
+
+                @pl.when(spot.line > 0)
+                def _():
+                    self.line_copy(step, spot.above, self.up_recv).wait_send()
+            else:
+                self.line_copy(step, spot.above, self.up_recv).wait_send()
+
+        @pl.when(target < spot.line)
+        def _():
+            if self.low:
+
+                @pl.when(spot.line == last)
+                def _():
+                    self.low_copy(step, spot.below, self.down_recv).wait_send()
+
+                @pl.when(spot.line < last)
+                def _():
+                    self.line_copy(step, spot.below, self.down_recv).wait_send()
+            else:
+                self.line_copy(step, spot.below, self.down_recv).wait_send()
+
+        @pl.when(target == spot.line)
+        def _():
+            if self.low:
+
+                @pl.when(spot.line == 1)
+                def _():
+                    self.low_copy(step, spot.above, self.up_recv).wait_recv()
+                    self.add(step, True)
+
+                @pl.when(spot.line > 1)
+                def _():
+                    self.line_copy(step, spot.above, self.up_recv).wait_recv()
+                    self.add(step, False)
+
+                @pl.when(spot.line == last - 1)
+                def _():
+                    self.low_copy(step, spot.below, self.down_recv).wait_recv()
+                    self.add(step, True)
+
+                @pl.when(spot.line < last - 1)
+                def _():
+                    self.line_copy(step, spot.below, self.down_recv).wait_recv()
+                    self.add(step, False)
+            else:
+
+                @pl.when(spot.has_below)
+                def _():
+                    self.line_copy(step, spot.above, self.up_recv).wait_recv()
+                    self.add(step, False)
+
+                @pl.when(spot.has_above)
+                def _():
+                    self.last_copy(step).wait_recv()
+                    here = pl.ds(pl.multiple_of(step // self.turns * self.rows, 16), self.rows)
+                    self.part[slot] += self.low_in[here]
+
+            give(step // self.turns, self.part[slot])
+
+
+def attend_back_kernel(parts, q_rows, lines, count_ref, branch_ref, weight_ref, qkv_ref, log_ref, normed1_in, embed_ref,
+                       resid_grad_ref, norm_ref, *rest):
+    late_in, rest = (rest[:2], rest[2:]) if lines else ((), rest)
+    grad_ref, embed_grad, gain_ref = rest[:3]
+    own_late, rest = (rest[3], rest[4:]) if lines else (None, rest[3:])
+    qkv_proj, attended_grad, qkv_grad, key_grad, value_grad, term, held, normed1_ref, load_sem = rest[:9]
+    comm, late_comm = rest[9:17], rest[17:]
     loads = Moves(load_sem, (weight_ref.at[pl.ds(0, held.shape[0])], held), (normed1_in, normed1_ref))
     loads.start()
     corner = Corner()
-    corner.greet()
+    size, width = embed_ref.shape
+    length, local = qkv_ref.shape[0], qkv_ref.shape[1] // 3
+    if lines:
+        spot = Lines(lines)
+        barrier = pltpu.get_barrier_semaphore()
+        for other in (corner.mate, corner.far):
+            pl.semaphore_signal(barrier, inc=1, device_id={"tensor": other}, device_id_type=MESH)
+        pl.semaphore_wait(barrier, 2 + spot.signal(barrier))
+        late = LineSum(
+            spot, SUM_PIECES, True, None, late_comm[:6], late_comm[6:11], 1, lines - 1, late_in + (late_comm[11],)
+        )
+
+        @pl.loop(0, late.count)
+        def _(step):
+            late.begin(step)
+
+    else:
+        corner.greet()
     scatter = Scatter(corner, PIECES, *comm)
-    size, width = embed_ref.shape
-    length, local = attended_ref.shape
     packed_ref, out_ref = held.at[pl.ds(0, 3 * local)], held.at[pl.ds(3 * local, local)]
     loads.wait(0)
     unpack_into(qkv_proj, packed_ref, parts)
@@ -1058,6 +1317,9 @@
                 found.append(dot(score_grad, keyset))
                 key_grad[:, lanes] += dot(score_grad, own_query, TN)
             qkv_grad[here, lanes] = (jnp.where(left, found[0], found[1]) * (DH ** (-0.5))).astype(LOW)
+        if lines:
+            for at in range(2):
+                late.advance(2 * turn + at)
 
     qkv_grad[:, local : 2 * local] = key_grad[...].astype(LOW)
     qkv_grad[:, 2 * local :] = value_grad[...].astype(LOW)
@@ -1071,16 +1333,18 @@
 
         column_loop(width, columns)
         scatter.step(step, term)
-
-    grad_ref[grad_ref.shape[0] - local :, :] = dot(attended_ref[...], branch_ref[...], TN)
+        if lines:
+            late.advance(12 + step)
+
     loads.wait(1)
-
-    @pl.loop(0, width // TILE)
-    def _(tile):
-        cols = pl.ds(pl.multiple_of(tile * TILE, TILE), TILE)
-        full_grad[cols, :] = dot(normed1_ref[:, cols], qkv_grad[...], TN)
-
-    pack_from(grad_ref, full_grad, parts)
+    for tile in range(width // TILE):
+        value = dot(normed1_ref[:, tile * TILE : (tile + 1) * TILE], qkv_grad[...], TN)
+        for row, rows, col, cols, at, at_col in qkv_places(parts, width, 3 * local):
+            if at // TILE == tile:
+                at = at % TILE
+                grad_ref[row : row + rows, col : col + cols] = value[at : at + rows, at_col : at_col + cols]
+        if lines:
+            late.advance(16 + tile)
 
     gain_sum, bias_sum = jnp.zeros((1, width), WIDE), jnp.zeros((1, width), WIDE)
     for piece in range(PIECES):
@@ -1092,244 +1356,64 @@
         bias_sum += jnp.sum(grad, 0, keepdims=True)
     gain_ref[0:1] = gain_sum
     gain_ref[1:2] = bias_sum
-    patch_grad_ref[...] = dot(patch_ref[...], embed_grad[...], TN)
     scatter.close()
-
-
-def attend_back(count, branch, weights, qkv, log_total, attended, normed1, embed, resid_grad, norm, patches, parts, collective_id):
-    length, local = attended.shape
+    if lines:
+        for step in range(20, late.count + lines - 1):
+            late.advance(step)
+
+        def keep_rows(piece, value):
+            own_late[pl.ds(pl.multiple_of(piece * late.rows, 16), late.rows)] = value
+
+        @pl.loop(0, late.count)
+        def _(step):
+            late.close(step, keep_rows)
+
+
+def attend_back(count, branch, weights, qkv, log_total, normed1, embed, resid_grad, norm, late, parts, lines, collective_id):
+    length, local = qkv.shape[0], qkv.shape[1] // 3
     size, width = embed.shape
     shape = jax.ShapeDtypeStruct
+    chunk = 3 * width // (2 * lines) if lines else 0
     return pl.pallas_call(
-        partial(attend_back_kernel, parts, 256),
+        partial(attend_back_kernel, parts, 256, lines),
         out_shape=(
-            shape((4 * local, width), WIDE),
-            shape((patches.shape[1], width), WIDE),
+            shape((3 * local, width), WIDE),
+            shape((size, width), LOW),
             shape((2, width), WIDE),
-        ),
-        in_specs=[pl.BlockSpec(memory_space=pltpu.SMEM), VMEM, HBM] + [VMEM] * 3 + [HBM] + [VMEM] * 4,
-        out_specs=(VMEM,) * 3,
+        )
+        + ((shape((chunk, width), WIDE),) if lines else ()),
+        in_specs=[pl.BlockSpec(memory_space=pltpu.SMEM), VMEM, HBM, VMEM, VMEM, HBM, VMEM, VMEM, VMEM] + [HBM] * len(late),
+        out_specs=(VMEM,) * (4 if lines else 3),
         scratch_shapes=[
             pltpu.VMEM((width, 3 * local), LOW),
             pltpu.VMEM((length, local), LOW),
             pltpu.VMEM((length, 3 * local), LOW),
             pltpu.VMEM((length, local), WIDE),
             pltpu.VMEM((length, local), WIDE),
-            pltpu.VMEM((width, 3 * local), WIDE),
             pltpu.VMEM((size, width), WIDE),
-            pltpu.VMEM((size, width), LOW),
             pltpu.VMEM((4 * local, width), LOW),
             pltpu.VMEM((length, width), LOW),
             pltpu.SemaphoreType.DMA((2,)),
         ]
-        + Scatter.scratch(size, width, PIECES),
+        + Scatter.scratch(size, width, PIECES)
+        + (
+            LineSum.scratch(lines - 1, chunk, SUM_PIECES, width, True, True)
+            + [pltpu.SemaphoreType.DMA(((lines - 1) * SUM_PIECES,))]
+            if lines
+            else []
+        ),
         compiler_params=pltpu.CompilerParams(
-            collective_id=collective_id, has_side_effects=True, vmem_limit_bytes=62 * 2**20
+            collective_id=collective_id, has_side_effects=True, vmem_limit_bytes=63 * 2**20
         ),
-    )(count, branch, weights, qkv, log_total, attended, normed1, embed, resid_grad, norm, patches)
-
-
-class LineSum:
-    def __init__(self, spot, pieces, low, source, buffers, sems):
-        self.spot, self.pieces, self.low, self.source = spot, pieces, low, source
-        self.pair_out, self.pair_in, self.part, self.line_in, self.low_out, self.low_in = buffers
-        self.p_send, self.p_recv, self.l_send, self.up_recv, self.down_recv = sems
-        self.count = spot.lines * pieces
-        self.rows = self.part.shape[0] // self.count
-
-    @staticmethod
-    def scratch(lines, rows, pieces, width, low):
-        half = (lines * rows, width)
-        kept = half if low else (rows, width)
-        kind = LOW if low else WIDE
-        return [
-            pltpu.VMEM(half, LOW),
-            pltpu.VMEM(half, LOW),
-            pltpu.VMEM(half, WIDE),
-            pltpu.VMEM(half, WIDE),
-            pltpu.VMEM(half if low else (16, 128), LOW),
-            pltpu.VMEM(kept, kind),
-        ] + [pltpu.SemaphoreType.DMA((lines * pieces,))] * 5
-
-    def target(self, step):
-        turn = lax.rem(step, self.spot.lines)
-        odd = lax.rem(turn, 2)
-        return (1 - odd) * (self.spot.lines - 1 - turn // 2) + odd * (turn // 2)
-
-    def slot(self, step):
-        return pl.ds(pl.multiple_of(step * self.rows, 16), self.rows)
-
-    def pair_copy(self, step):
-        slot = self.slot(step)
-        return remote(self.pair_out.at[slot], self.pair_in.at[slot], self.p_send.at[step], self.p_recv.at[step], self.spot.pair)
-
-    def line_copy(self, step, to, recv):
-        slot = self.slot(step)
-        return remote(self.part.at[slot], self.line_in.at[slot], self.l_send.at[step], recv.at[step], to)
-
-    def low_copy(self, step, to, recv):
-        slot = self.slot(step)
-        return remote(self.low_out.at[slot], self.low_in.at[slot], self.l_send.at[step], recv.at[step], to)
-
-    def last_copy(self, step):
-        here = pl.ds(pl.multiple_of(step // self.spot.lines * self.rows, 16), self.rows)
-        return remote(self.part.at[self.slot(step)], self.low_in.at[here], self.l_send.at[step], self.down_recv.at[step], self.spot.below)
-
-    def begin(self, step):
-        self.pair_out[self.slot(step)] = self.source(self.target(step), 1 - self.spot.side, step // self.spot.lines).astype(LOW)
-        self.pair_copy(step).start()
-
-    def add(self, step, low):
-        slot = self.slot(step)
-        self.part[slot] += self.low_in[slot].astype(WIDE) if low else self.line_in[slot]
-
-    def travel(self, step, rising):
-        spot, slot = self.spot, self.slot(step)
-        to, recv = (spot.above, self.up_recv) if rising else (spot.below, self.down_recv)
-        last = spot.lines - 1
-        from_end = spot.line == (1 if rising else last - 1)
-        at_end = spot.line == (0 if rising else last)
-        target = self.target(step)
-        if self.low:
-
-            @pl.when(at_end)
-            def _():
-                self.low_out[slot] = self.part[slot].astype(LOW)
-                self.low_copy(step, to, recv).start()
-
-            @pl.when(from_end)
-            def _():
-                self.low_copy(step, to, recv).wait_recv()
-                self.add(step, True)
-
-            @pl.when(jnp.logical_not(at_end | from_end))
-            def _():
-                self.line_copy(step, to, recv).wait_recv()
-                self.add(step, False)
-
-            @pl.when(jnp.logical_not(at_end))
-            def _():
-                self.line_copy(step, to, recv).start()
-        else:
-
-            @pl.when(jnp.logical_not(at_end))
-            def _():
-                self.line_copy(step, to, recv).wait_recv()
-                self.add(step, False)
-
-            if rising:
-                self.line_copy(step, to, recv).start()
-            else:
-
-                @pl.when(target == spot.line - 1)
-                def _():
-                    self.last_copy(step).start()
-
-                @pl.when(target < spot.line - 1)
-                def _():
-                    self.line_copy(step, to, recv).start()
-
-    def advance(self, step):
-        spot = self.spot
-
-        @pl.when(step < self.count)
-        def _():
-            slot = self.slot(step)
-            self.pair_copy(step).wait_recv()
-            own = self.source(self.target(step), spot.side, step // spot.lines)
-            self.part[slot] = own + self.pair_in[slot].astype(WIDE)
-
-        rising = step - spot.line
-
-        @pl.when((rising >= 0) & (rising < self.count) & (self.target(rising) > spot.line))
-        def _():
-            self.travel(rising, True)
-
-        falling = step - (spot.lines - 1 - spot.line)
-
-        @pl.when((falling >= 0) & (falling < self.count) & (self.target(falling) < spot.line))
-        def _():
-            self.travel(falling, False)
-
-    def close(self, step, give):
-        spot, slot = self.spot, self.slot(step)
-        target = self.target(step)
-        last = spot.lines - 1
-        self.pair_copy(step).wait_send()
-
-        @pl.when(target > spot.line)
-        def _():
-            if self.low:
-
-                @pl.when(spot.line == 0)
-                def _():
-                    self.low_copy(step, spot.above, self.up_recv).wait_send()
-
-                @pl.when(spot.line > 0)
-                def _():
-                    self.line_copy(step, spot.above, self.up_recv).wait_send()
-            else:
-                self.line_copy(step, spot.above, self.up_recv).wait_send()
-
-        @pl.when(target < spot.line)
-        def _():
-            if self.low:
-
-                @pl.when(spot.line == last)
-                def _():
-                    self.low_copy(step, spot.below, self.down_recv).wait_send()
-
-                @pl.when(spot.line < last)
-                def _():
-                    self.line_copy(step, spot.below, self.down_recv).wait_send()
-            else:
-                self.line_copy(step, spot.below, self.down_recv).wait_send()
-
-        @pl.when(target == spot.line)
-        def _():
-            if self.low:
-
-                @pl.when(spot.line == 1)
-                def _():
-                    self.low_copy(step, spot.above, self.up_recv).wait_recv()
-                    self.add(step, True)
-
-                @pl.when(spot.line > 1)
-                def _():
-                    self.line_copy(step, spot.above, self.up_recv).wait_recv()
-                    self.add(step, False)
-
-                @pl.when(spot.line == last - 1)
-                def _():
-                    self.low_copy(step, spot.below, self.down_recv).wait_recv()
-                    self.add(step, True)
-
-                @pl.when(spot.line < last - 1)
-                def _():
-                    self.line_copy(step, spot.below, self.down_recv).wait_recv()
-                    self.add(step, False)
-            else:
-
-                @pl.when(spot.has_below)
-                def _():
-                    self.line_copy(step, spot.above, self.up_recv).wait_recv()
-                    self.add(step, False)
-
-                @pl.when(spot.has_above)
-                def _():
-                    self.last_copy(step).wait_recv()
-                    here = pl.ds(pl.multiple_of(step // spot.lines * self.rows, 16), self.rows)
-                    self.part[slot] += self.low_in[here]
-
-            give(step // spot.lines, self.part[slot])
+    )(count, branch, weights, qkv, log_total, normed1, embed, resid_grad, norm, *late)
 
 
 SUM_PIECES = 6
 
 
-def share_kernel(lines, early_ref, late_ref, patch_ref, used_ref, gain_ref, loss_ref, label_ref,
+def share_kernel(lines, early_ref, late_ref, embed_ref, own_patch_ref, used_ref, gain_ref, loss_ref, label_ref,
                  row_ref, shared_ref, total_ref,
-                 term, windows, mine, slots, rows_out, *comm):
+                 term, windows, mine, slots, rows_out, patch_ref, *comm):
     corner, spot = Corner(), Lines(lines)
     pairs, width = 2 * lines, early_ref.shape[1]
     quarters = 4
@@ -1346,21 +1430,16 @@
         pl.semaphore_signal(barrier, inc=1, device_id=peer(step), device_id_type=MESH)
 
     pl.semaphore_wait(barrier, count - 1)
-    chunk = (early_ref.shape[0] + late_ref.shape[0]) // pairs
+    chunk = late_ref.shape[0]
     rows = chunk // SUM_PIECES
-    edge = early_ref.shape[0]
 
     def weight_term(line, side, piece):
-        start = (line * 2 + side) * chunk + piece * rows
-        inside = start < edge
-        first = early_ref[pl.ds(pl.multiple_of(jnp.where(inside, start, 0), 8), rows)]
-        second = late_ref[pl.ds(pl.multiple_of(jnp.where(inside, 0, start - edge), 8), rows)]
-        return jnp.where(inside, first, second)
+        return early_ref[pl.ds(pl.multiple_of(side * chunk + piece * rows, 8), rows)]
 
     def shared_term(line, side, piece):
-        return mine[pl.ds(pl.multiple_of((line * 2 + side) * WINDOW, 16), WINDOW)]
-
-    weights = LineSum(spot, SUM_PIECES, True, weight_term, comm[0:6], comm[6:11])
+        return mine[pl.ds(pl.multiple_of(window_row(line * 2 + side), 16), WINDOW)]
+
+    weights = LineSum(spot, SUM_PIECES, True, weight_term, comm[0:6], comm[6:11], 0, 1)
     shared = LineSum(spot, 1, False, shared_term, comm[11:17], comm[17:22])
     scatter = Scatter(corner, PIECES, *comm[22:30])
     gather = Gather(corner, windows, 1, comm[30:36])
@@ -1370,6 +1449,8 @@
     def _(step):
         weights.begin(step)
 
+    patch_ref[...] = dot(own_patch_ref[...], embed_ref[...], TN)
+
     @pl.loop(0, 4)
     def _(step):
         block = corner.block(step)
@@ -1395,7 +1476,7 @@
                 term[at + 32 : at + 48, j * 128 : (j + 1) * 128] = used_ref[rows_at(block * 48 + 16 * j, 16)]
 
         for owner in range(4, 8):
-            at = owner * WINDOW
+            at = window_row(owner)
             for j in range(4):
 
                 @pl.when((block < 3) | (owner < 7) | (j < 2))
@@ -1407,25 +1488,19 @@
         @pl.when(block == 0)
         def _():
             for row in range(8):
-                at = 7 * WINDOW + row
+                at = window_row(7) + row
                 term[at : at + 1, width // 2 :] = gain_ref[row // 2 : row // 2 + 1, row % 2 * width // 2 : (row % 2 + 1) * width // 2]
 
         scatter.step(step, term)
 
-    @pl.loop(0, 8)
-    def _(step):
+    for step in range(2):
         weights.advance(step)
-
     for piece in range(PIECES):
         mine[scatter.part(piece)] = scatter.land(piece, term)
     for step in range(lines):
         shared.begin(step)
-
-    @pl.loop(8, weights.count + lines - 1)
-    def _(step):
-        weights.advance(step)
-
     for step in range(2 * lines - 1):
+        weights.advance(2 + step)
         shared.advance(step)
 
     def keep_window(piece, value):
@@ -1443,6 +1518,10 @@
     @pl.loop(0, weights.count)
     def _(step):
         weights.close(step, keep_rows)
+
+    @pl.when(spot.line > 0)
+    def _():
+        rows_out[...] = late_ref[...]
 
     gather.relay(0)
 
@@ -1504,26 +1583,28 @@
     scatter.close()
 
 
-def share(early, late, patch_grad, used_grad, gains, loss_tile, labels, lines, collective_id):
+def share(early, late, embed_grad, patches, used_grad, gains, loss_tile, labels, lines, collective_id):
     width = early.shape[1]
-    chunk = (early.shape[0] + late.shape[0]) // (2 * lines)
+    chunk = late.shape[0]
+    packed = 4 * WINDOW + (2 * lines - 4) * SHORT
     count = 8 * lines
     shape = jax.ShapeDtypeStruct
     return pl.pallas_call(
         partial(share_kernel, lines),
         out_shape=(shape((chunk * width // 128, 128), WIDE), shape((PADDED, 128), WIDE), shape((8, 128), WIDE)),
-        in_specs=[VMEM] * 7,
+        in_specs=[VMEM] * 8,
         out_specs=(VMEM,) * 3,
         scratch_shapes=[
-            pltpu.VMEM((2 * lines * WINDOW, width), WIDE),
+            pltpu.VMEM((packed, width), WIDE),
             pltpu.VMEM((4 * WINDOW, width), WIDE),
-            pltpu.VMEM((2 * lines * WINDOW, width), WIDE),
+            pltpu.VMEM((packed + WINDOW - SHORT, width), WIDE),
             pltpu.VMEM((count, 8, 128), WIDE),
             pltpu.VMEM((chunk, width), WIDE),
+            pltpu.VMEM((patches.shape[1], width), WIDE),
         ]
-        + LineSum.scratch(lines, chunk, SUM_PIECES, width, True)
+        + LineSum.scratch(1, chunk, SUM_PIECES, width, True)
         + LineSum.scratch(lines, WINDOW, 1, width, False)
-        + Scatter.scratch(2 * lines * WINDOW, width, PIECES)
+        + Scatter.scratch(packed, width, PIECES)
         + Gather.scratch(1)
         + [
             pltpu.SemaphoreType.DMA(()),
@@ -1533,7 +1614,7 @@
         compiler_params=pltpu.CompilerParams(
             collective_id=collective_id, has_side_effects=True, vmem_limit_bytes=63 * 2**20
         ),
-    )(early, late, patch_grad, used_grad, gains, loss_tile, labels)
+    )(early, late, embed_grad, patches, used_grad, gains, loss_tile, labels)
 
 
 def render_kernel(area, wide, block, split, table_ref, splat_ref, dist_ref, label_ref, loss_ref, grad_ref, flip, picked, hot, spread_grad):
@@ -1942,21 +2023,34 @@
     hidden, active, resid2_low, gauss_table = mlp(normed2, weights, resid1, used_cols, 4)
     loss_tile, table_grad = render(gauss_table, splat_index[0], splat_dist[0], alpha_label, PATCH * PATCH)
     loss_part = loss_tile[0, 0]
-    unpatch_used, late_grad, resid_grad, branch, gain2_grad = mlp_back(
-        table_grad, used_cols, resid2_low, active, hidden, normed2, weights, resid1, norm, 5
+    unpatch_used, late_grad, late_low, resid_grad, branch, gain2_grad = mlp_back(
+        table_grad, used_cols, resid2_low, active, hidden, normed2, weights, resid1, norm, attended, 5
     )
-    early_grad, patch_grad, gain1_grad = attend_back(
-        view_counts, branch, weights, qkv, log_total, attended, normed1, embed, resid_grad, norm, own_patches, qkv_parts, 6
+    early_grad, embed_grad, gain1_grad, *own_late = attend_back(
+        view_counts,
+        branch,
+        weights,
+        qkv,
+        log_total,
+        normed1,
+        embed,
+        resid_grad,
+        norm,
+        (late_grad, late_low) if count_dp == 8 else (),
+        qkv_parts,
+        count_dp // 2 if count_dp == 8 else 0,
+        6,
     )
     gain_grad = jnp.concatenate([gain1_grad, gain2_grad], 0)
     if count_dp == 8:
         gains = jnp.pad(gain_grad, ((0, 4), (0, 0)))
         row_lanes, shared_kept, totals = share(
-            early_grad, late_grad, patch_grad, unpatch_used, gains, loss_tile, alpha_label, count_dp // 2, 8
+            early_grad, own_late[0], embed_grad, own_patches, unpatch_used, gains, loss_tile, alpha_label, count_dp // 2, 8
         )
         row_share = row_lanes.reshape(-1)
         shared_share = shared_kept[FRONT : FRONT + SHARED_LANES].reshape(-1)
     else:
+        patch_grad = dot(own_patches, embed_grad, TN)
         unpatch_grad = jnp.concatenate(
             [unpatch_used, jnp.zeros((D, POUT - unpatch_used.shape[1]), jnp.float32)], 1
         )

time: 506 us -> 487 us (0.962); the launches traced: 505 us -> 478 us
  Pallas kernels: 484 us -> 457 us
    pallas_call x1, Pallas kernels: 143 us -> 98.3 us  [share(): pl.pallas_call(partial(share_kernel, lines), out_shape=(shape((chunk * wi...]
    pallas_call x1, Pallas kernels: 63.7 us -> 77.8 us  [attend_back(): pl.pallas_call(partial(attend_back_kernel, parts, 256, lines), out_shape=...]
where the time goes in v6:
time: 487 us; the launch traced here: 478 us
  Pallas kernels  457 us (94%)
  between operations  8.14 us (2%)
  local copies, waits for them, and re-layouts  7.79 us (2%)
  other arithmetic  5.49 us (1%)
    pallas_call x1, Pallas kernels, forward(): pl.pallas_call(partial(forward_kernel, lines, 256), out_shape=(shape((3 *...  124 us
    pallas_call x1, Pallas kernels, share(): pl.pallas_call(partial(share_kernel, lines), out_shape=(shape((chunk * wi...  98.3 us
    pallas_call x1, Pallas kernels, attend_back(): pl.pallas_call(partial(attend_back_kernel, parts, 256, lines), out_shape=...  77.8 us
    pallas_call x1, Pallas kernels, mlp_back(): pl.pallas_call(mlp_back_kernel, out_shape=(shape((width, used), WIDE), sh...  63.3 us
    pallas_call x1, Pallas kernels, render(): pl.pallas_call(partial(render_kernel, area, wide, block, split), out_shap...  49.3 us
    pallas_call x1, Pallas kernels, mlp(): pl.pallas_call(mlp_kernel, out_shape=(shape((length, hidden), WIDE), shap...  35.9 us

profile of v6, /device:TPU:0, one launch (start us, length us, event | category | flops | bytes accessed | tf_op | source)
XLA Modules:
  0.0 478.0 jit_solution(12957339071830551214)
XLA Ops:
  0.6 2.0 copy.26
  3.3 2.0 pad.8.shared_ref
  5.3 123.7 %shard_map.229 = (bf16[3072,1024]{1,0:T(8,128)(2,1)}, bf16[1024,128]{1,0:T(8,128)(2,1)}, f32[8,1024]{1,0:T(8,128)}, f32[384,1024]{1,0:T(8,128)}, bf16[1536,1024]...) custom-call(s32[1]{0:T(128)S(6)} %copy.27.count_ref, ...), custom_call_target="tpu_custom_call" | custom-call | tf_op jit(solution)/shard_map/pallas_call | solution.py:739
  129.0 0.0 copy-start.2
  129.0 0.0 copy-start.3
  129.1 0.0 copy-start.4
  129.1 35.9 %shard_map.230 = (f32[1536,1024]{1,0:T(8,128)}, bf16[1536,1024]{1,0:T(8,128)(2,1)}, bf16[384,1024]{1,0:T(8,128)(2,1)}, bf16[1536,128]{1,0:T(8,128)(2,1)}) custom-call(bf16[1536,1024]{1,0:T(8,128)(2,1)} %get-tuple-element.46.normed2_ref.normed2_in, bf16[3072,1024]{1,0:T(8,128)(2,1)} %get-tuple-element.47.weight_ref, ...), custom_call_target="tpu_custom_call" | custom-call | tf_op jit(solution)/shard_map/pallas_call | solution.py:843
  165.0 0.0 copy-done.2
  165.0 0.0 copy-done.3
  165.0 1.0 copy-done
  166.0 49.3 %shard_map.231 = (f32[8,128]{1,0:T(8,128)S(1)}, bf16[1536,128]{1,0:T(8,128)(2,1)S(1)}) custom-call(bf16[1536,128]{1,0:T(8,128)(2,1)S(1)} %copy-done, s32[4,6144]{1,0:T(4,128)S(1)} %bitcast.20, s32[4,6144]{1,0:T(4,128)S(1)} %bitcast.21, s32[1,6144]{1,0:T(1,128)S(1)} %copy-done.2), custom_call_target="tpu_custom_call" | custom-call | tf_op jit(solution)/shard_map/pallas_call | solution.py:1694
  215.3 0.0 copy-start.1
  215.3 0.7 copy-done.1
  216.1 0.6 copy-done.5
  216.6 63.3 %shard_map.232 = (f32[1024,128]{1,0:T(8,128)}, f32[2304,1024]{1,0:T(8,128)}, bf16[2304,1024]{1,0:T(8,128)(2,1)}, f32[384,1024]{1,0:T(8,128)}, bf16[1536,1024]{1,0:T(8,128)(2,1)}, /*index=5*/f32[2,1024]{1,0:T(2,128)}) custom-call(bf16[1536,128]{1,0:T(8,128)(2,1)} %copy-done.1, bf16[1024,128]{1,0:T(8,128)(2,1)} %get-tuple-element.49.cols_ref, ...), custom_call_target="tpu_custom_call" | custom-call | tf_op jit(solution)/shard_map/pallas_call | solution.py:996
  279.9 77.8 %shard_map.233 = (f32[768,1024]{1,0:T(8,128)}, bf16[384,1024]{1,0:T(8,128)(2,1)}, f32[2,1024]{1,0:T(2,128)}, f32[384,1024]{1,0:T(8,128)}) custom-call(s32[1]{0:T(128)S(6)} %copy.27.count_ref, bf16[1536,1024]{1,0:T(8,128)(2,1)} %get-tuple-element.57.branch_ref, bf16[3072,1024]{1,0:T(8,128)(2,1)} %get-tuple-element.47.weight_ref, ...), custom_call_target="tpu_custom_call" | custom-call | tf_op jit(solution)/shard_map/pallas_call | solution.py:1377
  357.7 0.0 copy-done.9
  357.7 1.3 select_maximum_fusion.gain_ref
  359.0 98.3 %shard_map.234 = (f32[3072,128]{1,0:T(8,128)}, f32[1616,128]{1,0:T(8,128)}, f32[8,128]{1,0:T(8,128)}) custom-call(f32[768,1024]{1,0:T(8,128)} %get-tuple-element.65.early_ref, f32[384,1024]{1,0:T(8,128)} %get-tuple-element.66.late_ref, bf16[384,1024]{1,0:T(8,128)(2,1)} %get-tuple-element.67.embed_ref, bf16[384,576]{1,0:T(8,128)(2,1)} %bitcast.24, ...), custom_call_target="tpu_custom_call" | custom-call | tf_op jit(solution)/shard_map/pallas_call | solution.py:1592
  457.4 1.4 fusion.5
  461.7 0.0 copy-start.8
  461.7 3.1 fusion.2
  464.8 1.1 multiply_add_fusion
  465.9 8.4 %shard_map.235 = (f32[1,393216]{1,0:T(1,128)}, f32[1,393216]{1,0:T(1,128)}, f32[1,393216]{1,0:T(1,128)}, f32[1,393216]{1,0:T(1,128)}, bf16[1,393216]{1,0:T(2,128)(2,1)}) custom-call(f32[8,128]{1,0:T(8,128)} %get-tuple-element.72.total_ref, s32[1]{0:T(128)S(6)} %copy.28.count_ref, f32[1,393216]{1,0:T(1,128)} %bitcast.26, f32[1,393216]{1,0:T(1,128)} %refs_1_.1, ...), custom_call_target="tpu_custom_call" | custom-call | tf_op jit(solution)/shard_map/pallas_call | solution.py:1962
  (9 shorter events, 0.0 us)
Async XLA Ops:
  129.0 36.0 %copy-start.2 = (s32[1,6144]{1,0:T(1,128)S(1)}, s32[1,6144]{1,0:T(1,128)}, u32[]{:S(2)}) copy-start(s32[1,6144]{1,0:T(1,128)} %label_ref.3) | copy-start | bytes 73732
  129.0 36.0 %copy-start.3 = (s32[1,4,6144]{2,1,0:T(4,128)S(1)}, s32[1,4,6144]{2,1,0:T(4,128)}, u32[]{:S(2)}) copy-start(s32[1,4,6144]{2,1,0:T(4,128)} %param.16) | copy-start | bytes 294916
  129.1 36.0 %copy-start.4 = (s32[1,4,6144]{2,1,0:T(4,128)S(1)}, s32[1,4,6144]{2,1,0:T(4,128)}, u32[]{:S(2)}) copy-start(s32[1,4,6144]{2,1,0:T(4,128)} %param.17) | copy-start | bytes 294916
  165.0 1.0 copy-start
  215.3 0.7 copy-start.1
  216.1 0.6 copy-start.5
  279.9 77.8 %copy-start.9 = (f32[2,1024]{1,0:T(2,128)S(1)}, f32[2,1024]{1,0:T(2,128)}, u32[]{:S(2)}) copy-start(f32[2,1024]{1,0:T(2,128)} %get-tuple-element.70) | copy-start | bytes 24580
  359.0 102.6 %copy-start.7 = (f32[172544]{0:T(1024)S(1)}, f32[172544]{0:T(1024)}, u32[]{:S(2)}) copy-start(f32[172544]{0:T(1024)} %param.24) | copy-start | bytes 2070532
  461.7 3.1 copy-start.8
  464.8 9.4 %copy-start.6 = (f32[172544]{0:T(1024)}, f32[172544]{0:T(1024)S(1)}, u32[]{:S(2)}) copy-start(f32[172544]{0:T(1024)S(1)} %get-tuple-element.81) | copy-start | bytes 2070532

commit v7 on v6

--- a/solution.py
+++ b/solution.py
@@ -40,6 +40,7 @@
 WIDE = jnp.float32
 PIECES = 4
 TILE = 256
+UNIT = 128
 
 
 def dot(left, right, dims=NN):
@@ -427,13 +428,10 @@
 
         by_half(self.short, line < spot.lines // 2, self.rows, go)
 
-    def own(self, kind, first=0, last=None):
-        @pl.loop(first, self.pieces if last is None else last)
+    def own(self, kind):
+        @pl.loop(0, self.pieces)
         def _(piece):
             self.run("start", kind, self.spot.line, piece)
-
-    def early(self):
-        return jnp.where(self.spot.line == 0, self.pieces, jnp.minimum(self.spot.line, self.pieces - 1))
 
     def begin(self):
         spot = self.spot
@@ -460,7 +458,9 @@
         def _():
             self.own(1)
 
-        self.own(2, 0, self.early())
+        @pl.when(self.spot.line == 0)
+        def _():
+            self.own(2)
 
     def step(self, at):
         spot = self.spot
@@ -468,7 +468,8 @@
 
         @pl.when(at < spot.line * self.pieces)
         def _():
-            line = at // self.pieces
+            turn = at // self.pieces
+            line = jnp.minimum(turn, 1) * (spot.line - turn) if self.late_own else turn
             self.run("wait_recv", 0, line, piece)
 
             @pl.when(spot.has_above)
@@ -479,13 +480,13 @@
 
         if self.late_own:
 
-            @pl.when((at == spot.line * self.pieces - 1) & spot.has_above)
+            @pl.when((at == self.pieces - 1) & spot.has_below & spot.has_above)
             def _():
                 self.own(0)
 
-            @pl.when((at == self.pieces - 1) & spot.has_below)
+            @pl.when(at == spot.line * self.pieces - 1)
             def _():
-                self.own(2, self.early())
+                self.own(2)
 
         @pl.when(at < (spot.lines - 1 - spot.line) * self.pieces)
         def _():
@@ -711,16 +712,7 @@
             weights.wait_crossed(0)
         if place == "turn":
 
-            @pl.when(lax.rem(at, 2) == 1)
-            def _():
-                weights.step(6 + at // 2)
-
-        if place == "give":
-
-            @pl.when(at < 3)
-            def _():
-                weights.step(9 + at)
-
+            weights.step(6 + at)
         if place == "out":
             weights.wait_crossed(1)
 
@@ -868,7 +860,7 @@
     )(normed2, weights, resid1, used_cols)
 
 
-def mlp_back_kernel(table_ref, cols_ref, low_ref, active_in, hidden_in, normed2_in, weight_ref, resid1_ref, norm_ref, attended_ref,
+def mlp_back_kernel(chunk, table_ref, cols_ref, low_ref, active_in, hidden_in, normed2_in, weight_ref, resid1_ref, norm_ref, attended_ref,
                     unpatch_ref, grad_out, rounded_out, resid_grad_ref, branch_ref, gain_ref,
                     gauss, down_in, hidden_grad, term, tail, active_ref, hidden_ref, normed2_ref, up_ref, down_ref, grad_ref,
                     rounded_ref, load_sem, store_sem, *comm):
@@ -876,13 +868,22 @@
     loads = Moves(
         load_sem,
         (weight_ref.at[pl.ds(2 * first, down_ref.shape[0])], down_ref),
-        (hidden_in, hidden_ref),
         (weight_ref.at[pl.ds(first, first)], up_ref),
         (normed2_in, normed2_ref),
         (active_in, active_ref),
     )
-    loads.start()
     corner = Corner()
+
+    def load_hidden(step):
+        here = rows_of(corner.block(step), resid1_ref.shape[0])
+        return pltpu.make_async_copy(hidden_in.at[here], hidden_ref.at[here], load_sem.at[4 + step])
+
+    loads.start(0)
+    load_hidden(0).start()
+    loads.start(1)
+    for step in range(1, 4):
+        load_hidden(step).start()
+    loads.start(2, 3)
     corner.greet()
     small = Scatter(corner, 1, *comm[:8])
     spread = Gather(corner, gauss, 1, comm[8:14])
@@ -908,11 +909,12 @@
     spread.relay(0)
     spread.finish()
     small.close()
-    loads.wait(0, 1, 2)
+    loads.wait(0, 1)
 
     @pl.loop(0, 4)
     def _(step):
         here = rows_of(corner.block(step), size)
+        load_hidden(step).wait()
         term[...] = dot(gauss[here], cols_ref[...], NT)
         down_in[here] = term[...].astype(LOW)
 
@@ -934,21 +936,32 @@
         column_loop(width, back)
         scatter.step(step, term)
 
-    def stores(tile):
-        part = pl.ds(pl.multiple_of(tile * TILE, TILE), TILE)
-        return (
-            pltpu.make_async_copy(grad_ref.at[part], grad_out.at[part], store_sem.at[0, tile]),
-            pltpu.make_async_copy(rounded_ref.at[part], rounded_out.at[part], store_sem.at[1, tile]),
-        )
+    side = None if chunk is None else lax.rem(lax.axis_index("dp"), 2)
+
+    def store(at, act):
+        part = pl.ds(pl.multiple_of(at * UNIT, UNIT), UNIT)
+
+        def wide():
+            getattr(pltpu.make_async_copy(grad_ref.at[part], grad_out.at[part], store_sem.at[at]), act)()
+
+        def rounded():
+            getattr(pltpu.make_async_copy(rounded_ref.at[part], rounded_out.at[part], store_sem.at[at]), act)()
+
+        if chunk is None:
+            wide()
+            return
+        mine = lax.rem(at * UNIT // chunk, 2) == side
+        pl.when(mine)(wide)
+        pl.when(jnp.logical_not(mine))(rounded)
 
     def keep(tile, value):
         part = pl.ds(pl.multiple_of(tile * TILE, TILE), TILE)
         grad_ref[part, :] = value
         rounded_ref[part, :] = value.astype(LOW)
-        for copy in stores(tile):
-            copy.start()
-
-    loads.wait(3, 4)
+        for at in range(TILE // UNIT):
+            store(tile * (TILE // UNIT) + at, "start")
+
+    loads.wait(2, 3)
     tiles = attended_ref.shape[1] // TILE
 
     @pl.loop(0, width // TILE)
@@ -982,19 +995,18 @@
     for tile in range(tiles):
         keep(tile, dot(attended_ref[:, tile * TILE : (tile + 1) * TILE], branch_ref[...], TN))
 
-    @pl.loop(0, grad_ref.shape[0] // TILE)
-    def _(tile):
-        for copy in stores(tile):
-            copy.wait()
-
-
-def mlp_back(table_grad, used_cols, low, active, hidden, normed2, weights, resid1, norm, attended, collective_id):
+    @pl.loop(0, grad_ref.shape[0] // UNIT)
+    def _(at):
+        store(at, "wait")
+
+
+def mlp_back(table_grad, used_cols, low, active, hidden, normed2, weights, resid1, norm, attended, chunk, collective_id):
     length, size, width = normed2.shape[0], resid1.shape[0], resid1.shape[1]
     ff, used = hidden.shape[1], used_cols.shape[1]
     total = attended.shape[1] + width + ff
     shape = jax.ShapeDtypeStruct
     return pl.pallas_call(
-        mlp_back_kernel,
+        partial(mlp_back_kernel, chunk),
         out_shape=(
             shape((width, used), WIDE),
             shape((total, width), WIDE),
@@ -1018,8 +1030,8 @@
             pltpu.VMEM((ff, width), LOW),
             pltpu.VMEM((total, width), WIDE),
             pltpu.VMEM((total, width), LOW),
-            pltpu.SemaphoreType.DMA((5,)),
-            pltpu.SemaphoreType.DMA((2, total // TILE)),
+            pltpu.SemaphoreType.DMA((8,)),
+            pltpu.SemaphoreType.DMA((total // UNIT,)),
         ]
         + Scatter.scratch(size, used, 1)
         + Gather.scratch(1)
@@ -1105,31 +1117,38 @@
         slot = self.slot(step)
         self.part[slot] += self.low_in[slot].astype(WIDE) if low else self.line_in[slot]
 
+    def low_hop(self, rising, target):
+        line, last = self.spot.line, self.spot.lines - 1
+        if rising:
+            top = target == last
+            return (line == 0) | ((line == 1) & top), (line == 1) | ((line == 2) & top)
+        return line == last, line == last - 1
+
     def travel(self, step, rising):
         spot, slot = self.spot, self.slot(step)
         to, recv = (spot.above, self.up_recv) if rising else (spot.below, self.down_recv)
         last = spot.lines - 1
-        from_end = spot.line == (1 if rising else last - 1)
         at_end = spot.line == (0 if rising else last)
         target = self.target(step)
         if self.low:
-
-            @pl.when(at_end)
+            low_sent, low_taken = self.low_hop(rising, target)
+
+            @pl.when(jnp.logical_not(at_end) & low_taken)
+            def _():
+                self.low_copy(step, to, recv).wait_recv()
+                self.add(step, True)
+
+            @pl.when(jnp.logical_not(at_end | low_taken))
+            def _():
+                self.line_copy(step, to, recv).wait_recv()
+                self.add(step, False)
+
+            @pl.when(low_sent)
             def _():
                 self.low_out[slot] = self.part[slot].astype(LOW)
                 self.low_copy(step, to, recv).start()
 
-            @pl.when(from_end)
-            def _():
-                self.low_copy(step, to, recv).wait_recv()
-                self.add(step, True)
-
-            @pl.when(jnp.logical_not(at_end | from_end))
-            def _():
-                self.line_copy(step, to, recv).wait_recv()
-                self.add(step, False)
-
-            @pl.when(jnp.logical_not(at_end))
+            @pl.when(jnp.logical_not(low_sent))
             def _():
                 self.line_copy(step, to, recv).start()
         else:
@@ -1187,11 +1206,13 @@
         def _():
             if self.low:
 
-                @pl.when(spot.line == 0)
+                low_sent, low_taken = self.low_hop(True, target)
+
+                @pl.when(low_sent)
                 def _():
                     self.low_copy(step, spot.above, self.up_recv).wait_send()
 
-                @pl.when(spot.line > 0)
+                @pl.when(jnp.logical_not(low_sent))
                 def _():
                     self.line_copy(step, spot.above, self.up_recv).wait_send()
             else:
@@ -1318,7 +1339,9 @@
                 key_grad[:, lanes] += dot(score_grad, own_query, TN)
             qkv_grad[here, lanes] = (jnp.where(left, found[0], found[1]) * (DH ** (-0.5))).astype(LOW)
         if lines:
-            for at in range(2):
+
+            @pl.loop(0, 2)
+            def _(at):
                 late.advance(2 * turn + at)
 
     qkv_grad[:, local : 2 * local] = key_grad[...].astype(LOW)
@@ -1343,8 +1366,11 @@
             if at // TILE == tile:
                 at = at % TILE
                 grad_ref[row : row + rows, col : col + cols] = value[at : at + rows, at_col : at_col + cols]
-        if lines:
-            late.advance(16 + tile)
+    if lines:
+
+        @pl.loop(16, 20)
+        def _(step):
+            late.advance(step)
 
     gain_sum, bias_sum = jnp.zeros((1, width), WIDE), jnp.zeros((1, width), WIDE)
     for piece in range(PIECES):
@@ -1358,7 +1384,9 @@
     gain_ref[1:2] = bias_sum
     scatter.close()
     if lines:
-        for step in range(20, late.count + lines - 1):
+
+        @pl.loop(20, late.count + lines - 1)
+        def _(step):
             late.advance(step)
 
         def keep_rows(piece, value):
@@ -1493,13 +1521,19 @@
 
         scatter.step(step, term)
 
-    for step in range(2):
+    @pl.loop(0, 2)
+    def _(step):
         weights.advance(step)
+
     for piece in range(PIECES):
         mine[scatter.part(piece)] = scatter.land(piece, term)
-    for step in range(lines):
+
+    @pl.loop(0, lines)
+    def _(step):
         shared.begin(step)
-    for step in range(2 * lines - 1):
+
+    @pl.loop(0, 2 * lines - 1)
+    def _(step):
         weights.advance(2 + step)
         shared.advance(step)
 
@@ -1542,13 +1576,14 @@
     gather.finish()
     shared_ref[...] = jnp.zeros_like(shared_ref)
     for phase in range(5):
-        for quarter in range(4):
-
+
+        @pl.loop(0, 4)
+        def _(quarter):
             def take(condition, row, height, j, start, stride):
                 @pl.when(condition)
                 def _():
-                    at = quarter * WINDOW + row
-                    shared_ref[pl.ds(start, height, stride)] = windows[at : at + height, j * 128 : (j + 1) * 128]
+                    here = pl.ds(pl.multiple_of(quarter * WINDOW + row, 16), height)
+                    shared_ref[pl.ds(start, height, stride)] = windows[here, j * 128 : (j + 1) * 128]
 
             shared_walk(spot.me, quarter, take, (phase,))
     kept = shared_ref[FRONT : FRONT + PADDED - FRONT]
@@ -2024,7 +2059,7 @@
     loss_tile, table_grad = render(gauss_table, splat_index[0], splat_dist[0], alpha_label, PATCH * PATCH)
     loss_part = loss_tile[0, 0]
     unpatch_used, late_grad, late_low, resid_grad, branch, gain2_grad = mlp_back(
-        table_grad, used_cols, resid2_low, active, hidden, normed2, weights, resid1, norm, attended, 5
+        table_grad, used_cols, resid2_low, active, hidden, normed2, weights, resid1, norm, attended, share_rows if count_dp == 8 else None, 5
     )
     early_grad, embed_grad, gain1_grad, *own_late = attend_back(
         view_counts,

time: 487 us -> 471 us (0.967); the launches traced: 478 us -> 470 us
  Pallas kernels: 457 us -> 449 us
    pallas_call x1, Pallas kernels: 98.3 us -> 92.3 us  [share(): pl.pallas_call(partial(share_kernel, lines), out_shape=(shape((chunk * wi...]
where the time goes in v7:
time: 471 us; the launch traced here: 470 us
  Pallas kernels  449 us (95%)
  between operations  7.96 us (2%)
  local copies, waits for them, and re-layouts  7.79 us (2%)
  other arithmetic  5.49 us (1%)
    pallas_call x1, Pallas kernels, forward(): pl.pallas_call(partial(forward_kernel, lines, 256), out_shape=(shape((3 *...  124 us
    pallas_call x1, Pallas kernels, share(): pl.pallas_call(partial(share_kernel, lines), out_shape=(shape((chunk * wi...  92.3 us
    pallas_call x1, Pallas kernels, attend_back(): pl.pallas_call(partial(attend_back_kernel, parts, 256, lines), out_shape=...  76.7 us
    pallas_call x1, Pallas kernels, mlp_back(): pl.pallas_call(partial(mlp_back_kernel, chunk), out_shape=(shape((width,...  62.8 us
    pallas_call x1, Pallas kernels, render(): pl.pallas_call(partial(render_kernel, area, wide, block, split), out_shap...  49.3 us
    pallas_call x1, Pallas kernels, mlp(): pl.pallas_call(mlp_kernel, out_shape=(shape((length, hidden), WIDE), shap...  35.9 us

profile of v7, /device:TPU:0, one launch (start us, length us, event | category | flops | bytes accessed | tf_op | source)
XLA Modules:
  0.0 470.5 jit_solution(8154704835714084175)
XLA Ops:
  0.6 2.0 copy.26
  3.3 2.0 pad.8.shared_ref
  5.3 123.8 %shard_map.229 = (bf16[3072,1024]{1,0:T(8,128)(2,1)}, bf16[1024,128]{1,0:T(8,128)(2,1)}, f32[8,1024]{1,0:T(8,128)}, f32[384,1024]{1,0:T(8,128)}, bf16[1536,1024]...) custom-call(s32[1]{0:T(128)S(6)} %copy.27.count_ref, ...), custom_call_target="tpu_custom_call" | custom-call | tf_op jit(solution)/shard_map/pallas_call | solution.py:731
  129.2 0.0 copy-start.2
  129.2 0.0 copy-start.3
  129.2 0.0 copy-start.4
  129.2 35.9 %shard_map.230 = (f32[1536,1024]{1,0:T(8,128)}, bf16[1536,1024]{1,0:T(8,128)(2,1)}, bf16[384,1024]{1,0:T(8,128)(2,1)}, bf16[1536,128]{1,0:T(8,128)(2,1)}) custom-call(bf16[1536,1024]{1,0:T(8,128)(2,1)} %get-tuple-element.46.normed2_ref.normed2_in, bf16[3072,1024]{1,0:T(8,128)(2,1)} %get-tuple-element.47.weight_ref, ...), custom_call_target="tpu_custom_call" | custom-call | tf_op jit(solution)/shard_map/pallas_call | solution.py:835
  165.2 1.0 copy-done
  166.1 49.3 %shard_map.231 = (f32[8,128]{1,0:T(8,128)S(1)}, bf16[1536,128]{1,0:T(8,128)(2,1)S(1)}) custom-call(bf16[1536,128]{1,0:T(8,128)(2,1)S(1)} %copy-done, s32[4,6144]{1,0:T(4,128)S(1)} %bitcast.20, s32[4,6144]{1,0:T(4,128)S(1)} %bitcast.21, s32[1,6144]{1,0:T(1,128)S(1)} %copy-done.2), custom_call_target="tpu_custom_call" | custom-call | tf_op jit(solution)/shard_map/pallas_call | solution.py:1729
  215.4 0.0 copy-start.1
  215.4 0.7 copy-done.1
  216.2 0.6 copy-done.5
  216.8 62.8 %shard_map.232 = (f32[1024,128]{1,0:T(8,128)}, f32[2304,1024]{1,0:T(8,128)}, bf16[2304,1024]{1,0:T(8,128)(2,1)}, f32[384,1024]{1,0:T(8,128)}, bf16[1536,1024]{1,0:T(8,128)(2,1)}, /*index=5*/f32[2,1024]{1,0:T(2,128)}) custom-call(bf16[1536,128]{1,0:T(8,128)(2,1)} %copy-done.1, bf16[1024,128]{1,0:T(8,128)(2,1)} %get-tuple-element.49.cols_ref, ...), custom_call_target="tpu_custom_call" | custom-call | tf_op jit(solution)/shard_map/pallas_call | solution.py:1008
  279.6 76.7 %shard_map.233 = (f32[768,1024]{1,0:T(8,128)}, bf16[384,1024]{1,0:T(8,128)(2,1)}, f32[2,1024]{1,0:T(2,128)}, f32[384,1024]{1,0:T(8,128)}) custom-call(s32[1]{0:T(128)S(6)} %copy.27.count_ref, bf16[1536,1024]{1,0:T(8,128)(2,1)} %get-tuple-element.57.branch_ref, bf16[3072,1024]{1,0:T(8,128)(2,1)} %get-tuple-element.47.weight_ref, ...), custom_call_target="tpu_custom_call" | custom-call | tf_op jit(solution)/shard_map/pallas_call | solution.py:1405
  356.3 0.0 copy-done.9
  356.3 1.3 select_maximum_fusion.gain_ref
  357.7 92.3 %shard_map.234 = (f32[3072,128]{1,0:T(8,128)}, f32[1616,128]{1,0:T(8,128)}, f32[8,128]{1,0:T(8,128)}) custom-call(f32[768,1024]{1,0:T(8,128)} %get-tuple-element.65.early_ref, f32[384,1024]{1,0:T(8,128)} %get-tuple-element.66.late_ref, bf16[384,1024]{1,0:T(8,128)(2,1)} %get-tuple-element.67.embed_ref, bf16[384,576]{1,0:T(8,128)(2,1)} %bitcast.24, ...), custom_call_target="tpu_custom_call" | custom-call | tf_op jit(solution)/shard_map/pallas_call | solution.py:1627
  450.0 1.4 fusion.5
  454.3 0.0 copy-done.7
  454.3 0.0 copy-start.8
  454.3 3.1 fusion.2
  457.4 1.1 multiply_add_fusion
  458.5 8.4 %shard_map.235 = (f32[1,393216]{1,0:T(1,128)}, f32[1,393216]{1,0:T(1,128)}, f32[1,393216]{1,0:T(1,128)}, f32[1,393216]{1,0:T(1,128)}, bf16[1,393216]{1,0:T(2,128)(2,1)}) custom-call(f32[8,128]{1,0:T(8,128)} %get-tuple-element.72.total_ref, s32[1]{0:T(128)S(6)} %copy.28.count_ref, f32[1,393216]{1,0:T(1,128)} %bitcast.26, f32[1,393216]{1,0:T(1,128)} %refs_1_.1, ...), custom_call_target="tpu_custom_call" | custom-call | tf_op jit(solution)/shard_map/pallas_call | solution.py:1997
  466.9 0.0 copy-done.6
  (9 shorter events, 0.0 us)
Async XLA Ops:
  129.2 36.0 %copy-start.2 = (s32[1,6144]{1,0:T(1,128)S(1)}, s32[1,6144]{1,0:T(1,128)}, u32[]{:S(2)}) copy-start(s32[1,6144]{1,0:T(1,128)} %label_ref.3) | copy-start | bytes 73732
  129.2 36.0 %copy-start.3 = (s32[1,4,6144]{2,1,0:T(4,128)S(1)}, s32[1,4,6144]{2,1,0:T(4,128)}, u32[]{:S(2)}) copy-start(s32[1,4,6144]{2,1,0:T(4,128)} %param.16) | copy-start | bytes 294916
  129.2 36.0 %copy-start.4 = (s32[1,4,6144]{2,1,0:T(4,128)S(1)}, s32[1,4,6144]{2,1,0:T(4,128)}, u32[]{:S(2)}) copy-start(s32[1,4,6144]{2,1,0:T(4,128)} %param.17) | copy-start | bytes 294916
  165.2 1.0 copy-start
  215.4 0.7 copy-start.1
  216.2 0.6 copy-start.5
  279.6 76.7 %copy-start.9 = (f32[2,1024]{1,0:T(2,128)S(1)}, f32[2,1024]{1,0:T(2,128)}, u32[]{:S(2)}) copy-start(f32[2,1024]{1,0:T(2,128)} %get-tuple-element.70) | copy-start | bytes 24580
  357.7 96.6 %copy-start.7 = (f32[172544]{0:T(1024)S(1)}, f32[172544]{0:T(1024)}, u32[]{:S(2)}) copy-start(f32[172544]{0:T(1024)} %param.24) | copy-start | bytes 2070532
  454.3 3.1 copy-start.8
  457.4 9.4 %copy-start.6 = (f32[172544]{0:T(1024)}, f32[172544]{0:T(1024)S(1)}, u32[]{:S(2)}) copy-start(f32[172544]{0:T(1024)S(1)} %get-tuple-element.81) | copy-start | bytes 2070532

commit v8 on v7

--- a/solution.py
+++ b/solution.py
@@ -1652,7 +1652,7 @@
     )(early, late, embed_grad, patches, used_grad, gains, loss_tile, labels)
 
 
-def render_kernel(area, wide, block, split, table_ref, splat_ref, dist_ref, label_ref, loss_ref, grad_ref, flip, picked, hot, spread_grad):
+def render_kernel(area, wide, block, split, span, table_ref, splat_ref, dist_ref, label_ref, loss_ref, grad_ref, flip, hot, weighted, spread_grad):
     tokens = table_ref.shape[0]
     groups = tokens // wide
     splats, pixels = splat_ref.shape
@@ -1671,20 +1671,22 @@
             index = splat_ref[k : k + 1, here]
             token = index // area
             column = (token % wide).astype(jnp.float32).astype(jnp.bfloat16)
-            group = (token // wide)
-            cell = (index % area).astype(jnp.float32)
-            match = jnp.where(wide_ids == column, one, nil)
-            hot[k] = match
-            picked[...] = lax.dot_general(flip[...], match, NN, preferred_element_type=jnp.float32)
+            lows.append((token // wide, (index % area).astype(jnp.float32)))
+            hot[:, k * block : (k + 1) * block] = jnp.where(wide_ids == column, one, nil)
+        for k in range(splats):
+            lanes = slice(k * block, (k + 1) * block)
+            group, cell = lows[k]
             op_sum = jnp.zeros((area, block), jnp.float32)
             sp_sum = jnp.zeros((area, block), jnp.float32)
-            for j in range(groups):
-                same = cell_ids == jnp.where(group == j, cell, -1.0)
-                op_sum += jnp.where(same, picked[j * 2 * area : j * 2 * area + area], 0.0)
-                sp_sum += jnp.where(same, picked[j * 2 * area + area : (j + 1) * 2 * area], 0.0)
+            for at in range(0, groups, span):
+                rows = slice(at * 2 * area, (at + span) * 2 * area)
+                found = lax.dot_general(flip[rows], hot[:, lanes], NN, preferred_element_type=jnp.float32)
+                for j in range(span):
+                    same = cell_ids == jnp.where(group == at + j, cell, -1.0)
+                    op_sum += jnp.where(same, found[j * 2 * area : j * 2 * area + area], 0.0)
+                    sp_sum += jnp.where(same, found[j * 2 * area + area : (j + 1) * 2 * area], 0.0)
             opacities.append(jnp.sum(op_sum, 0, keepdims=True))
             spreads.append(jnp.sum(sp_sum, 0, keepdims=True))
-            lows.append((group, cell))
         opacity, spread = jnp.concatenate(opacities, 0), jnp.concatenate(spreads, 0)
         distance = dist_ref[:, here].astype(jnp.float32)
         labels = label_ref[:, here]
@@ -1702,19 +1704,27 @@
         contrib_grad = -keep_grad / (1.0 - contrib)
         op_grad = contrib_grad * (0.96 * op_sig * (1.0 - op_sig)) * fade
         sp_grad = contrib_grad * contrib * (-0.25 * distance * sp_sig * (1.0 - sp_sig))
-        for k in range(splats):
-            group, cell = lows[k]
-            parts_op, parts_sp = op_grad[k : k + 1], sp_grad[k : k + 1]
+        zero = jnp.zeros((area, block), jnp.bfloat16)
+        op_parts, sp_parts = [], []
+        for part in range(split):
+            op_parts.append(op_grad.astype(jnp.bfloat16))
+            sp_parts.append(sp_grad.astype(jnp.bfloat16))
+            op_grad, sp_grad = op_grad - op_parts[-1].astype(jnp.float32), sp_grad - sp_parts[-1].astype(jnp.float32)
+        for at in range(0, groups, span):
+            rows = slice(at * 2 * area, (at + span) * 2 * area)
+            for k in range(splats):
+                lanes = slice(k * block, (k + 1) * block)
+                group, cell = lows[k]
+                for j in range(span):
+                    same = cell_low == jnp.where(group == at + j, cell, -1.0).astype(jnp.bfloat16)
+                    first = (at + j) * 2 * area
+                    for part in range(split):
+                        weighted[part, first : first + area, lanes] = jnp.where(same, op_parts[part][k : k + 1], zero)
+                        weighted[part, first + area : first + 2 * area, lanes] = jnp.where(same, sp_parts[part][k : k + 1], zero)
+            total = spread_grad[rows]
             for part in range(split):
-                low_op, low_sp = parts_op.astype(jnp.bfloat16), parts_sp.astype(jnp.bfloat16)
-                parts_op, parts_sp = parts_op - low_op.astype(jnp.float32), parts_sp - low_sp.astype(jnp.float32)
-                pieces = []
-                for j in range(groups):
-                    same = cell_low == jnp.where(group == j, cell, -1.0).astype(jnp.bfloat16)
-                    pieces.append(jnp.where(same, low_op, jnp.bfloat16(0)))
-                    pieces.append(jnp.where(same, low_sp, jnp.bfloat16(0)))
-                weighted = jnp.concatenate(pieces, 0)
-                spread_grad[...] += lax.dot_general(weighted, hot[k], NT, preferred_element_type=jnp.float32)
+                total += lax.dot_general(weighted[part, rows], hot[...], NT, preferred_element_type=jnp.float32)
+            spread_grad[rows] = total
         return loss
 
     loss = lax.fori_loop(0, pixels // block, one_block, jnp.zeros((1, block), jnp.float32))
@@ -1722,17 +1732,18 @@
     for j in range(groups):
         grad_ref[j * wide : (j + 1) * wide] = jnp.transpose(spread_grad[j * 2 * area : (j + 1) * 2 * area]).astype(grad_ref.dtype)
 
-def render(table, splats, distance, labels, area, block=512, wide=256, split=2):
+def render(table, splats, distance, labels, area, block=768, wide=256, split=2, span=3):
     tokens = table.shape[0]
     vm = pl.BlockSpec(memory_space=pltpu.VMEM)
     groups = tokens // wide
+    count = splats.shape[0]
     return pl.pallas_call(
-        partial(render_kernel, area, wide, block, split),
+        partial(render_kernel, area, wide, block, split, span),
         out_shape=(jax.ShapeDtypeStruct((8, 128), jnp.float32), jax.ShapeDtypeStruct(table.shape, jnp.bfloat16)),
         in_specs=[vm] * 4, out_specs=(vm, vm),
-        scratch_shapes=[pltpu.VMEM((groups * 2 * area, wide), jnp.bfloat16), pltpu.VMEM((groups * 2 * area, block), jnp.float32),
-            pltpu.VMEM((splats.shape[0], wide, block), jnp.bfloat16), pltpu.VMEM((groups * 2 * area, wide), jnp.float32)],
-        compiler_params=pltpu.CompilerParams(vmem_limit_bytes=48 * 2**20),
+        scratch_shapes=[pltpu.VMEM((groups * 2 * area, wide), jnp.bfloat16),
+            pltpu.VMEM((wide, count * block), jnp.bfloat16), pltpu.VMEM((split, groups * 2 * area, count * block), jnp.bfloat16), pltpu.VMEM((groups * 2 * area, wide), jnp.float32)],
+        compiler_params=pltpu.CompilerParams(vmem_limit_bytes=60 * 2**20),
     )(table, splats, distance, labels)
 
 

time: 471 us -> 454 us (0.964)
  Pallas kernels: 449 us -> 435 us
    pallas_call x1, Pallas kernels: 49.3 us -> 35.1 us  [render(): pl.pallas_call(partial(render_kernel, area, wide, block, split, span), ou...]
where the time goes in v8:
time: 454 us
  Pallas kernels  435 us (96%)
  between operations  7.72 us (2%)
  other arithmetic  5.49 us (1%)
  local copies, waits for them, and re-layouts  5.43 us (1%)
    pallas_call x1, Pallas kernels, forward(): pl.pallas_call(partial(forward_kernel, lines, 256), out_shape=(shape((3 *...  124 us
    pallas_call x1, Pallas kernels, share(): pl.pallas_call(partial(share_kernel, lines), out_shape=(shape((chunk * wi...  92.3 us
    pallas_call x1, Pallas kernels, attend_back(): pl.pallas_call(partial(attend_back_kernel, parts, 256, lines), out_shape=...  76.8 us
    pallas_call x1, Pallas kernels, mlp_back(): pl.pallas_call(partial(mlp_back_kernel, chunk), out_shape=(shape((width,...  62.8 us
    pallas_call x1, Pallas kernels, mlp(): pl.pallas_call(mlp_kernel, out_shape=(shape((length, hidden), WIDE), shap...  35.9 us
    pallas_call x1, Pallas kernels, render(): pl.pallas_call(partial(render_kernel, area, wide, block, split, span), ou...  35.1 us

profile of v8, /device:TPU:0, one launch (start us, length us, event | category | flops | bytes accessed | tf_op | source)
XLA Modules:
  0.0 453.6 jit_solution(3640915727446512086)
XLA Ops:
  0.6 2.0 copy.26
  3.3 2.0 pad.8.shared_ref
  5.3 123.8 %shard_map.229 = (bf16[3072,1024]{1,0:T(8,128)(2,1)}, bf16[1024,128]{1,0:T(8,128)(2,1)}, f32[8,1024]{1,0:T(8,128)}, f32[384,1024]{1,0:T(8,128)}, bf16[1536,1024]...) custom-call(s32[1]{0:T(128)S(6)} %copy.27.count_ref, ...), custom_call_target="tpu_custom_call" | custom-call | tf_op jit(solution)/shard_map/pallas_call | solution.py:731
  129.1 35.9 %shard_map.230 = (f32[1536,1024]{1,0:T(8,128)}, bf16[1536,1024]{1,0:T(8,128)(2,1)}, bf16[384,1024]{1,0:T(8,128)(2,1)}, bf16[1536,128]{1,0:T(8,128)(2,1)}) custom-call(bf16[1536,1024]{1,0:T(8,128)(2,1)} %get-tuple-element.46.normed2_ref.normed2_in, bf16[3072,1024]{1,0:T(8,128)(2,1)} %get-tuple-element.47.weight_ref, ...), custom_call_target="tpu_custom_call" | custom-call | tf_op jit(solution)/shard_map/pallas_call | solution.py:835
  165.0 35.1 %shard_map.231 = (f32[8,128]{1,0:T(8,128)}, bf16[1536,128]{1,0:T(8,128)(2,1)}) custom-call(bf16[1536,128]{1,0:T(8,128)(2,1)} %get-tuple-element.50.table_ref, s32[4,6144]{1,0:T(4,128)} %bitcast.25, s32[4,6144]{1,0:T(4,128)} %bitcast.26, s32[1,6144]{1,0:T(1,128)} %label_ref.3), custom_call_target="tpu_custom_call" | custom-call | tf_op jit(solution)/shard_map/pallas_call | solution.py:1740
  200.1 62.8 %shard_map.232 = (f32[1024,128]{1,0:T(8,128)}, f32[2304,1024]{1,0:T(8,128)}, bf16[2304,1024]{1,0:T(8,128)(2,1)}, f32[384,1024]{1,0:T(8,128)}, bf16[1536,1024]{1,0:T(8,128)(2,1)}, /*index=5*/f32[2,1024]{1,0:T(2,128)}) custom-call(bf16[1536,128]{1,0:T(8,128)(2,1)} %get-tuple-element.51.table_ref, bf16[1024,128]{1,0:T(8,128)(2,1)} %get-tuple-element.49.cols_ref, ...), custom_call_target="tpu_custom_call" | custom-call | tf_op jit(solution)/shard_map/pallas_call | solution.py:1008
  262.9 0.0 copy-start.3
  262.9 76.8 %shard_map.233 = (f32[768,1024]{1,0:T(8,128)}, bf16[384,1024]{1,0:T(8,128)(2,1)}, f32[2,1024]{1,0:T(2,128)}, f32[384,1024]{1,0:T(8,128)}) custom-call(s32[1]{0:T(128)S(6)} %copy.27.count_ref, bf16[1536,1024]{1,0:T(8,128)(2,1)} %get-tuple-element.57.branch_ref, bf16[3072,1024]{1,0:T(8,128)(2,1)} %get-tuple-element.47.weight_ref, ...), custom_call_target="tpu_custom_call" | custom-call | tf_op jit(solution)/shard_map/pallas_call | solution.py:1405
  339.7 0.0 copy-done.3
  339.7 1.3 select_maximum_fusion.gain_ref
  341.0 0.0 copy-start.1
  341.0 92.3 %shard_map.234 = (f32[3072,128]{1,0:T(8,128)}, f32[1616,128]{1,0:T(8,128)}, f32[8,128]{1,0:T(8,128)}) custom-call(f32[768,1024]{1,0:T(8,128)} %get-tuple-element.65.early_ref, f32[384,1024]{1,0:T(8,128)} %get-tuple-element.66.late_ref, bf16[384,1024]{1,0:T(8,128)(2,1)} %get-tuple-element.67.embed_ref, bf16[384,576]{1,0:T(8,128)(2,1)} %bitcast.22, ...), custom_call_target="tpu_custom_call" | custom-call | tf_op jit(solution)/shard_map/pallas_call | solution.py:1627
  433.3 1.4 fusion.5
  437.5 0.0 copy-done.1
  437.5 0.0 copy-start.2
  437.5 3.1 fusion.2
  440.6 0.0 copy-start
  440.6 0.0 copy-done.2
  440.6 1.1 multiply_add_fusion
  441.6 8.4 %shard_map.235 = (f32[1,393216]{1,0:T(1,128)}, f32[1,393216]{1,0:T(1,128)}, f32[1,393216]{1,0:T(1,128)}, f32[1,393216]{1,0:T(1,128)}, bf16[1,393216]{1,0:T(2,128)(2,1)}) custom-call(f32[8,128]{1,0:T(8,128)} %get-tuple-element.72.total_ref, s32[1]{0:T(128)S(6)} %copy.28.count_ref, f32[1,393216]{1,0:T(1,128)} %bitcast.24, f32[1,393216]{1,0:T(1,128)} %refs_1_.1, ...), custom_call_target="tpu_custom_call" | custom-call | tf_op jit(solution)/shard_map/pallas_call | solution.py:2008
  450.0 0.0 copy-done
Async XLA Ops:
  262.9 76.8 %copy-start.3 = (f32[2,1024]{1,0:T(2,128)S(1)}, f32[2,1024]{1,0:T(2,128)}, u32[]{:S(2)}) copy-start(f32[2,1024]{1,0:T(2,128)} %get-tuple-element.70) | copy-start | bytes 24580
  341.0 96.4 %copy-start.1 = (f32[172544]{0:T(1024)S(1)}, f32[172544]{0:T(1024)}, u32[]{:S(2)}) copy-start(f32[172544]{0:T(1024)} %param.24) | copy-start | bytes 2070532
  437.5 3.1 copy-start.2
  440.6 9.4 %copy-start = (f32[172544]{0:T(1024)}, f32[172544]{0:T(1024)S(1)}, u32[]{:S(2)}) copy-start(f32[172544]{0:T(1024)S(1)} %get-tuple-element.81) | copy-start | bytes 2070532

commit v9 on v8

--- a/solution.py
+++ b/solution.py
@@ -535,6 +535,22 @@
     return jnp.minimum(owner, 4) * WINDOW + jnp.maximum(owner - 4, 0) * SHORT
 
 
+def window_valid(me, quarter, width):
+    row = lax.broadcasted_iota(jnp.int32, (WINDOW, width), 0)
+    block = lax.broadcasted_iota(jnp.int32, (WINDOW, width), 1) // 128
+    start, stop = me * SHARED_LANES, (me + 1) * SHARED_LANES
+    patch_row = jnp.where(me == 3, ROW_START[3] + 32 * quarter, 160 * me + 16 * (me // 2) + WINDOW * quarter) + row
+    lane = 8 * patch_row + block
+    patch = (me < 4) & ((me < 3) | ((quarter < 3) & (row < 32))) & (lane >= start) & (lane < stop) & (lane < PATCH_LANES)
+    first = (me == 3) & (quarter < 3) & (row >= 32) & (block < 3)
+    other = (me > 3) & (row < SHORT) & (block < 4)
+    index = jnp.where(me == 3, 48 * quarter + 16 * block + row - 32, 224 * me - 768 + 64 * quarter + SHORT * block + row)
+    lane = PATCH_LANES + 6 * index
+    used = (first | other) & (index < D) & (lane >= start) & (lane < stop)
+    norm = (me == 7) & (quarter == 0) & (row < 8) & (block >= 4)
+    return patch | used | norm
+
+
 def shared_offsets(me, quarter):
     chunk = SHARED_LANES
     rows = jnp.where(me == 0, 0, jnp.where(me == 1, 160, jnp.where(me == 2, 336, 496)))
@@ -590,10 +606,10 @@
 CHUNK_PIECES = 4
 
 
-def forward_kernel(lines, q_rows, count_ref, row_ref, shared_ref, own_patch_ref,
+def forward_kernel(lines, q_rows, count_ref, row_ref, lanes_ref, own_patch_ref,
                    weight_ref, used_ref, norm_ref,
                    embed_ref, normed1_ref, qkv_ref, attended_ref, log_ref, resid_ref, normed2_ref,
-                   patches, proj, windows, own_chunk, own_sem, *rest):
+                   patches, proj, windows, shared_ref, own_chunk, own_sem, *rest):
     body, extra = rest[:4 + 14], rest[4 + 14:]
     corner, spot = Corner(), Lines(lines)
     barrier = pltpu.get_barrier_semaphore()
@@ -612,6 +628,8 @@
     given.start(0)
     base = pl.multiple_of((corner.me * 2 * lines + spot.me) * WINDOW, 16)
     windows[pl.ds(base, WINDOW)] = jnp.zeros((WINDOW, windows.shape[1]), LOW)
+    shared_ref[...] = jnp.zeros_like(shared_ref)
+    shared_ref[FRONT : FRONT + SHARED_LANES] = lanes_ref[...]
 
     def take(condition, row, rows, j, start, stride):
         @pl.when(condition)
@@ -748,6 +766,7 @@
             pltpu.VMEM((length, inputs), LOW),
             pltpu.VMEM((inputs, width), LOW),
             pltpu.VMEM((8 * lines * WINDOW, width), LOW),
+            pltpu.VMEM((PADDED, 128), WIDE),
             pltpu.VMEM((3 * D // (2 * lines), width), LOW),
             pltpu.SemaphoreType.DMA(()),
             pltpu.VMEM((width, 3 * local), LOW),
@@ -1440,8 +1459,8 @@
 
 
 def share_kernel(lines, early_ref, late_ref, embed_ref, own_patch_ref, used_ref, gain_ref, loss_ref, label_ref,
-                 row_ref, shared_ref, total_ref,
-                 term, windows, mine, slots, rows_out, patch_ref, *comm):
+                 row_ref, shared_out, total_ref,
+                 term, windows, mine, slots, rows_out, patch_ref, shared_ref, *comm):
     corner, spot = Corner(), Lines(lines)
     pairs, width = 2 * lines, early_ref.shape[1]
     quarters = 4
@@ -1556,6 +1575,23 @@
     @pl.when(spot.line > 0)
     def _():
         rows_out[...] = late_ref[...]
+
+    window = jnp.where(window_valid(spot.me, corner.me, width), windows[gather.part(corner.me, 0)], 0.0)
+    square = jnp.sum(window * window) + jnp.sum(rows_out[...] * rows_out[...])
+    counted = jnp.sum(jnp.where(label_ref[...] < 2, 1.0, 0.0))
+    line = lax.broadcasted_iota(jnp.int32, total_ref.shape, 0)
+    slots[me] = jnp.where(line == 0, square, jnp.where(line == 1, loss_ref[...], jnp.where(line == 2, counted, 0.0)))
+
+    def send(step):
+        return remote(slots.at[me], slots.at[me], send_sem.at[step], recv_sem.at[step], peer(step))
+
+    def arrive(step):
+        source = lax.rem(me - step + count, count)
+        return remote(slots.at[source], slots.at[source], send_sem.at[step], recv_sem.at[step], peer(step))
+
+    @pl.loop(1, count)
+    def _(step):
+        send(step).start()
 
     gather.relay(0)
 
@@ -1572,7 +1608,6 @@
         for j in range(8):
             row_ref[pl.ds(j, chunk, 8)] = rows_out[:, j * 128 : (j + 1) * 128]
 
-    squares = jnp.sum(rows_out[...] * rows_out[...], 0, keepdims=True)
     gather.finish()
     shared_ref[...] = jnp.zeros_like(shared_ref)
     for phase in range(5):
@@ -1586,24 +1621,8 @@
                     shared_ref[pl.ds(start, height, stride)] = windows[here, j * 128 : (j + 1) * 128]
 
             shared_walk(spot.me, quarter, take, (phase,))
-    kept = shared_ref[FRONT : FRONT + PADDED - FRONT]
-    place = lax.broadcasted_iota(jnp.int32, kept.shape, 0)
-    kept = jnp.where((place < SHARED_LANES) & (corner.me == 0), kept, 0.0)
-    square = jnp.sum(jnp.sum(squares, 1, keepdims=True)) + jnp.sum(kept * kept)
-    counted = jnp.sum(jnp.where(label_ref[...] < 2, 1.0, 0.0))
-    line = lax.broadcasted_iota(jnp.int32, total_ref.shape, 0)
-    slots[me] = jnp.where(line == 0, square, jnp.where(line == 1, loss_ref[...], jnp.where(line == 2, counted, 0.0)))
-
-    def send(step):
-        return remote(slots.at[me], slots.at[me], send_sem.at[step], recv_sem.at[step], peer(step))
-
-    def arrive(step):
-        source = lax.rem(me - step + count, count)
-        return remote(slots.at[source], slots.at[source], send_sem.at[step], recv_sem.at[step], peer(step))
-
-    @pl.loop(1, count)
-    def _(step):
-        send(step).start()
+
+    shared_out[...] = shared_ref[FRONT : FRONT + SHARED_LANES]
 
     @pl.loop(1, count)
     def _(step):
@@ -1626,7 +1645,7 @@
     shape = jax.ShapeDtypeStruct
     return pl.pallas_call(
         partial(share_kernel, lines),
-        out_shape=(shape((chunk * width // 128, 128), WIDE), shape((PADDED, 128), WIDE), shape((8, 128), WIDE)),
+        out_shape=(shape((chunk * width // 128, 128), WIDE), shape((SHARED_LANES, 128), WIDE), shape((8, 128), WIDE)),
         in_specs=[VMEM] * 8,
         out_specs=(VMEM,) * 3,
         scratch_shapes=[
@@ -1636,6 +1655,7 @@
             pltpu.VMEM((count, 8, 128), WIDE),
             pltpu.VMEM((chunk, width), WIDE),
             pltpu.VMEM((patches.shape[1], width), WIDE),
+            pltpu.VMEM((PADDED, 128), WIDE),
         ]
         + LineSum.scratch(1, chunk, SUM_PIECES, width, True)
         + LineSum.scratch(lines, WINDOW, 1, width, False)
@@ -1994,24 +2014,37 @@
 
 def adam_kernel(total_ref, count_ref, *refs):
     norm_value = jnp.sqrt(total_ref[0, 0:1]) / total_ref[2, 0:1]
-    factor = clip_norm / jnp.maximum(norm_value, clip_norm) / total_ref[2, 0:1]
+    factor = (clip_norm / jnp.maximum(norm_value, clip_norm) / total_ref[2, 0:1]).reshape(1, 1)
     step_float = jnp.full((1, 1), count_ref[0], jnp.int32).astype(WIDE)
-    grad, master, first, second, ema = (ref[...] for ref in refs[:5])
-    new, first_new, second_new = adam_update(master, first, second, grad * factor.reshape(1, 1), step_float)
-    for ref, value in zip(refs[5:], (new, first_new, second_new, ema_rate * ema + (1.0 - ema_rate) * new, new.astype(LOW))):
-        ref[...] = value
-
-
-def adam(totals, step_count, grad, master, first, second, ema, block):
-    size = master.shape[1]
-    spec = pl.BlockSpec((1, block), lambda at: (0, at))
+
+    def update(ins, outs):
+        grad, master, first, second, ema = (ref[...] for ref in ins)
+        new, first_new, second_new = adam_update(master, first, second, grad * factor, step_float)
+        ema_new = ema_rate * ema + (1.0 - ema_rate) * new
+        for ref, value in zip(outs, (new, first_new, second_new, ema_new, new.astype(LOW))):
+            ref[...] = value
+
+    parts = len(refs) // 10
+    for part in range(parts):
+        update(refs[5 * part : 5 * part + 5], refs[5 * (parts + part) : 5 * (parts + part) + 5])
+
+
+def adam(totals, step_count, rows, shared, blocks):
+    size = rows[1].shape[1] // blocks
+    spec = pl.BlockSpec((1, size), lambda at: (0, at))
+    if shared[0].shape[0] == 1:
+        kept = [pl.BlockSpec(array.shape, lambda at: (0, 0)) for array in shared]
+    else:
+        kept = [pl.BlockSpec((-(-array.shape[0] // (8 * blocks)) * 8, 128), lambda at: (at, 0)) for array in shared]
+    kinds = (WIDE,) * 4 + (LOW,)
+    shapes = [jax.ShapeDtypeStruct(arrays[1].shape, kind) for arrays in (rows, shared) if arrays for kind in kinds]
     return pl.pallas_call(
         adam_kernel,
-        grid=(size // block,),
-        out_shape=tuple(jax.ShapeDtypeStruct(master.shape, kind) for kind in (WIDE,) * 4 + (LOW,)),
-        in_specs=[pl.BlockSpec((8, 128), lambda at: (0, 0)), pl.BlockSpec(memory_space=pltpu.SMEM)] + [spec] * 5,
-        out_specs=(spec,) * 5,
-    )(totals, step_count, grad, master, first, second, ema)
+        grid=(blocks,),
+        out_shape=tuple(shapes),
+        in_specs=[pl.BlockSpec((8, 128), lambda at: (0, 0)), pl.BlockSpec(memory_space=pltpu.SMEM)] + [spec] * 5 + kept,
+        out_specs=(spec,) * 5 + tuple(kept),
+    )(totals, step_count, *rows, *shared)
 
 
 def per_device(
@@ -2038,9 +2071,7 @@
     share_rows = row_master.shape[1] // D
     own_patches = patches[0]
     if count_dp == 8:
-        shared_lanes = jnp.pad(
-            shared_master.reshape(SHARED_LANES, 128), ((FRONT, PADDED - FRONT - SHARED_LANES), (0, 0))
-        )
+        shared_lanes = shared_master.reshape(SHARED_LANES, 128)
         weights, used_cols, norm, embed, normed1, qkv, attended, log_total, resid1, normed2 = forward(
             view_counts, row_master.reshape(-1, 128), shared_lanes, own_patches, count_dp // 2, 7
         )
@@ -2090,11 +2121,10 @@
     gain_grad = jnp.concatenate([gain1_grad, gain2_grad], 0)
     if count_dp == 8:
         gains = jnp.pad(gain_grad, ((0, 4), (0, 0)))
-        row_lanes, shared_kept, totals = share(
+        row_lanes, shared_share, totals = share(
             early_grad, own_late[0], embed_grad, own_patches, unpatch_used, gains, loss_tile, alpha_label, count_dp // 2, 8
         )
         row_share = row_lanes.reshape(-1)
-        shared_share = shared_kept[FRONT : FRONT + SHARED_LANES].reshape(-1)
     else:
         patch_grad = dot(own_patches, embed_grad, TN)
         unpatch_grad = jnp.concatenate(
@@ -2122,15 +2152,12 @@
         totals = total_over_all(jnp.pad(jnp.broadcast_to(scalars, (3, 128)), ((0, 5), (0, 0))), 2)
     square_total, loss_total, pixel_total = totals[0, 0], totals[1, 0], totals[2, 0]
     norm_value = jnp.sqrt(square_total) / pixel_total
-    factor = clip_norm / jnp.maximum(norm_value, clip_norm) / pixel_total
-    step_float = step_count[0].astype(jnp.float32)
-    row_new, row_first_new, row_second_new, row_ema_new, row_copy = adam(
-        totals, step_count, row_share[None], row_master, row_first, row_second, row_ema, row_master.shape[1] // 6
-    )
-    shared_new, shared_first_new, shared_second_new = adam_update(
-        shared_master, shared_first, shared_second, shared_share * factor, step_float
-    )
-    shared_ema_new = ema_rate * shared_ema + (1.0 - ema_rate) * shared_new
+    flat = shared_master.shape
+    lanes = (-1, 128) if flat[0] % 128 == 0 else (1, -1)
+    shared = [array.reshape(lanes) for array in (shared_share, shared_master, shared_first, shared_second, shared_ema)]
+    updated = adam(totals, step_count, (row_share[None], row_master, row_first, row_second, row_ema), shared, 6)
+    row_new, row_first_new, row_second_new, row_ema_new, row_copy = updated[:5]
+    shared_new, shared_first_new, shared_second_new, shared_ema_new, shared_copy = (array.reshape(flat) for array in updated[5:])
     return (
         norm_value.reshape(1),
         (loss_total / pixel_total).reshape(1),
@@ -2143,7 +2170,7 @@
         shared_first_new,
         shared_second_new,
         shared_ema_new,
-        shared_new.astype(jnp.bfloat16),
+        shared_copy,
     )
 
 

time: 454 us -> 446 us (0.982)
  no operation moved by 1% of the time
where the time goes in v9:
time: 446 us; the launch traced here: 445 us
  Pallas kernels  434 us (97%)
  between operations  7 us (2%)
    pallas_call x1, Pallas kernels, forward(): pl.pallas_call(partial(forward_kernel, lines, 256), out_shape=(shape((3 *...  124 us
    pallas_call x1, Pallas kernels, share(): pl.pallas_call(partial(share_kernel, lines), out_shape=(shape((chunk * wi...  89 us
    pallas_call x1, Pallas kernels, attend_back(): pl.pallas_call(partial(attend_back_kernel, parts, 256, lines), out_shape=...  76.7 us
    pallas_call x1, Pallas kernels, mlp_back(): pl.pallas_call(partial(mlp_back_kernel, chunk), out_shape=(shape((width,...  62.9 us
    pallas_call x1, Pallas kernels, mlp(): pl.pallas_call(mlp_kernel, out_shape=(shape((length, hidden), WIDE), shap...  35.9 us
    pallas_call x1, Pallas kernels, render(): pl.pallas_call(partial(render_kernel, area, wide, block, split, span), ou...  35.1 us
    pallas_call x1, Pallas kernels, adam(): pl.pallas_call(adam_kernel, grid=(blocks,), out_shape=tuple(shapes), in_s...  10.3 us

profile of v9, /device:TPU:0, one launch (start us, length us, event | category | flops | bytes accessed | tf_op | source)
XLA Modules:
  0.0 445.3 jit_solution(10153816757499062097)
XLA Ops:
  0.6 2.0 copy.26
  3.3 123.7 %shard_map.229 = (bf16[3072,1024]{1,0:T(8,128)(2,1)}, bf16[1024,128]{1,0:T(8,128)(2,1)}, f32[8,1024]{1,0:T(8,128)}, f32[384,1024]{1,0:T(8,128)}, bf16[1536,1024]...) custom-call(s32[1]{0:T(128)S(6)} %copy.27.count_ref, ...), custom_call_target="tpu_custom_call" | custom-call | tf_op jit(solution)/shard_map/pallas_call | solution.py:749
  127.0 35.9 %shard_map.230 = (f32[1536,1024]{1,0:T(8,128)}, bf16[1536,1024]{1,0:T(8,128)(2,1)}, bf16[384,1024]{1,0:T(8,128)(2,1)}, bf16[1536,128]{1,0:T(8,128)(2,1)}) custom-call(bf16[1536,1024]{1,0:T(8,128)(2,1)} %get-tuple-element.51.normed2_ref.normed2_in, bf16[3072,1024]{1,0:T(8,128)(2,1)} %get-tuple-element.52.weight_ref, ...), custom_call_target="tpu_custom_call" | custom-call | tf_op jit(solution)/shard_map/pallas_call | solution.py:854
  162.9 35.1 %shard_map.231 = (f32[8,128]{1,0:T(8,128)}, bf16[1536,128]{1,0:T(8,128)(2,1)}) custom-call(bf16[1536,128]{1,0:T(8,128)(2,1)} %get-tuple-element.55.table_ref, s32[4,6144]{1,0:T(4,128)} %bitcast.25, s32[4,6144]{1,0:T(4,128)} %bitcast.26, s32[1,6144]{1,0:T(1,128)} %label_ref.3), custom_call_target="tpu_custom_call" | custom-call | tf_op jit(solution)/shard_map/pallas_call | solution.py:1760
  198.0 62.9 %shard_map.232 = (f32[1024,128]{1,0:T(8,128)}, f32[2304,1024]{1,0:T(8,128)}, bf16[2304,1024]{1,0:T(8,128)(2,1)}, f32[384,1024]{1,0:T(8,128)}, bf16[1536,1024]{1,0:T(8,128)(2,1)}, /*index=5*/f32[2,1024]{1,0:T(2,128)}) custom-call(bf16[1536,128]{1,0:T(8,128)(2,1)} %get-tuple-element.56.table_ref, bf16[1024,128]{1,0:T(8,128)(2,1)} %get-tuple-element.54.cols_ref, ...), custom_call_target="tpu_custom_call" | custom-call | tf_op jit(solution)/shard_map/pallas_call | solution.py:1027
  260.9 0.0 copy-start
  260.9 76.7 %shard_map.233 = (f32[768,1024]{1,0:T(8,128)}, bf16[384,1024]{1,0:T(8,128)(2,1)}, f32[2,1024]{1,0:T(2,128)}, f32[384,1024]{1,0:T(8,128)}) custom-call(s32[1]{0:T(128)S(6)} %copy.27.count_ref, bf16[1536,1024]{1,0:T(8,128)(2,1)} %get-tuple-element.62.branch_ref, bf16[3072,1024]{1,0:T(8,128)(2,1)} %get-tuple-element.52.weight_ref, ...), custom_call_target="tpu_custom_call" | custom-call | tf_op jit(solution)/shard_map/pallas_call | solution.py:1424
  337.6 0.0 copy-done
  337.6 1.3 select_maximum_fusion.gain_ref
  339.0 89.0 %shard_map.234 = (f32[3072,128]{1,0:T(8,128)}, f32[1348,128]{1,0:T(8,128)}, f32[8,128]{1,0:T(8,128)}) custom-call(f32[768,1024]{1,0:T(8,128)} %get-tuple-element.70.early_ref, f32[384,1024]{1,0:T(8,128)} %get-tuple-element.71.late_ref, bf16[384,1024]{1,0:T(8,128)(2,1)} %get-tuple-element.72.embed_ref, bf16[384,576]{1,0:T(8,128)(2,1)} %bitcast.18, ...), custom_call_target="tpu_custom_call" | custom-call | tf_op jit(solution)/shard_map/pallas_call | solution.py:1646
  428.6 10.3 %shard_map.235 = (f32[1,393216]{1,0:T(1,128)}, f32[1,393216]{1,0:T(1,128)}, f32[1,393216]{1,0:T(1,128)}, f32[1,393216]{1,0:T(1,128)}, bf16[1,393216]{1,0:T(2,128...) custom-call(f32[8,128]{1,0:T(8,128)} %get-tuple-element.77.total_ref, ...), custom_call_target="tpu_custom_call" | custom-call | tf_op jit(solution)/shard_map/pallas_call | solution.py:2041
  439.0 1.4 fusion
Async XLA Ops:
  260.9 76.8 %copy-start = (f32[2,1024]{1,0:T(2,128)S(1)}, f32[2,1024]{1,0:T(2,128)}, u32[]{:S(2)}) copy-start(f32[2,1024]{1,0:T(2,128)} %get-tuple-element.75) | copy-start | bytes 24580

commit v10 on v9

--- a/solution.py
+++ b/solution.py
@@ -244,10 +244,10 @@
     return pl.ds(pl.multiple_of(block * size, size), size)
 
 
-def column_loop(width, body):
-    @pl.loop(0, width // TILE)
+def column_loop(width, body, size=TILE):
+    @pl.loop(0, width // size)
     def _(tile):
-        body(pl.ds(pl.multiple_of(tile * TILE, TILE), TILE))
+        body(pl.ds(pl.multiple_of(tile * size, size), size))
 
 
 def attend_kernel(parts, q_rows, count_ref, patch_ref, proj_ref, norm_ref, weight_ref, *rest):
@@ -827,10 +827,10 @@
             hidden_ref[here, cols] = hidden
             active_ref[here, cols] = (0.5 * hidden * (1.0 + lax.erf(hidden * ROOT_HALF))).astype(LOW)
 
-        column_loop(up_ref.shape[1], columns)
+        column_loop(up_ref.shape[1], columns, 2 * TILE)
         for copy in stores(step):
             copy.start()
-        column_loop(width, lambda cols: term.__setitem__((slice(None), cols), dot(active_ref[here], down_ref[:, cols])))
+        column_loop(width, lambda cols: term.__setitem__((slice(None), cols), dot(active_ref[here], down_ref[:, cols])), 2 * TILE)
         scatter.step(step, term)
 
     for piece in range(PIECES):

time: 446 us -> 444 us (level)
  no operation moved by 1% of the time
where the time goes in v10:
time: 444 us
  Pallas kernels  432 us (97%)
  between operations  7 us (2%)
    pallas_call x1, Pallas kernels, forward(): pl.pallas_call(partial(forward_kernel, lines, 256), out_shape=(shape((3 *...  124 us
    pallas_call x1, Pallas kernels, share(): pl.pallas_call(partial(share_kernel, lines), out_shape=(shape((chunk * wi...  89 us
    pallas_call x1, Pallas kernels, attend_back(): pl.pallas_call(partial(attend_back_kernel, parts, 256, lines), out_shape=...  76.8 us
    pallas_call x1, Pallas kernels, mlp_back(): pl.pallas_call(partial(mlp_back_kernel, chunk), out_shape=(shape((width,...  62.8 us
    pallas_call x1, Pallas kernels, render(): pl.pallas_call(partial(render_kernel, area, wide, block, split, span), ou...  35.1 us
    pallas_call x1, Pallas kernels, mlp(): pl.pallas_call(mlp_kernel, out_shape=(shape((length, hidden), WIDE), shap...  34.5 us
    pallas_call x1, Pallas kernels, adam(): pl.pallas_call(adam_kernel, grid=(blocks,), out_shape=tuple(shapes), in_s...  10.3 us

profile of v10, /device:TPU:0, one launch (start us, length us, event | category | flops | bytes accessed | tf_op | source)
XLA Modules:
  0.0 443.9 jit_solution(5432811614693675689)
XLA Ops:
  0.6 2.0 copy.26
  3.3 123.7 %shard_map.229 = (bf16[3072,1024]{1,0:T(8,128)(2,1)}, bf16[1024,128]{1,0:T(8,128)(2,1)}, f32[8,1024]{1,0:T(8,128)}, f32[384,1024]{1,0:T(8,128)}, bf16[1536,1024]...) custom-call(s32[1]{0:T(128)S(6)} %copy.27.count_ref, ...), custom_call_target="tpu_custom_call" | custom-call | tf_op jit(solution)/shard_map/pallas_call | solution.py:749
  127.0 34.5 %shard_map.230 = (f32[1536,1024]{1,0:T(8,128)}, bf16[1536,1024]{1,0:T(8,128)(2,1)}, bf16[384,1024]{1,0:T(8,128)(2,1)}, bf16[1536,128]{1,0:T(8,128)(2,1)}) custom-call(bf16[1536,1024]{1,0:T(8,128)(2,1)} %get-tuple-element.51.normed2_ref.normed2_in, bf16[3072,1024]{1,0:T(8,128)(2,1)} %get-tuple-element.52.weight_ref, ...), custom_call_target="tpu_custom_call" | custom-call | tf_op jit(solution)/shard_map/pallas_call | solution.py:854
  161.5 35.1 %shard_map.231 = (f32[8,128]{1,0:T(8,128)}, bf16[1536,128]{1,0:T(8,128)(2,1)}) custom-call(bf16[1536,128]{1,0:T(8,128)(2,1)} %get-tuple-element.55.table_ref, s32[4,6144]{1,0:T(4,128)} %bitcast.25, s32[4,6144]{1,0:T(4,128)} %bitcast.26, s32[1,6144]{1,0:T(1,128)} %label_ref.3), custom_call_target="tpu_custom_call" | custom-call | tf_op jit(solution)/shard_map/pallas_call | solution.py:1760
  196.6 62.8 %shard_map.232 = (f32[1024,128]{1,0:T(8,128)}, f32[2304,1024]{1,0:T(8,128)}, bf16[2304,1024]{1,0:T(8,128)(2,1)}, f32[384,1024]{1,0:T(8,128)}, bf16[1536,1024]{1,0:T(8,128)(2,1)}, /*index=5*/f32[2,1024]{1,0:T(2,128)}) custom-call(bf16[1536,128]{1,0:T(8,128)(2,1)} %get-tuple-element.56.table_ref, bf16[1024,128]{1,0:T(8,128)(2,1)} %get-tuple-element.54.cols_ref, ...), custom_call_target="tpu_custom_call" | custom-call | tf_op jit(solution)/shard_map/pallas_call | solution.py:1027
  259.4 0.0 copy-start
  259.4 76.8 %shard_map.233 = (f32[768,1024]{1,0:T(8,128)}, bf16[384,1024]{1,0:T(8,128)(2,1)}, f32[2,1024]{1,0:T(2,128)}, f32[384,1024]{1,0:T(8,128)}) custom-call(s32[1]{0:T(128)S(6)} %copy.27.count_ref, bf16[1536,1024]{1,0:T(8,128)(2,1)} %get-tuple-element.62.branch_ref, bf16[3072,1024]{1,0:T(8,128)(2,1)} %get-tuple-element.52.weight_ref, ...), custom_call_target="tpu_custom_call" | custom-call | tf_op jit(solution)/shard_map/pallas_call | solution.py:1424
  336.2 0.0 copy-done
  336.2 1.3 select_maximum_fusion.gain_ref
  337.5 89.0 %shard_map.234 = (f32[3072,128]{1,0:T(8,128)}, f32[1348,128]{1,0:T(8,128)}, f32[8,128]{1,0:T(8,128)}) custom-call(f32[768,1024]{1,0:T(8,128)} %get-tuple-element.70.early_ref, f32[384,1024]{1,0:T(8,128)} %get-tuple-element.71.late_ref, bf16[384,1024]{1,0:T(8,128)(2,1)} %get-tuple-element.72.embed_ref, bf16[384,576]{1,0:T(8,128)(2,1)} %bitcast.18, ...), custom_call_target="tpu_custom_call" | custom-call | tf_op jit(solution)/shard_map/pallas_call | solution.py:1646
  427.2 10.3 %shard_map.235 = (f32[1,393216]{1,0:T(1,128)}, f32[1,393216]{1,0:T(1,128)}, f32[1,393216]{1,0:T(1,128)}, f32[1,393216]{1,0:T(1,128)}, bf16[1,393216]{1,0:T(2,128...) custom-call(f32[8,128]{1,0:T(8,128)} %get-tuple-element.77.total_ref, ...), custom_call_target="tpu_custom_call" | custom-call | tf_op jit(solution)/shard_map/pallas_call | solution.py:2041
  437.5 1.4 fusion
Async XLA Ops:
  259.4 76.8 %copy-start = (f32[2,1024]{1,0:T(2,128)S(1)}, f32[2,1024]{1,0:T(2,128)}, u32[]{:S(2)}) copy-start(f32[2,1024]{1,0:T(2,128)} %get-tuple-element.75) | copy-start | bytes 24580
